TPU v7x, 512 devices: a whole 4x8x8 slice. The times are simulated.
512 devices in a mesh: ens: 16 (over x, y_lo), lat: 32 (over y_hi, z, core).
Axes of the slice: x: 4, y: 8 (y_hi: 2, y_lo: 4; y = y_hi * 4 + y_lo), z: 8, core: 2. Of those that a mesh axis runs over, the one named last changes fastest.
Arguments:
- features: bfloat16 [128, 128, 128], P('lat'), may hold values from -6 to 6
- random_perturbation: bfloat16 [16, 128, 128, 128], P('ens', 'lat'), may hold values from -6 to 6
- observed_truth: float32 [69, 128, 128], P(None, 'lat'), may hold values from -6 to 6
- stencil_taps: float32 [49, 128], replicated, may hold values from -0.875 to 0.875
- affine_factor: float32 [128], replicated, may hold values from 0.5 to 1.5
- widen_matrix: bfloat16 [512, 128], P('lat'), may hold values from -0.5 to 0.5
- shrink_matrix: bfloat16 [512, 128], P('lat'), may hold values from -0.25 to 0.25
- readout_matrix: bfloat16 [69, 128], replicated, may hold values from -0.5 to 0.5
Outputs:
- crps_score: float32 [], replicated
- stencil_taps_sensitivity: float32 [49, 128], replicated
- affine_factor_sensitivity: float32 [128], replicated
- widen_matrix_sensitivity: float32 [512, 128], P('lat')
- shrink_matrix_sensitivity: float32 [512, 128], P('lat')
- readout_matrix_sensitivity: float32 [69, 128], replicated
- sample_outlook: bfloat16 [16, 69, 128, 128], P('ens', None, 'lat')
- sample_average_spread: float32 [16, 69, 128, 128], P('ens', None, 'lat')
All inputs are finite; a program needn't handle non-finite values.
Results may differ from a plain program's by a relative error of at most 0.0024.
The roundings to bfloat16 on the way count: a program that leaves them out, or rounds other values in their place, can miss the bound.
Values may be sent and summed in bfloat16 or wider, within the bound.
No kernel may reach another device: no remote copies, remote signals or barrier semaphores. Data moves between devices by JAX's collectives and lax.ppermute only.
A program may use at most 64 MiB of HBM per device.

v0:
```python
import math

import jax
import jax.numpy as jnp
from jax import lax
from jax.sharding import PartitionSpec as P

STENCIL_SIDE = 7


SQRT_TWO_PI = 0.7978845608028654
CUBIC = 0.044715
EPSILON = 1e-06
SMOOTHING = 0.01


def extended(cells, sides, width):
    for axis, dim in sides:
        count = lax.axis_size(axis)
        ends = count - 1
        head = lax.slice_in_dim(cells, 0, width, axis=dim)
        tail = lax.slice_in_dim(cells, cells.shape[dim] - width, cells.shape[dim], axis=dim)
        cells = jnp.concatenate(
            [
                lax.ppermute(tail, axis, [(i, (i + 1) % count) for i in range(ends)]),
                cells,
                lax.ppermute(head, axis, [((i + 1) % count, i) for i in range(ends)]),
            ],
            axis=dim,
        )
    return cells


def smooth_magnitude(value):
    return jnp.sqrt(value * value + SMOOTHING)


def smooth_slope(value):
    return value * lax.rsqrt(value * value + SMOOTHING)


def gelu_tanh(northern_margin):
    return (
        0.5
        * northern_margin
        * (
            1.0
            + jnp.tanh(
                SQRT_TWO_PI
                * (northern_margin + CUBIC * northern_margin * northern_margin * northern_margin)
            )
        )
    )


def gelu_slope(northern_margin):
    inner = jnp.tanh(
        SQRT_TWO_PI
        * (northern_margin + CUBIC * northern_margin * northern_margin * northern_margin)
    )
    return 0.5 * (1.0 + inner) + 0.5 * northern_margin * (1.0 - inner * inner) * SQRT_TWO_PI * (
        1.0 + 3.0 * CUBIC * northern_margin * northern_margin
    )


def depthwise(margin_extended, stencil_taps, meridian_slab):
    half = STENCIL_SIDE // 2
    wide = margin_extended.astype(jnp.float32)
    axis_rows = wide.ndim - 3
    result = jnp.zeros(
        wide.shape[:axis_rows] + (meridian_slab,) + wide.shape[axis_rows + 1 :], jnp.float32
    )
    for offset_row in range(STENCIL_SIDE):
        band = lax.slice_in_dim(wide, offset_row, offset_row + meridian_slab, axis=axis_rows)
        for offset_col in range(STENCIL_SIDE):
            result = result + stencil_taps[offset_row * STENCIL_SIDE + offset_col] * jnp.roll(
                band, half - offset_col, axis=-2
            )
    return result


def kernel_grad(margin_extended, upstream, meridian_slab):
    half = STENCIL_SIDE // 2
    wide = margin_extended.astype(jnp.float32)
    axis_rows = wide.ndim - 3
    channels = upstream.shape[-1]
    taps = []
    for offset_row in range(STENCIL_SIDE):
        band = lax.slice_in_dim(wide, offset_row, offset_row + meridian_slab, axis=axis_rows)
        for offset_col in range(STENCIL_SIDE):
            shifted = jnp.roll(band, half - offset_col, axis=-2)
            taps.append(jnp.sum((upstream * shifted).reshape(-1, channels), axis=0))
    return jnp.stack(taps)


def normalize(depth_out):
    centre = jnp.mean(depth_out, axis=-1, keepdims=True)
    centred = depth_out - centre
    variance = jnp.mean(centred * centred, axis=-1, keepdims=True)
    reciprocal_spread = lax.rsqrt(variance + EPSILON)
    return (centred * reciprocal_spread, reciprocal_spread)


def pair_terms(carry, owned_subset, piece):

    def one_pair(totals, other):
        gap = owned_subset - other.astype(jnp.float32)[None]
        return ((totals[0] + smooth_magnitude(gap), totals[1] + smooth_slope(gap)), None)

    carry, ignored_entry = lax.scan(one_pair, carry, piece)
    return carry


def on_device(
    features,
    random_perturbation,
    observed_truth,
    stencil_taps,
    affine_factor,
    widen_matrix,
    shrink_matrix,
    readout_matrix,
):
    sample_count, meridian_slab, zonal_points, channels = random_perturbation.shape
    outlook_quantities = readout_matrix.shape[0]
    half = STENCIL_SIDE // 2
    latitudes = meridian_slab * lax.axis_size("lat")
    ensemble = sample_count * lax.axis_size("ens")
    point_tally = meridian_slab * zonal_points
    planar_map = (
        features[None].astype(jnp.float32) + random_perturbation.astype(jnp.float32)
    ).astype(jnp.bfloat16)
    margin_extended = extended(planar_map, (("lat", 1),), half)
    up_full, down_full = (
        lax.all_gather(widen_matrix, "lat", axis=0, tiled=True),
        lax.all_gather(shrink_matrix, "lat", axis=0, tiled=True),
    )
    depth_out = depthwise(margin_extended, stencil_taps, meridian_slab)
    factor_multiplied, reciprocal_spread = normalize(depth_out)
    standardized_activation = (
        (affine_factor * factor_multiplied)
        .astype(jnp.bfloat16)
        .reshape(sample_count * point_tally, channels)
    )
    northern_margin = lax.dot_general(
        standardized_activation,
        up_full,
        (((1,), (1,)), ((), ())),
        preferred_element_type=jnp.float32,
    )
    nonlinear_response = gelu_tanh(northern_margin).astype(jnp.bfloat16)
    mixed = jnp.dot(nonlinear_response, down_full, preferred_element_type=jnp.float32)
    skip_activation = (
        planar_map.reshape(sample_count * point_tally, channels).astype(jnp.float32) + mixed
    ).astype(jnp.bfloat16)
    residual_row_block = skip_activation.reshape(sample_count, point_tally, channels)
    sample_outlook = jnp.einsum(
        "au,blu->bal", readout_matrix, residual_row_block, preferred_element_type=jnp.float32
    )
    sample_outlook = sample_outlook.astype(jnp.bfloat16).reshape(
        sample_count, outlook_quantities, meridian_slab, zonal_points
    )
    row_index = (
        lax.axis_index("lat") * meridian_slab + jnp.arange(meridian_slab, dtype=jnp.int32)
    ).astype(jnp.float32)
    area = jnp.cos(math.pi * ((row_index + 0.5) / latitudes - 0.5))
    weight = (area * (1.0 / (latitudes * zonal_points)))[None, None, :, None]
    pair_norm = 1.0 / (ensemble * (ensemble - 1))
    owned_subset = sample_outlook.astype(jnp.float32)
    blank_buffer = jnp.zeros_like(owned_subset)
    spread, ranks = pair_terms(
        (blank_buffer, blank_buffer),
        owned_subset,
        lax.all_gather(sample_outlook, "ens", axis=0, tiled=True),
    )
    miss = owned_subset - observed_truth[None]
    loss_part = jnp.sum(weight * (smooth_magnitude(miss) / ensemble - 0.5 * pair_norm * spread))
    carried_signal = (weight * (smooth_slope(miss) / ensemble - pair_norm * ranks)).astype(
        jnp.bfloat16
    )
    carried_signal = carried_signal.reshape(sample_count, outlook_quantities, point_tally)
    sample_average_spread = spread / (ensemble - 1)
    readout_matrix_sensitivity = jnp.einsum(
        "mvp,mpc->vc", carried_signal, residual_row_block, preferred_element_type=jnp.float32
    )
    back_residual = jnp.einsum(
        "mvp,vc->mpc", carried_signal, readout_matrix, preferred_element_type=jnp.float32
    )
    back_residual = back_residual.astype(jnp.bfloat16).reshape(sample_count * point_tally, channels)
    shrink_matrix_sensitivity = lax.dot_general(
        nonlinear_response,
        back_residual,
        (((0,), (0,)), ((), ())),
        preferred_element_type=jnp.float32,
    )
    back_gate = lax.dot_general(
        back_residual, down_full, (((1,), (1,)), ((), ())), preferred_element_type=jnp.float32
    )
    back_upper = (back_gate * gelu_slope(northern_margin)).astype(jnp.bfloat16)
    widen_matrix_sensitivity = lax.dot_general(
        back_upper,
        standardized_activation,
        (((0,), (0,)), ((), ())),
        preferred_element_type=jnp.float32,
    )
    back_norm = jnp.dot(back_upper, up_full, preferred_element_type=jnp.float32).reshape(
        sample_count, meridian_slab, zonal_points, channels
    )
    affine_factor_sensitivity = jnp.sum(
        (back_norm * factor_multiplied).reshape(-1, channels), axis=0
    )
    back_scaled = back_norm * affine_factor
    back_depth = reciprocal_spread * (
        back_scaled
        - jnp.mean(back_scaled, axis=-1, keepdims=True)
        - factor_multiplied * jnp.mean(back_scaled * factor_multiplied, axis=-1, keepdims=True)
    )
    stencil_taps_sensitivity = kernel_grad(margin_extended, back_depth, meridian_slab)
    summed_up, summed_down = lax.psum((widen_matrix_sensitivity, shrink_matrix_sensitivity), "ens")
    owned_up, owned_down = (
        lax.psum_scatter(summed_up, "lat", scatter_dimension=0, tiled=True),
        lax.psum_scatter(summed_down, "lat", scatter_dimension=0, tiled=True),
    )
    crps_score, total_out, total_gain, total_kernel = lax.psum(
        (
            loss_part,
            readout_matrix_sensitivity,
            affine_factor_sensitivity,
            stencil_taps_sensitivity,
        ),
        ("ens", "lat"),
    )
    return (
        crps_score,
        total_kernel,
        total_gain,
        owned_up,
        owned_down,
        total_out,
        sample_outlook,
        sample_average_spread,
    )


def solution(mesh):
    in_specs = (
        P("lat", None, None),
        P("ens", "lat", None, None),
        P(None, "lat", None),
        P(),
        P(),
        P("lat", None),
        P("lat", None),
        P(),
    )
    out_specs = (
        P(),
        P(),
        P(),
        P("lat", None),
        P("lat", None),
        P(),
        P("ens", None, "lat", None),
        P("ens", None, "lat", None),
    )
    return jax.shard_map(
        on_device, mesh=mesh, in_specs=in_specs, out_specs=out_specs, check_vma=False
    )
```

profile of v0, /device:TPU:64, one launch (start us, length us, event | category | flops | bytes accessed | tf_op | source)
XLA Modules:
  0.0 579.8 jit_solution(15327835750314781220)
XLA Ops:
  7.2 1.0 fusion.8
  8.3 1.9 collective-permute-start
  10.2 3.6 collective-permute-start.1
  13.8 1.0 slice_bitcast_fusion.48
  14.9 1.0 slice_bitcast_fusion.47
  15.9 0.9 slice_bitcast_fusion.46
  16.8 53.0 %all_gather.9 = bf16[512,128]{1,0:T(8,128)(2,1)S(1)} all-gather(bf16[16,128]{1,0:T(8,128)(2,1)} %param.15), channel_id=1, replica_groups=mesh['ens'=16,'lat'=32] {'lat'}, dimensions={0}, use_global_device_ids=true | all-gather | bytes 135168 | tf_op jit(solution)/shard_map/all_gather | solution.py:135
  69.8 54.0 %all_gather.10 = bf16[512,128]{1,0:T(8,128)(2,1)S(1)} all-gather(bf16[16,128]{1,0:T(8,128)(2,1)} %param.16), channel_id=1, replica_groups=mesh['ens'=16,'lat'=32] {'lat'}, dimensions={0}, use_global_device_ids=true | all-gather | bytes 135168 | tf_op jit(solution)/shard_map/all_gather | solution.py:136
  123.9 0.3 fusion.16
  124.3 0.3 fusion.17
  124.7 0.3 fusion.18
  125.3 1.1 maximum_convert_fusion.37
  126.4 1.3 maximum_convert_fusion.34
  127.7 0.6 maximum_convert_fusion.36
  128.3 0.6 maximum_convert_fusion.35
  128.9 0.6 maximum_convert_fusion.9
  129.5 0.6 maximum_convert_fusion.8
  130.2 0.6 maximum_convert_fusion.33
  130.8 0.6 maximum_convert_fusion.32
  131.7 3.9 fusion.14
  135.6 0.2 multiply_reduce_fusion.52
  135.9 0.2 multiply_convert_fusion.1
  136.1 1.4 multiply_convert_fusion
  137.6 0.3 fusion.1
  137.9 0.5 copy-done.62
  138.4 0.2 fusion.2
  138.6 0.7 reshape.1579
  139.4 0.6 cosine_multiply_fusion
  139.9 0.9 convert_element_type.102
  140.8 0.7 reshape.1584
  141.5 74.7 %all-gather.2.cloned.1.call-done = bf16[16,69,4,128]{3,2,1,0:T(4,128)(2,1)} async-done(((bf16[1,69,4,128]{3,2,1,0:T(4,128)(2,1)}), bf16[16,69,4,128]{3,2,1,0:T(4,128)(2,1)}) %all-gather.2.cloned.1.call-update) | async-done | bytes 1130512 | tf_op jit(solution)/shard_map/all_gather | solution.py:174
  216.3 17.6 %while.13 = (s32[]{:T(128)}, f32[1,69,4,128]{3,2,1,0:T(4,128)S(1)}, f32[1,69,4,128]{3,2,1,0:T(4,128)S(1)}, bf16[16,69,4,128]{3,2,1,0:T(4,128)(2,1)}, f32[1,69,4,128]{3,2,1,0:T(4,128)S(1)}, /*index=5*/s32[]{:T(128)}, s32[]{:T(128)}) while((s32[]{:T(128)}, f32[1,69,4,128]{3,2,1,0:T(4,128)S(1)}, f32[1,69,4,128]{3,2,1,0:T(4,128)S(1)}, ...), condition=%wide.region_3.4_spmd.clone, body=%wide.region_2.3_spmd.clone.sunk | while | flops 317955 | bytes 777307 | solution.py:110
  216.3 1.1 select_add_fusion.3
  217.4 1.1 select_add_fusion.3
  218.5 1.1 select_add_fusion.3
  219.6 1.1 select_add_fusion.3
  220.7 1.1 select_add_fusion.3
  221.8 1.1 select_add_fusion.3
  222.9 1.1 select_add_fusion.3
  224.0 1.1 select_add_fusion.3
  225.1 1.1 select_add_fusion.3
  226.2 1.1 select_add_fusion.3
  227.3 1.1 select_add_fusion.3
  228.4 1.1 select_add_fusion.3
  229.5 1.1 select_add_fusion.3
  230.6 1.1 select_add_fusion.3
  231.7 1.1 select_add_fusion.3
  232.8 1.1 select_add_fusion.3
  233.9 2.5 fusion.13
  236.4 0.2 convolution_convert_fusion
  236.7 1.1 fusion.21
  237.8 2.1 fusion
  239.9 0.4 multiply_reduce_fusion.51
  240.3 0.7 multiply_reduce_fusion
  241.5 2.0 multiply_reduce_fusion.7
  243.5 1.8 multiply_reduce_fusion.17
  245.4 1.1 multiply_reduce_fusion.1
  246.6 1.8 multiply_reduce_fusion.28
  248.5 1.0 fusion.20
  249.8 1.1 multiply_reduce_fusion.38
  251.4 99.0 %all-reduce = (f32[]{:T(128)}, f32[49,128]{1,0:T(8,128)}, f32[128]{0:T(128)}, f32[69,128]{1,0:T(8,128)}) all-reduce(f32[]{:T(128)} %get-tuple-element.219, f32[49,128]{1,0:T(8,128)S(1)} %stack.199, f32[128]{0:T(128)S(1)} %copy-done.86, f32[69,128]{1,0:T(8,128)S(1)} %fusion.22), channel_id=1, replica_groups=mesh['ens'=16,'lat'=32] {'ens','lat'}, use_global_device_ids=true, to_apply=%region_5.6 | all-reduce | flops 15233 | bytes 121864 | tf_op jit(solution)/shard_map/psum | solution.py:224
  350.3 20.7 %reduce-scatter.5.cloned.1.call-done = f32[16,128]{1,0:T(8,128)} async-done(((f32[512,128]{1,0:T(8,128)}), f32[16,128]{1,0:T(8,128)}) %reduce-scatter.5.cloned.1.call-update) | async-done | bytes 8208 | tf_op jit(solution)/shard_map/reduce_scatter | solution.py:222
  371.0 125.0 %reduce-scatter.3.cloned.1.call-done = f32[16,128]{1,0:T(8,128)} async-done(((f32[512,128]{1,0:T(8,128)}), f32[16,128]{1,0:T(8,128)}) %reduce-scatter.3.cloned.1.call-update) | async-done | bytes 8208 | tf_op jit(solution)/shard_map/reduce_scatter | solution.py:221
  496.0 77.3 %all-reduce.1 = (f32[16,128]{1,0:T(8,128)}, f32[16,128]{1,0:T(8,128)}) all-reduce(f32[16,128]{1,0:T(8,128)} %reduce-scatter.3.cloned.1.call-done, f32[16,128]{1,0:T(8,128)} %reduce-scatter.5.cloned.1.call-done), channel_id=1, replica_groups=mesh['ens'=16,'lat'=32] {'ens'}, use_global_device_ids=true, to_apply=%region_60.61 | all-reduce | flops 4096 | bytes 32768 | tf_op jit(solution)/shard_map/psum | solution.py:219
  (233 shorter events, 1.5 us)
Async XLA Ops:
  7.2 131.2 %copy-start = (bf16[69,128]{1,0:T(8,128)(2,1)S(1)}, bf16[69,128]{1,0:T(8,128)(2,1)}, u32[]{:S(2)}) copy-start(bf16[69,128]{1,0:T(8,128)(2,1)} %param.17) | copy-start | bytes 52996
  7.2 209.1 %all-gather.2.cloned.1.call-start = ((), (), s32[]{:S(2)}) async-start(), calls=%async_computation.2 | async-start | bytes 1201152 | tf_op jit(solution)/shard_map/all_gather | solution.py:174
  8.3 115.6 %collective-permute-start = (bf16[1,3,128,128]{3,2,1,0:T(8,128)(2,1)S(1)}, bf16[1,3,128,128]{3,2,1,0:T(8,128)(2,1)S(1)}, u32[]{:S(2)}, u32[]{:S(2)}) collective-permute-start(bf16[1,3,128,128]{3,2,1,0:T(8,128)(2,1)S(1)} %get-tuple-element.221), channel_id=1, source_target_pairs={{0,1},{1,2},{2,3},{3,4},{4,5},{5,6},{6,7},{7,8},{8,9},{9,10},{10,1... | collective-permute-start | bytes 294920 | tf_op jit(solution)/shard_map/ppermute | solution.py:25
  10.2 113.7 %collective-permute-start.1 = (bf16[1,3,128,128]{3,2,1,0:T(8,128)(2,1)S(1)}, bf16[1,3,128,128]{3,2,1,0:T(8,128)(2,1)S(1)}, u32[]{:S(2)}, u32[]{:S(2)}) collective-permute-start(bf16[1,3,128,128]{3,2,1,0:T(8,128)(2,1)S(1)} %get-tuple-element.222), channel_id=1, source_target_pairs={{1,0},{2,1},{3,2},{4,3},{5,4},{6,5},{7,6},{8,7},{9,8},{10,9},{11,1... | collective-permute-start | bytes 294920 | tf_op jit(solution)/shard_map/ppermute | solution.py:27
  69.8 66.3 %copy-start.68 = (bf16[512,128]{1,0:T(8,128)(2,1)}, bf16[512,128]{1,0:T(8,128)(2,1)S(1)}, u32[]{:S(2)}) copy-start(bf16[512,128]{1,0:T(8,128)(2,1)S(1)} %all_gather.9) | copy-start | bytes 393220
  123.8 13.7 %copy-start.70 = (bf16[512,128]{1,0:T(8,128)(2,1)}, bf16[512,128]{1,0:T(8,128)(2,1)S(1)}, u32[]{:S(2)}) copy-start(bf16[512,128]{1,0:T(8,128)(2,1)S(1)} %all_gather.10) | copy-start | bytes 393220
  124.2 7.1 %copy-start.7 = (f32[1,4,125,128]{3,2,1,0:T(8,128)}, f32[1,4,125,128]{3,2,1,0:T(8,128)S(1)}, u32[]{:S(2)}) copy-start(f32[1,4,125,128]{3,2,1,0:T(8,128)S(1)} %get-tuple-element.141) | copy-start | bytes 768004
  124.2 7.1 %copy-start.9 = (f32[1,4,125,128]{3,2,1,0:T(8,128)}, f32[1,4,125,128]{3,2,1,0:T(8,128)S(1)}, u32[]{:S(2)}) copy-start(f32[1,4,125,128]{3,2,1,0:T(8,128)S(1)} %get-tuple-element.142) | copy-start | bytes 768004
  124.2 7.1 %copy-start.11 = (f32[1,4,125,128]{3,2,1,0:T(8,128)}, f32[1,4,125,128]{3,2,1,0:T(8,128)S(1)}, u32[]{:S(2)}) copy-start(f32[1,4,125,128]{3,2,1,0:T(8,128)S(1)} %get-tuple-element.145) | copy-start | bytes 768004
  124.3 7.1 %copy-start.12 = (f32[1,4,125,128]{3,2,1,0:T(8,128)}, f32[1,4,125,128]{3,2,1,0:T(8,128)S(1)}, u32[]{:S(2)}) copy-start(f32[1,4,125,128]{3,2,1,0:T(8,128)S(1)} %get-tuple-element.146) | copy-start | bytes 768004
  124.3 7.1 %copy-start.18 = (f32[1,4,125,128]{3,2,1,0:T(8,128)}, f32[1,4,125,128]{3,2,1,0:T(8,128)S(1)}, u32[]{:S(2)}) copy-start(f32[1,4,125,128]{3,2,1,0:T(8,128)S(1)} %get-tuple-element.152) | copy-start | bytes 768004
  124.3 7.1 %copy-start.28 = (f32[1,4,125,128]{3,2,1,0:T(8,128)}, f32[1,4,125,128]{3,2,1,0:T(8,128)S(1)}, u32[]{:S(2)}) copy-start(f32[1,4,125,128]{3,2,1,0:T(8,128)S(1)} %get-tuple-element.147) | copy-start | bytes 768004
  124.3 7.1 %copy-start.44 = (f32[1,4,125,128]{3,2,1,0:T(8,128)}, f32[1,4,125,128]{3,2,1,0:T(8,128)S(1)}, u32[]{:S(2)}) copy-start(f32[1,4,125,128]{3,2,1,0:T(8,128)S(1)} %get-tuple-element.140) | copy-start | bytes 768004
  124.3 7.1 %copy-start.46 = (f32[1,4,125,128]{3,2,1,0:T(8,128)}, f32[1,4,125,128]{3,2,1,0:T(8,128)S(1)}, u32[]{:S(2)}) copy-start(f32[1,4,125,128]{3,2,1,0:T(8,128)S(1)} %get-tuple-element.143) | copy-start | bytes 768004
  124.3 7.1 %copy-start.48 = (f32[1,4,125,128]{3,2,1,0:T(8,128)}, f32[1,4,125,128]{3,2,1,0:T(8,128)S(1)}, u32[]{:S(2)}) copy-start(f32[1,4,125,128]{3,2,1,0:T(8,128)S(1)} %get-tuple-element.148) | copy-start | bytes 768004
  124.3 7.1 %copy-start.50 = (f32[1,4,125,128]{3,2,1,0:T(8,128)}, f32[1,4,125,128]{3,2,1,0:T(8,128)S(1)}, u32[]{:S(2)}) copy-start(f32[1,4,125,128]{3,2,1,0:T(8,128)S(1)} %get-tuple-element.151) | copy-start | bytes 768004
  124.6 6.8 %copy-start.13 = (f32[1,4,126,128]{3,2,1,0:T(8,128)}, f32[1,4,126,128]{3,2,1,0:T(8,128)S(1)}, u32[]{:S(2)}) copy-start(f32[1,4,126,128]{3,2,1,0:T(8,128)S(1)} %get-tuple-element.159) | copy-start | bytes 774148
  124.6 6.8 %copy-start.14 = (f32[1,4,126,128]{3,2,1,0:T(8,128)}, f32[1,4,126,128]{3,2,1,0:T(8,128)S(1)}, u32[]{:S(2)}) copy-start(f32[1,4,126,128]{3,2,1,0:T(8,128)S(1)} %get-tuple-element.161) | copy-start | bytes 774148
  124.7 6.8 %copy-start.15 = (f32[1,4,126,128]{3,2,1,0:T(8,128)}, f32[1,4,126,128]{3,2,1,0:T(8,128)S(1)}, u32[]{:S(2)}) copy-start(f32[1,4,126,128]{3,2,1,0:T(8,128)S(1)} %get-tuple-element.162) | copy-start | bytes 774148
  124.7 6.8 %copy-start.20 = (f32[1,4,126,128]{3,2,1,0:T(8,128)}, f32[1,4,126,128]{3,2,1,0:T(8,128)S(1)}, u32[]{:S(2)}) copy-start(f32[1,4,126,128]{3,2,1,0:T(8,128)S(1)} %get-tuple-element.160) | copy-start | bytes 774148
  124.7 6.8 %copy-start.22 = (f32[1,4,126,128]{3,2,1,0:T(8,128)}, f32[1,4,126,128]{3,2,1,0:T(8,128)S(1)}, u32[]{:S(2)}) copy-start(f32[1,4,126,128]{3,2,1,0:T(8,128)S(1)} %get-tuple-element.164) | copy-start | bytes 774148
  124.7 6.8 %copy-start.30 = (f32[1,4,126,128]{3,2,1,0:T(8,128)}, f32[1,4,126,128]{3,2,1,0:T(8,128)S(1)}, u32[]{:S(2)}) copy-start(f32[1,4,126,128]{3,2,1,0:T(8,128)S(1)} %get-tuple-element.154) | copy-start | bytes 774148
  124.7 6.8 %copy-start.32 = (f32[1,4,126,128]{3,2,1,0:T(8,128)}, f32[1,4,126,128]{3,2,1,0:T(8,128)S(1)}, u32[]{:S(2)}) copy-start(f32[1,4,126,128]{3,2,1,0:T(8,128)S(1)} %get-tuple-element.157) | copy-start | bytes 774148
  124.7 6.8 %copy-start.34 = (f32[1,4,126,128]{3,2,1,0:T(8,128)}, f32[1,4,126,128]{3,2,1,0:T(8,128)S(1)}, u32[]{:S(2)}) copy-start(f32[1,4,126,128]{3,2,1,0:T(8,128)S(1)} %get-tuple-element.166) | copy-start | bytes 774148
  124.7 6.8 %copy-start.52 = (f32[1,4,126,128]{3,2,1,0:T(8,128)}, f32[1,4,126,128]{3,2,1,0:T(8,128)S(1)}, u32[]{:S(2)}) copy-start(f32[1,4,126,128]{3,2,1,0:T(8,128)S(1)} %get-tuple-element.155) | copy-start | bytes 774148
  124.7 6.8 %copy-start.54 = (f32[1,4,126,128]{3,2,1,0:T(8,128)}, f32[1,4,126,128]{3,2,1,0:T(8,128)S(1)}, u32[]{:S(2)}) copy-start(f32[1,4,126,128]{3,2,1,0:T(8,128)S(1)} %get-tuple-element.156) | copy-start | bytes 774148
  124.7 6.8 %copy-start.56 = (f32[1,4,126,128]{3,2,1,0:T(8,128)}, f32[1,4,126,128]{3,2,1,0:T(8,128)S(1)}, u32[]{:S(2)}) copy-start(f32[1,4,126,128]{3,2,1,0:T(8,128)S(1)} %get-tuple-element.158) | copy-start | bytes 774148
  125.1 6.4 %copy-start.1 = (f32[1,4,127,128]{3,2,1,0:T(8,128)}, f32[1,4,127,128]{3,2,1,0:T(8,128)S(1)}, u32[]{:S(2)}) copy-start(f32[1,4,127,128]{3,2,1,0:T(8,128)S(1)} %get-tuple-element.176) | copy-start | bytes 780292
  125.1 6.4 %copy-start.3 = (f32[1,4,127,128]{3,2,1,0:T(8,128)}, f32[1,4,127,128]{3,2,1,0:T(8,128)S(1)}, u32[]{:S(2)}) copy-start(f32[1,4,127,128]{3,2,1,0:T(8,128)S(1)} %get-tuple-element.177) | copy-start | bytes 780292
  125.1 6.4 %copy-start.5 = (f32[1,4,127,128]{3,2,1,0:T(8,128)}, f32[1,4,127,128]{3,2,1,0:T(8,128)S(1)}, u32[]{:S(2)}) copy-start(f32[1,4,127,128]{3,2,1,0:T(8,128)S(1)} %get-tuple-element.179) | copy-start | bytes 780292
  125.1 6.4 %copy-start.16 = (f32[1,4,127,128]{3,2,1,0:T(8,128)}, f32[1,4,127,128]{3,2,1,0:T(8,128)S(1)}, u32[]{:S(2)}) copy-start(f32[1,4,127,128]{3,2,1,0:T(8,128)S(1)} %get-tuple-element.171) | copy-start | bytes 780292
  125.1 6.4 %copy-start.17 = (f32[1,4,127,128]{3,2,1,0:T(8,128)}, f32[1,4,127,128]{3,2,1,0:T(8,128)S(1)}, u32[]{:S(2)}) copy-start(f32[1,4,127,128]{3,2,1,0:T(8,128)S(1)} %get-tuple-element.173) | copy-start | bytes 780292
  125.1 6.4 %copy-start.24 = (f32[1,4,127,128]{3,2,1,0:T(8,128)}, f32[1,4,127,128]{3,2,1,0:T(8,128)S(1)}, u32[]{:S(2)}) copy-start(f32[1,4,127,128]{3,2,1,0:T(8,128)S(1)} %get-tuple-element.175) | copy-start | bytes 780292
  125.2 6.4 %copy-start.26 = (f32[1,4,127,128]{3,2,1,0:T(8,128)}, f32[1,4,127,128]{3,2,1,0:T(8,128)S(1)}, u32[]{:S(2)}) copy-start(f32[1,4,127,128]{3,2,1,0:T(8,128)S(1)} %get-tuple-element.178) | copy-start | bytes 780292
  125.2 6.4 %copy-start.36 = (f32[1,4,127,128]{3,2,1,0:T(8,128)}, f32[1,4,127,128]{3,2,1,0:T(8,128)S(1)}, u32[]{:S(2)}) copy-start(f32[1,4,127,128]{3,2,1,0:T(8,128)S(1)} %get-tuple-element.168) | copy-start | bytes 780292
  125.2 6.4 %copy-start.38 = (f32[1,4,127,128]{3,2,1,0:T(8,128)}, f32[1,4,127,128]{3,2,1,0:T(8,128)S(1)}, u32[]{:S(2)}) copy-start(f32[1,4,127,128]{3,2,1,0:T(8,128)S(1)} %get-tuple-element.169) | copy-start | bytes 780292
  125.2 6.4 %copy-start.40 = (f32[1,4,127,128]{3,2,1,0:T(8,128)}, f32[1,4,127,128]{3,2,1,0:T(8,128)S(1)}, u32[]{:S(2)}) copy-start(f32[1,4,127,128]{3,2,1,0:T(8,128)S(1)} %get-tuple-element.170) | copy-start | bytes 780292
  125.2 6.4 %copy-start.42 = (f32[1,4,127,128]{3,2,1,0:T(8,128)}, f32[1,4,127,128]{3,2,1,0:T(8,128)S(1)}, u32[]{:S(2)}) copy-start(f32[1,4,127,128]{3,2,1,0:T(8,128)S(1)} %get-tuple-element.174) | copy-start | bytes 780292
  125.2 10.4 %copy-start.58 = (f32[1,4,127,128]{3,2,1,0:T(8,128)}, f32[1,4,127,128]{3,2,1,0:T(8,128)S(1)}, u32[]{:S(2)}) copy-start(f32[1,4,127,128]{3,2,1,0:T(8,128)S(1)} %get-tuple-element.172) | copy-start | bytes 780292
  125.2 10.4 %copy-start.60 = (f32[1,4,127,128]{3,2,1,0:T(8,128)}, f32[1,4,127,128]{3,2,1,0:T(8,128)S(1)}, u32[]{:S(2)}) copy-start(f32[1,4,127,128]{3,2,1,0:T(8,128)S(1)} %get-tuple-element.180) | copy-start | bytes 780292
  125.2 10.3 %copy-start.74 = (f32[1,4,3,128]{3,2,1,0:T(4,128)}, f32[1,4,3,128]{3,2,1,0:T(4,128)S(1)}, u32[]{:S(2)}) copy-start(f32[1,4,3,128]{3,2,1,0:T(4,128)S(1)} %get-tuple-element.134) | copy-start | bytes 18436
  125.3 10.3 %copy-start.76 = (f32[1,4,3,128]{3,2,1,0:T(4,128)}, f32[1,4,3,128]{3,2,1,0:T(4,128)S(1)}, u32[]{:S(2)}) copy-start(f32[1,4,3,128]{3,2,1,0:T(4,128)S(1)} %get-tuple-element.135) | copy-start | bytes 18436
  125.3 10.3 %copy-start.78 = (f32[1,4,3,128]{3,2,1,0:T(4,128)}, f32[1,4,3,128]{3,2,1,0:T(4,128)S(1)}, u32[]{:S(2)}) copy-start(f32[1,4,3,128]{3,2,1,0:T(4,128)S(1)} %get-tuple-element.136) | copy-start | bytes 18436
  131.7 4.2 copy-start.84
  139.3 231.7 %reduce-scatter.5.cloned.1.call-start = ((), (), s32[]{:S(2)}) async-start(), calls=%async_computation.4 | async-start | bytes 270336 | tf_op jit(solution)/shard_map/reduce_scatter | solution.py:222
  216.3 17.6 %copy-start.105 = (f32[4]{0:T(128)S(1)}, f32[4]{0:T(128)}, u32[]{:S(2)}) copy-start(f32[4]{0:T(128)} %cosine_multiply_fusion) | copy-start | bytes 52
  233.8 2.8 copy-start.63
  233.9 3.9 copy-start.71
  237.7 2.1 copy-start.69
  237.7 2.1 copy-start.85
  237.7 2.6 copy-start.81
  237.7 2.6 copy-start.83
  237.8 3.3 copy-start.57
  237.8 3.3 copy-start.59
  237.8 3.3 copy-start.61
  241.4 2.0 copy-start.31
  241.4 2.0 copy-start.33
  241.4 2.0 copy-start.35
  241.4 2.0 copy-start.37
  241.4 2.0 copy-start.39
  241.4 2.0 copy-start.41
  241.4 2.0 copy-start.43
  246.5 2.1 copy-start.73
  246.5 249.5 %reduce-scatter.3.cloned.1.call-start = ((), (), s32[]{:S(2)}) async-start(), calls=%async_computation.3 | async-start | bytes 270336 | tf_op jit(solution)/shard_map/reduce_scatter | solution.py:221
  (47 other events, 65.2 us)
Sparse Core Ops, SparseCore 0:
  139.4 76.8 all-gather.1
  246.6 124.4 reduce-scatter.4
  375.6 120.3 reduce-scatter.2
where the time goes:
time: 581 us; the launch traced here: 580 us
  blocking collectives  283 us (49%)
  waiting for transfers between devices  220 us (38%)
  other arithmetic  41.3 us (7%)
  between operations  15.3 us (3%)
  matrix products  6.82 us (1%)
  local copies, waits for them, and re-layouts  6.71 us (1%)
    reduce_scatter x1, waiting for transfers between devices, on_device(): lax.psum_scatter(summed_up, 'lat', scatter_dimension=0, tiled=True)  125 us
    psum x1, blocking collectives, on_device(): lax.psum((loss_part, readout_matrix_sensitivity, affine_factor_sensitivit...  99 us
    psum x1, blocking collectives, on_device(): lax.psum((widen_matrix_sensitivity, shrink_matrix_sensitivity), 'ens')  77.3 us
    all_gather x1, waiting for transfers between devices, on_device(): lax.all_gather(sample_outlook, 'ens', axis=0, tiled=True)  74.7 us
    all_gather x1, blocking collectives, on_device(): lax.all_gather(shrink_matrix, 'lat', axis=0, tiled=True)  54 us
    all_gather x1, blocking collectives, on_device(): lax.all_gather(widen_matrix, 'lat', axis=0, tiled=True)  53 us
    reduce_scatter x1, waiting for transfers between devices, on_device(): lax.psum_scatter(summed_down, 'lat', scatter_dimension=0, tiled=True)  20.7 us
    add x16, other arithmetic, one_pair(): totals[1] + smooth_slope(gap)  17.3 us
  transfers between devices with their start and end apart: 5, of which 3 were waited for; matrix products, arithmetic and copies ran while one was open for 2% of the time, Pallas kernels for 0%

commit v1 on v0

v1 whole, which is shorter than its diff:
```python
import math

import jax
import jax.numpy as jnp
from jax import lax
from jax.sharding import PartitionSpec as P

STENCIL_SIDE = 7
SQRT_TWO_PI = 0.7978845608028654
CUBIC = 0.044715
EPSILON = 1e-06
SMOOTHING = 0.01
PER_CHUNK = 5
CHUNK_ROWS = 8


def core_swap(value):
    count = lax.axis_size("lat")
    return lax.ppermute(value, "lat", [(i, i ^ 1) for i in range(count)])


def odd_swap(value):
    count = lax.axis_size("lat")
    pairs = [(i, i + 1) for i in range(1, count - 1, 2)]
    return lax.ppermute(value, "lat", pairs + [(b, a) for a, b in pairs])


def halo_rows(field, half):
    even = lax.rem(lax.axis_index("lat"), 2) == 0
    head, tail = field[:half], field[field.shape[0] - half :]
    partner = core_swap(jnp.where(even, tail, head))
    other = odd_swap(jnp.where(even, head, tail))
    above = jnp.where(even, other, partner)
    below = jnp.where(even, partner, other)
    return above, below


def exchange(value, axis, groups=None):
    return lax.all_to_all(value, axis, 0, 0, tiled=True, axis_index_groups=groups)


def gelu_parts(u):
    inner = jnp.tanh(SQRT_TWO_PI * (u + CUBIC * u * u * u))
    value = 0.5 * u * (1.0 + inner)
    slope = 0.5 * (1.0 + inner) + 0.5 * u * (1.0 - inner * inner) * SQRT_TWO_PI * (
        1.0 + 3.0 * CUBIC * u * u
    )
    return value, slope


def depthwise(extended, taps, rows):
    half = STENCIL_SIDE // 2
    wide = extended.astype(jnp.float32)
    result = jnp.zeros((rows,) + wide.shape[1:], jnp.float32)
    for a in range(STENCIL_SIDE):
        band = wide[a : a + rows]
        for b in range(STENCIL_SIDE):
            result = result + taps[a * STENCIL_SIDE + b] * jnp.roll(band, half - b, axis=1)
    return result


def kernel_grad(extended, upstream):
    half = STENCIL_SIDE // 2
    wide = extended.astype(jnp.float32)
    rows, _, channels = upstream.shape
    taps = []
    for a in range(STENCIL_SIDE):
        band = wide[a : a + rows]
        for b in range(STENCIL_SIDE):
            shifted = jnp.roll(band, half - b, axis=1)
            taps.append(jnp.sum((upstream * shifted).reshape(-1, channels), axis=0))
    return jnp.stack(taps)


def spread_rows(table, members):
    width = table.shape[1]
    table = jnp.pad(table, ((0, members * PER_CHUNK - table.shape[0]), (0, 0)))
    table = table.reshape(members, PER_CHUNK, width)
    table = jnp.pad(table, ((0, 0), (0, CHUNK_ROWS - PER_CHUNK), (0, 0)))
    return table.reshape(members * CHUNK_ROWS, width)


def gather_rows(table, members, variables):
    width = table.shape[1]
    table = table.reshape(members, CHUNK_ROWS, width)[:, :PER_CHUNK]
    return table.reshape(members * PER_CHUNK, width)[:variables]


def on_device(
    features,
    random_perturbation,
    observed_truth,
    stencil_taps,
    affine_factor,
    widen_matrix,
    shrink_matrix,
    readout_matrix,
):
    f32, bf16 = jnp.float32, jnp.bfloat16
    rows, zonal, channels = features.shape
    variables = readout_matrix.shape[0]
    half = STENCIL_SIDE // 2
    bands, members = lax.axis_size("lat"), lax.axis_size("ens")
    band, member = lax.axis_index("lat"), lax.axis_index("ens")
    core = lax.rem(band, 2)
    points = rows * zonal
    latitudes = rows * bands
    owned = widen_matrix.shape[0]
    hidden = owned * bands

    field = (features.astype(f32) + random_perturbation[0].astype(f32)).astype(bf16)
    pair = jnp.concatenate([widen_matrix, shrink_matrix], axis=0)
    both = exchange(jnp.broadcast_to(pair[None], (bands,) + pair.shape), "lat")
    above, below = halo_rows(field, half)
    extended = jnp.concatenate([above, field, below], axis=0)
    widen = both[:, :owned].reshape(hidden, channels)
    shrink = both[:, owned:].reshape(hidden, channels)

    depth = depthwise(extended, stencil_taps, rows)
    centred = depth - jnp.mean(depth, axis=-1, keepdims=True)
    inverse = lax.rsqrt(jnp.mean(centred * centred, axis=-1, keepdims=True) + EPSILON)
    scaled = centred * inverse
    normed = (affine_factor * scaled).astype(bf16).reshape(points, channels)
    upper = lax.dot_general(normed, widen, (((1,), (1,)), ((), ())), preferred_element_type=f32)
    value, slope = gelu_parts(upper)
    gated = value.astype(bf16)
    mixed = jnp.dot(gated, shrink, preferred_element_type=f32)
    residual = (field.reshape(points, channels).astype(f32) + mixed).astype(bf16)
    readout_spread = spread_rows(readout_matrix, members)
    outlook_spread = lax.dot_general(
        readout_spread, residual, (((1,), (1,)), ((), ())), preferred_element_type=f32
    ).astype(bf16)
    sample_outlook = gather_rows(outlook_spread, members, variables).reshape(
        1, variables, rows, zonal
    )

    everyone = exchange(outlook_spread.reshape(members, CHUNK_ROWS, points), "ens").astype(f32)
    truth = lax.dynamic_index_in_dim(
        spread_rows(observed_truth.reshape(variables, points), members).reshape(
            members, CHUNK_ROWS, points
        ),
        member,
        0,
        keepdims=False,
    )
    latitude = (band * rows + jnp.arange(points, dtype=jnp.int32) // zonal).astype(f32)
    area = jnp.cos(math.pi * ((latitude + 0.5) / latitudes - 0.5))
    weight = (area * (1.0 / (latitudes * zonal)))[None, None, :]
    real = (
        lax.broadcasted_iota(jnp.int32, (1, CHUNK_ROWS, 1), 1)
        < jnp.minimum(PER_CHUNK, variables - member * PER_CHUNK)
    )
    pair_norm = 1.0 / (members * (members - 1))
    gap = everyone[:, None] - everyone[None]
    square = gap * gap + SMOOTHING
    root = lax.rsqrt(square)
    spread = jnp.sum(square * root, axis=1)
    ranks = jnp.sum(gap * root, axis=1)
    miss = everyone - truth[None]
    square = miss * miss + SMOOTHING
    root = lax.rsqrt(square)
    loss = jnp.sum(
        jnp.where(real, weight * (square * root / members - 0.5 * pair_norm * spread), 0.0)
    )
    flow = (weight * (miss * root / members - pair_norm * ranks)).astype(bf16)
    average = (spread / (members - 1)).astype(bf16)
    back = exchange(jnp.concatenate([flow, average], axis=1), "ens")
    flow = back[:, :CHUNK_ROWS].reshape(members * CHUNK_ROWS, points)
    sample_average_spread = (
        gather_rows(back[:, CHUNK_ROWS:].reshape(members * CHUNK_ROWS, points), members, variables)
        .astype(f32)
        .reshape(1, variables, rows, zonal)
    )

    readout_grad = gather_rows(
        jnp.dot(flow, residual, preferred_element_type=f32), members, variables
    )
    back_residual = lax.dot_general(
        flow, readout_spread, (((0,), (0,)), ((), ())), preferred_element_type=f32
    ).astype(bf16)
    shrink_grad = lax.dot_general(
        gated, back_residual, (((0,), (0,)), ((), ())), preferred_element_type=f32
    )
    back_gate = lax.dot_general(
        back_residual, shrink, (((1,), (1,)), ((), ())), preferred_element_type=f32
    )
    back_upper = (back_gate * slope).astype(bf16)
    widen_grad = lax.dot_general(
        back_upper, normed, (((0,), (0,)), ((), ())), preferred_element_type=f32
    )
    back_norm = jnp.dot(back_upper, widen, preferred_element_type=f32).reshape(
        rows, zonal, channels
    )
    gain_grad = jnp.sum((back_norm * scaled).reshape(-1, channels), axis=0)
    g = back_norm * affine_factor
    back_depth = inverse * (
        g
        - jnp.mean(g, axis=-1, keepdims=True)
        - scaled * jnp.mean(g * scaled, axis=-1, keepdims=True)
    )
    taps_grad = kernel_grad(extended, back_depth)

    small = jnp.concatenate(
        [
            readout_grad,
            taps_grad,
            gain_grad[None],
            jnp.broadcast_to(loss, (1, channels)),
            jnp.zeros((128 - variables - 51, channels), f32),
        ],
        axis=0,
    )
    halves = bands // 2
    share = 128 // (2 * members)
    big = jnp.stack([widen_grad, shrink_grad]).reshape(2, halves, 2, members, channels)
    packed = jnp.concatenate(
        [
            big.transpose(2, 3, 0, 1, 4).reshape(2, members, 2 * halves, channels),
            small.reshape(2, members, share, channels),
        ],
        axis=2,
    )
    mine = lax.dynamic_index_in_dim(packed, core, 0, keepdims=False)
    theirs = core_swap(lax.dynamic_index_in_dim(packed, 1 - core, 0, keepdims=False))
    part = jnp.sum(exchange(mine + theirs, "ens"), axis=0)
    same_core = [list(range(c, bands, 2)) for c in range(2)]
    outgoing = jnp.concatenate(
        [
            part[: 2 * halves].reshape(2, halves, channels).transpose(1, 0, 2),
            jnp.broadcast_to(part[None, 2 * halves :], (halves, share, channels)),
        ],
        axis=1,
    )
    done = jnp.sum(exchange(outgoing, "lat", same_core), axis=0)
    final = exchange(jnp.broadcast_to(done[None], (members,) + done.shape), "ens")
    owned_up, owned_down = final[:, 0], final[:, 1]
    half_small = final[:, 2:].reshape(members * share, channels)
    other_small = core_swap(half_small)
    low = jnp.where(core == 0, half_small, other_small)
    high = jnp.where(core == 0, other_small, half_small)
    small = jnp.concatenate([low, high], axis=0)
    return (
        small[variables + 50, 0],
        small[variables : variables + 49],
        small[variables + 49],
        owned_up,
        owned_down,
        small[:variables],
        sample_outlook,
        sample_average_spread,
    )


def solution(mesh):
    in_specs = (
        P("lat", None, None),
        P("ens", "lat", None, None),
        P(None, "lat", None),
        P(),
        P(),
        P("lat", None),
        P("lat", None),
        P(),
    )
    out_specs = (
        P(),
        P(),
        P(),
        P("lat", None),
        P("lat", None),
        P(),
        P("ens", None, "lat", None),
        P("ens", None, "lat", None),
    )
    return jax.shard_map(
        on_device, mesh=mesh, in_specs=in_specs, out_specs=out_specs, check_vma=False
    )
```

time: 581 us -> 155 us (0.27)
  the two profiles are of different devices: /device:TPU:64 before, /device:TPU:1 now
where the time goes in v1:
time: 155 us; the launch traced here: 154 us
  starting transfers between devices  59 us (38%)
  waiting for transfers between devices  29.9 us (19%)
  other arithmetic  23.4 us (15%)
  local copies, waits for them, and re-layouts  17.5 us (11%)
  blocking collectives  14 us (9%)
  matrix products  7.67 us (5%)
  between operations  2.84 us (2%)
    all_to_all x5, starting transfers between devices, exchange(): lax.all_to_all(value, axis, 0, 0, tiled=True, axis_index_groups=groups)  38.2 us
    all_to_all x5, waiting for transfers between devices, exchange(): lax.all_to_all(value, axis, 0, 0, tiled=True, axis_index_groups=groups)  28.5 us
    ppermute x3, starting transfers between devices, core_swap(): return lax.ppermute(value, 'lat', [(i, i ^ 1) for i in range(count)])  15.5 us
    all_to_all x1, blocking collectives, exchange(): lax.all_to_all(value, axis, 0, 0, tiled=True, axis_index_groups=groups)  14 us
    reduce_sum x6, other arithmetic, kernel_grad(): taps.append(jnp.sum((upstream * shifted).reshape(-1, channels), axis=0))  6.63 us
    slice x8, other arithmetic, depthwise(): jnp.roll(band, half - b, axis=1)  5.69 us
    ppermute x1, starting transfers between devices, odd_swap(): return lax.ppermute(value, 'lat', pairs + [(b, a) for a, b in pairs])  5.38 us
    reduce_sum x1, other arithmetic, on_device(): centred = depth - jnp.mean(depth, axis=-1, keepdims=True)  3.84 us
  transfers between devices with their start and end apart: 9, of which 6 were waited for; matrix products, arithmetic and copies ran while one was open for 14% of the time, Pallas kernels for 0%

profile of v1, /device:TPU:1, one launch (start us, length us, event | category | flops | bytes accessed | tf_op | source)
XLA Modules:
  0.0 154.4 jit_solution(2933842954090899825)
XLA Ops:
  0.7 1.0 fusion.33
  1.7 5.4 %collective-permute-start = (bf16[3,128,128]{2,1,0:T(8,128)(2,1)S(1)}, bf16[3,128,128]{2,1,0:T(8,128)(2,1)S(1)}, u32[]{:S(2)}, u32[]{:S(2)}) collective-permute-start(bf16[3,128,128]{2,1,0:T(8,128)(2,1)S(1)} %get-tuple-element.164), channel_id=1, source_target_pairs={{1,2},{3,4},{5,6},{7,8},{9,10},{11,12},{13,14},{15,16},{17,18},{19... | collective-permute-start | bytes 294920 | tf_op jit(solution)/shard_map/ppermute | solution.py:25
  7.1 4.0 %collective-permute-start.1 = (bf16[3,128,128]{2,1,0:T(8,128)(2,1)S(1)}, bf16[3,128,128]{2,1,0:T(8,128)(2,1)S(1)}, u32[]{:S(2)}, u32[]{:S(2)}) collective-permute-start(bf16[3,128,128]{2,1,0:T(8,128)(2,1)S(1)} %get-tuple-element.165), channel_id=1, source_target_pairs={{0,1},{1,0},{2,3},{3,2},{4,5},{5,4},{6,7},{7,6},{8,9},{9,8},{10,11... | collective-permute-start | bytes 294920 | tf_op jit(solution)/shard_map/ppermute | solution.py:19
  11.1 0.7 pad_maximum_fusion.46
  11.8 0.7 broadcast_in_dim.24
  12.6 13.3 %all-to-all-start = ((bf16[32,32,128]{2,1,0:T(8,128)(2,1)}), bf16[32,32,128]{2,1,0:T(8,128)(2,1)}, u32[]{:S(2)}, u32[]{:S(2)}) async-start(bf16[32,32,128]{2,1,0:T(8,128)(2,1)} %broadcast_in_dim.24), calls=%async_computation | async-start | bytes 524288 | tf_op jit(solution)/shard_map/all_to_all | solution.py:39
  25.9 0.6 slice_bitcast_fusion.48
  26.5 0.6 slice_bitcast_fusion.47
  27.2 0.6 pad.17
  28.8 0.3 fusion.56
  29.3 1.2 fusion.55
  30.5 1.4 maximum_convert_fusion.37
  31.9 0.6 maximum_convert_fusion.34
  32.5 0.6 maximum_convert_fusion.36
  33.3 0.6 maximum_convert_fusion.35
  34.0 0.6 maximum_convert_fusion.9
  34.6 0.6 maximum_convert_fusion.8
  35.2 0.6 maximum_convert_fusion.33
  35.8 0.6 maximum_convert_fusion.32
  37.0 3.8 %fusion.54 = (f32[4,128]{1,0:T(4,128)S(1)}, f32[4,128,128]{2,1,0:T(8,128)S(1)}) fusion(f32[4,3,128]{2,1,0:T(4,128)} %get-tuple-element.149, f32[4,125,128]{2,1,0:T(8,128)S(1)} %get-tuple-element.89, f32[128]{0:T(128)S(1)} %copy-done.130, f32[4,2,128]{2,1,0:T(2,128)} %get-tuple-element.121, f32[4,126,128]{2,1,0:T(8,128)S(1)} %get-tuple-element.101, ...), kind=kLoop, calls=%fused_computation.287 | loop fusion | flops 9174528 | bytes 13134336 | tf_op jit(solution)/shard_map/reduce_sum | solution.py:120
  41.4 1.0 fusion.59
  42.5 1.4 multiply_convert_fusion
  44.2 0.8 fusion.5
  45.1 5.2 %all-to-all-start.1 = ((bf16[16,8,512]{2,1,0:T(8,128)(2,1)}), bf16[16,8,512]{2,1,0:T(8,128)(2,1)S(1)}, u32[]{:S(2)}, u32[]{:S(2)}) async-start(bf16[16,8,512]{2,1,0:T(8,128)(2,1)} %fusion.5), calls=%async_computation.1 | async-start | bytes 262144 | tf_op jit(solution)/shard_map/all_to_all | solution.py:39
  50.5 7.0 %all-to-all-done.1 = bf16[16,8,512]{2,1,0:T(8,128)(2,1)S(1)} async-done(((bf16[16,8,512]{2,1,0:T(8,128)(2,1)}), bf16[16,8,512]{2,1,0:T(8,128)(2,1)S(1)}, u32[]{:S(2)}, u32[]{:S(2)}) %all-to-all-start.1) | async-done | bytes 131104 | tf_op jit(solution)/shard_map/all_to_all | solution.py:39
  57.6 1.2 fusion.1
  58.8 0.7 fusion.32
  59.5 0.7 pad_maximum_fusion.43
  60.3 4.4 %all-to-all-start.2 = ((bf16[16,16,512]{2,1,0:T(8,128)(2,1)}), bf16[16,16,512]{2,1,0:T(8,128)(2,1)}, u32[]{:S(2)}, u32[]{:S(2)}) async-start(bf16[16,16,512]{2,1,0:T(8,128)(2,1)} %pad_maximum_fusion.43), calls=%async_computation.2 | async-start | bytes 524288 | tf_op jit(solution)/shard_map/all_to_all | solution.py:39
  64.7 1.6 %copy.69 = f32[512,512]{0,1:T(8,128)S(1)} copy(f32[512,512]{1,0:T(8,128)} %get-tuple-element.220) | data formatting | bytes 2097152 | tf_op jit(solution)/shard_map/dot_general | solution.py:124
  66.3 6.5 %all-to-all-done.2 = bf16[16,16,512]{2,1,0:T(8,128)(2,1)} async-done(((bf16[16,16,512]{2,1,0:T(8,128)(2,1)}), bf16[16,16,512]{2,1,0:T(8,128)(2,1)}, u32[]{:S(2)}, u32[]{:S(2)}) %all-to-all-start.2) | async-done | bytes 262176 | tf_op jit(solution)/shard_map/all_to_all | solution.py:39
  72.8 1.0 slice.889
  73.8 0.9 fusion.3
  74.8 1.7 %fusion.19 = (bf16[512,512]{1,0:T(8,128)(2,1)S(1)}, f32[512,512]{1,0:T(8,128)}) fusion(f32[512,512]{1,0:T(8,128)S(1)} %copy-done.77, bf16[512,128]{1,0:T(8,128)(2,1)S(1)} %fusion.3, bf16[512,128]{1,0:T(8,128)(2,1)S(1)} %bitcast.240), kind=kOutput, calls=%fused_computation.30 | convolution fusion | flops 72089600 | bytes 2883584 | tf_op jit(solution)/shard_map/dot_general | solution.py:184
  76.5 0.8 multiply_reduce_fusion
  77.7 2.0 %multiply_reduce_fusion.7 = (f32[128]{0:T(128)}, f32[128]{0:T(128)}, f32[128]{0:T(128)}, f32[128]{0:T(128)}, f32[128]{0:T(128)}, /*index=5*/f32[128]{0:T(128)}, ...) fusion(f32[4,125,128]{2,1,0:T(8,128)S(1)} %copy-done.69, f32[4,3,128]{2,1,0:T(4,128)} %get-tuple-element.150, ...), kind=kLoop, calls=%fused_computation.108 | loop fusion | flops 2227072 | bytes 3159040 | tf_op jit(solution)/shard_map/reduce_sum | solution.py:71
  79.9 1.2 multiply_reduce_fusion.17
  81.5 1.1 multiply_reduce_fusion.28
  82.8 1.1 multiply_reduce_fusion.1
  84.0 1.1 multiply_reduce_fusion.38
  85.3 0.3 fusion.61
  85.6 1.1 fusion.34
  86.8 0.6 broadcast_in_dim.28
  87.7 0.3 copy.68
  88.0 0.7 fusion.14
  89.5 5.5 %collective-permute-start.2 = (f32[16,36,128]{2,1,0:T(8,128)S(1)}, f32[16,36,128]{2,1,0:T(8,128)S(1)}, u32[]{:S(2)}, u32[]{:S(2)}) collective-permute-start(f32[16,36,128]{2,1,0:T(8,128)S(1)} %bitcast.243), channel_id=1, source_target_pairs={{0,1},{1,0},{2,3},{3,2},{4,5},{5,4},{6,7},{7,6},{8,9},{9,8},{10,11... | collective-permute-start | bytes 884744 | tf_op jit(solution)/shard_map/ppermute | solution.py:19
  95.0 1.2 collective-permute-done.2
  96.3 14.0 %all_to_all.30 = f32[16,36,128]{2,1,0:T(8,128)S(1)} all-to-all(f32[16,36,128]{2,1,0:T(8,128)S(1)} %bitcast_add_fusion), channel_id=1, replica_groups=mesh['ens'=16,'lat'=32] {'ens'}, dimensions={0} | all-to-all | bytes 589824 | tf_op jit(solution)/shard_map/all_to_all | solution.py:39
  110.4 0.6 pad_maximum_fusion.44
  111.0 11.4 %all-to-all-start.4 = ((f32[16,6,128]{2,1,0:T(8,128)}), f32[16,6,128]{2,1,0:T(8,128)S(1)}, u32[]{:S(2)}, u32[]{:S(2)}) async-start(f32[16,6,128]{2,1,0:T(8,128)} %pad_maximum_fusion.44), calls=%async_computation.4 | async-start | bytes 131072 | tf_op jit(solution)/shard_map/all_to_all | solution.py:39
  122.5 0.9 reshape.258
  123.4 0.7 reshape.259
  124.1 0.9 slice.902
  125.1 8.7 %all-to-all-done.4 = f32[16,6,128]{2,1,0:T(8,128)S(1)} async-done(((f32[16,6,128]{2,1,0:T(8,128)}), f32[16,6,128]{2,1,0:T(8,128)S(1)}, u32[]{:S(2)}, u32[]{:S(2)}) %all-to-all-start.4) | async-done | bytes 49184 | tf_op jit(solution)/shard_map/all_to_all | solution.py:39
  133.8 0.6 broadcast_in_dim.31
  134.4 3.9 %all-to-all-start.5 = ((f32[16,6,128]{2,1,0:T(8,128)}), f32[16,6,128]{2,1,0:T(8,128)S(1)}, u32[]{:S(2)}, u32[]{:S(2)}) async-start(f32[16,6,128]{2,1,0:T(8,128)} %broadcast_in_dim.31), calls=%async_computation.5 | async-start | bytes 131072 | tf_op jit(solution)/shard_map/all_to_all | solution.py:39
  138.3 0.7 reshape.266
  139.0 6.3 %all-to-all-done.5 = f32[16,6,128]{2,1,0:T(8,128)S(1)} async-done(((f32[16,6,128]{2,1,0:T(8,128)}), f32[16,6,128]{2,1,0:T(8,128)S(1)}, u32[]{:S(2)}, u32[]{:S(2)}) %all-to-all-start.5) | async-done | bytes 49184 | tf_op jit(solution)/shard_map/all_to_all | solution.py:39
  145.3 6.0 %collective-permute-start.3 = (f32[64,128]{1,0:T(8,128)S(1)}, f32[64,128]{1,0:T(8,128)S(1)}, u32[]{:S(2)}, u32[]{:S(2)}) collective-permute-start(f32[64,128]{1,0:T(8,128)S(1)} %bitcast.245), channel_id=1, source_target_pairs={{0,1},{1,0},{2,3},{3,2},{4,5},{5,4},{6,7},{7,6},{8,9},{9,8},{10,11... | collective-permute-start | bytes 98312 | tf_op jit(solution)/shard_map/ppermute | solution.py:19
  151.2 0.6 fusion.60
  152.1 0.6 slice.896
  152.7 0.5 slice.895
  153.2 0.5 slice_bitcast_fusion
  153.7 0.6 pad_maximum_fusion.45
  (313 shorter events, 4.4 us)
Async XLA Ops:
  0.6 25.2 %copy-start.95 = (f32[49,128]{1,0:T(8,128)S(1)}, f32[49,128]{1,0:T(8,128)}, u32[]{:S(2)}) copy-start(f32[49,128]{1,0:T(8,128)} %param.11) | copy-start | bytes 75268
  0.6 26.5 %copy-start.96 = (bf16[69,128]{1,0:T(8,128)(2,1)S(1)}, bf16[69,128]{1,0:T(8,128)(2,1)}, u32[]{:S(2)}) copy-start(bf16[69,128]{1,0:T(8,128)(2,1)} %param.15) | copy-start | bytes 52996
  1.7 26.1 %collective-permute-start = (bf16[3,128,128]{2,1,0:T(8,128)(2,1)S(1)}, bf16[3,128,128]{2,1,0:T(8,128)(2,1)S(1)}, u32[]{:S(2)}, u32[]{:S(2)}) collective-permute-start(bf16[3,128,128]{2,1,0:T(8,128)(2,1)S(1)} %get-tuple-element.164), channel_id=1, source_target_pairs={{1,2},{3,4},{5,6},{7,8},{9,10},{11,12},{13,14},{15,16},{17,18},{19... | collective-permute-start | bytes 294920 | tf_op jit(solution)/shard_map/ppermute | solution.py:25
  7.1 20.8 %collective-permute-start.1 = (bf16[3,128,128]{2,1,0:T(8,128)(2,1)S(1)}, bf16[3,128,128]{2,1,0:T(8,128)(2,1)S(1)}, u32[]{:S(2)}, u32[]{:S(2)}) collective-permute-start(bf16[3,128,128]{2,1,0:T(8,128)(2,1)S(1)} %get-tuple-element.165), channel_id=1, source_target_pairs={{0,1},{1,0},{2,3},{3,2},{4,5},{5,4},{6,7},{7,6},{8,9},{9,8},{10,11... | collective-permute-start | bytes 294920 | tf_op jit(solution)/shard_map/ppermute | solution.py:19
  12.6 28.8 %all-to-all-start = ((bf16[32,32,128]{2,1,0:T(8,128)(2,1)}), bf16[32,32,128]{2,1,0:T(8,128)(2,1)}, u32[]{:S(2)}, u32[]{:S(2)}) async-start(bf16[32,32,128]{2,1,0:T(8,128)(2,1)} %broadcast_in_dim.24), calls=%async_computation | async-start | bytes 524288 | tf_op jit(solution)/shard_map/all_to_all | solution.py:39
  28.2 8.2 %copy-start.6 = (f32[4,126,128]{2,1,0:T(8,128)}, f32[4,126,128]{2,1,0:T(8,128)S(1)}, u32[]{:S(2)}) copy-start(f32[4,126,128]{2,1,0:T(8,128)S(1)} %get-tuple-element.97) | copy-start | bytes 774148
  28.3 8.2 %copy-start.8 = (f32[4,126,128]{2,1,0:T(8,128)}, f32[4,126,128]{2,1,0:T(8,128)S(1)}, u32[]{:S(2)}) copy-start(f32[4,126,128]{2,1,0:T(8,128)S(1)} %get-tuple-element.101) | copy-start | bytes 774148
  28.3 8.2 %copy-start.20 = (f32[4,126,128]{2,1,0:T(8,128)}, f32[4,126,128]{2,1,0:T(8,128)S(1)}, u32[]{:S(2)}) copy-start(f32[4,126,128]{2,1,0:T(8,128)S(1)} %get-tuple-element.96) | copy-start | bytes 774148
  28.3 8.2 %copy-start.22 = (f32[4,126,128]{2,1,0:T(8,128)}, f32[4,126,128]{2,1,0:T(8,128)S(1)}, u32[]{:S(2)}) copy-start(f32[4,126,128]{2,1,0:T(8,128)S(1)} %get-tuple-element.98) | copy-start | bytes 774148
  28.3 8.2 %copy-start.24 = (f32[4,126,128]{2,1,0:T(8,128)}, f32[4,126,128]{2,1,0:T(8,128)S(1)}, u32[]{:S(2)}) copy-start(f32[4,126,128]{2,1,0:T(8,128)S(1)} %get-tuple-element.99) | copy-start | bytes 774148
  28.3 8.2 %copy-start.30 = (f32[4,126,128]{2,1,0:T(8,128)}, f32[4,126,128]{2,1,0:T(8,128)S(1)}, u32[]{:S(2)}) copy-start(f32[4,126,128]{2,1,0:T(8,128)S(1)} %get-tuple-element.91) | copy-start | bytes 774148
  28.3 8.2 %copy-start.32 = (f32[4,126,128]{2,1,0:T(8,128)}, f32[4,126,128]{2,1,0:T(8,128)S(1)}, u32[]{:S(2)}) copy-start(f32[4,126,128]{2,1,0:T(8,128)S(1)} %get-tuple-element.94) | copy-start | bytes 774148
  28.3 8.2 %copy-start.34 = (f32[4,126,128]{2,1,0:T(8,128)}, f32[4,126,128]{2,1,0:T(8,128)S(1)}, u32[]{:S(2)}) copy-start(f32[4,126,128]{2,1,0:T(8,128)S(1)} %get-tuple-element.103) | copy-start | bytes 774148
  28.3 8.2 %copy-start.56 = (f32[4,126,128]{2,1,0:T(8,128)}, f32[4,126,128]{2,1,0:T(8,128)S(1)}, u32[]{:S(2)}) copy-start(f32[4,126,128]{2,1,0:T(8,128)S(1)} %get-tuple-element.92) | copy-start | bytes 774148
  28.3 8.2 %copy-start.58 = (f32[4,126,128]{2,1,0:T(8,128)}, f32[4,126,128]{2,1,0:T(8,128)S(1)}, u32[]{:S(2)}) copy-start(f32[4,126,128]{2,1,0:T(8,128)S(1)} %get-tuple-element.93) | copy-start | bytes 774148
  28.3 8.2 %copy-start.60 = (f32[4,126,128]{2,1,0:T(8,128)}, f32[4,126,128]{2,1,0:T(8,128)S(1)}, u32[]{:S(2)}) copy-start(f32[4,126,128]{2,1,0:T(8,128)S(1)} %get-tuple-element.95) | copy-start | bytes 774148
  28.7 7.9 %copy-start = (f32[4,127,128]{2,1,0:T(8,128)}, f32[4,127,128]{2,1,0:T(8,128)S(1)}, u32[]{:S(2)}) copy-start(f32[4,127,128]{2,1,0:T(8,128)S(1)} %get-tuple-element.114) | copy-start | bytes 780292
  28.7 7.9 %copy-start.2 = (f32[4,127,128]{2,1,0:T(8,128)}, f32[4,127,128]{2,1,0:T(8,128)S(1)}, u32[]{:S(2)}) copy-start(f32[4,127,128]{2,1,0:T(8,128)S(1)} %get-tuple-element.116) | copy-start | bytes 780292
  28.7 7.9 %copy-start.14 = (f32[4,127,128]{2,1,0:T(8,128)}, f32[4,127,128]{2,1,0:T(8,128)S(1)}, u32[]{:S(2)}) copy-start(f32[4,127,128]{2,1,0:T(8,128)S(1)} %get-tuple-element.112) | copy-start | bytes 780292
  28.7 7.9 %copy-start.16 = (f32[4,127,128]{2,1,0:T(8,128)}, f32[4,127,128]{2,1,0:T(8,128)S(1)}, u32[]{:S(2)}) copy-start(f32[4,127,128]{2,1,0:T(8,128)S(1)} %get-tuple-element.115) | copy-start | bytes 780292
  28.7 7.9 %copy-start.26 = (f32[4,127,128]{2,1,0:T(8,128)}, f32[4,127,128]{2,1,0:T(8,128)S(1)}, u32[]{:S(2)}) copy-start(f32[4,127,128]{2,1,0:T(8,128)S(1)} %get-tuple-element.108) | copy-start | bytes 780292
  28.7 7.9 %copy-start.28 = (f32[4,127,128]{2,1,0:T(8,128)}, f32[4,127,128]{2,1,0:T(8,128)S(1)}, u32[]{:S(2)}) copy-start(f32[4,127,128]{2,1,0:T(8,128)S(1)} %get-tuple-element.110) | copy-start | bytes 780292
  28.7 7.9 %copy-start.44 = (f32[4,127,128]{2,1,0:T(8,128)}, f32[4,127,128]{2,1,0:T(8,128)S(1)}, u32[]{:S(2)}) copy-start(f32[4,127,128]{2,1,0:T(8,128)S(1)} %get-tuple-element.105) | copy-start | bytes 780292
  28.7 7.9 %copy-start.46 = (f32[4,127,128]{2,1,0:T(8,128)}, f32[4,127,128]{2,1,0:T(8,128)S(1)}, u32[]{:S(2)}) copy-start(f32[4,127,128]{2,1,0:T(8,128)S(1)} %get-tuple-element.106) | copy-start | bytes 780292
  28.7 7.9 %copy-start.48 = (f32[4,127,128]{2,1,0:T(8,128)}, f32[4,127,128]{2,1,0:T(8,128)S(1)}, u32[]{:S(2)}) copy-start(f32[4,127,128]{2,1,0:T(8,128)S(1)} %get-tuple-element.107) | copy-start | bytes 780292
  28.8 7.9 %copy-start.50 = (f32[4,127,128]{2,1,0:T(8,128)}, f32[4,127,128]{2,1,0:T(8,128)S(1)}, u32[]{:S(2)}) copy-start(f32[4,127,128]{2,1,0:T(8,128)S(1)} %get-tuple-element.111) | copy-start | bytes 780292
  28.8 7.9 %copy-start.62 = (f32[4,127,128]{2,1,0:T(8,128)}, f32[4,127,128]{2,1,0:T(8,128)S(1)}, u32[]{:S(2)}) copy-start(f32[4,127,128]{2,1,0:T(8,128)S(1)} %get-tuple-element.109) | copy-start | bytes 780292
  28.8 7.9 %copy-start.64 = (f32[4,127,128]{2,1,0:T(8,128)}, f32[4,127,128]{2,1,0:T(8,128)S(1)}, u32[]{:S(2)}) copy-start(f32[4,127,128]{2,1,0:T(8,128)S(1)} %get-tuple-element.117) | copy-start | bytes 780292
  29.1 7.5 %copy-start.4 = (f32[4,125,128]{2,1,0:T(8,128)}, f32[4,125,128]{2,1,0:T(8,128)S(1)}, u32[]{:S(2)}) copy-start(f32[4,125,128]{2,1,0:T(8,128)S(1)} %get-tuple-element.76) | copy-start | bytes 768004
  29.1 7.5 %copy-start.10 = (f32[4,125,128]{2,1,0:T(8,128)}, f32[4,125,128]{2,1,0:T(8,128)S(1)}, u32[]{:S(2)}) copy-start(f32[4,125,128]{2,1,0:T(8,128)S(1)} %get-tuple-element.86) | copy-start | bytes 768004
  29.2 7.5 %copy-start.12 = (f32[4,125,128]{2,1,0:T(8,128)}, f32[4,125,128]{2,1,0:T(8,128)S(1)}, u32[]{:S(2)}) copy-start(f32[4,125,128]{2,1,0:T(8,128)S(1)} %get-tuple-element.87) | copy-start | bytes 768004
  29.2 7.5 %copy-start.18 = (f32[4,125,128]{2,1,0:T(8,128)}, f32[4,125,128]{2,1,0:T(8,128)S(1)}, u32[]{:S(2)}) copy-start(f32[4,125,128]{2,1,0:T(8,128)S(1)} %get-tuple-element.89) | copy-start | bytes 768004
  29.2 7.5 %copy-start.36 = (f32[4,125,128]{2,1,0:T(8,128)}, f32[4,125,128]{2,1,0:T(8,128)S(1)}, u32[]{:S(2)}) copy-start(f32[4,125,128]{2,1,0:T(8,128)S(1)} %get-tuple-element.78) | copy-start | bytes 768004
  29.2 7.5 %copy-start.38 = (f32[4,125,128]{2,1,0:T(8,128)}, f32[4,125,128]{2,1,0:T(8,128)S(1)}, u32[]{:S(2)}) copy-start(f32[4,125,128]{2,1,0:T(8,128)S(1)} %get-tuple-element.79) | copy-start | bytes 768004
  29.2 7.5 %copy-start.40 = (f32[4,125,128]{2,1,0:T(8,128)}, f32[4,125,128]{2,1,0:T(8,128)S(1)}, u32[]{:S(2)}) copy-start(f32[4,125,128]{2,1,0:T(8,128)S(1)} %get-tuple-element.82) | copy-start | bytes 768004
  29.2 7.5 %copy-start.42 = (f32[4,125,128]{2,1,0:T(8,128)}, f32[4,125,128]{2,1,0:T(8,128)S(1)}, u32[]{:S(2)}) copy-start(f32[4,125,128]{2,1,0:T(8,128)S(1)} %get-tuple-element.83) | copy-start | bytes 768004
  29.2 7.5 %copy-start.52 = (f32[4,125,128]{2,1,0:T(8,128)}, f32[4,125,128]{2,1,0:T(8,128)S(1)}, u32[]{:S(2)}) copy-start(f32[4,125,128]{2,1,0:T(8,128)S(1)} %get-tuple-element.81) | copy-start | bytes 768004
  29.2 7.5 %copy-start.54 = (f32[4,125,128]{2,1,0:T(8,128)}, f32[4,125,128]{2,1,0:T(8,128)S(1)}, u32[]{:S(2)}) copy-start(f32[4,125,128]{2,1,0:T(8,128)S(1)} %get-tuple-element.84) | copy-start | bytes 768004
  29.2 7.5 %copy-start.66 = (f32[4,125,128]{2,1,0:T(8,128)}, f32[4,125,128]{2,1,0:T(8,128)S(1)}, u32[]{:S(2)}) copy-start(f32[4,125,128]{2,1,0:T(8,128)S(1)} %get-tuple-element.77) | copy-start | bytes 768004
  29.2 11.6 %copy-start.68 = (f32[4,125,128]{2,1,0:T(8,128)}, f32[4,125,128]{2,1,0:T(8,128)S(1)}, u32[]{:S(2)}) copy-start(f32[4,125,128]{2,1,0:T(8,128)S(1)} %get-tuple-element.80) | copy-start | bytes 768004
  29.3 11.6 %copy-start.70 = (f32[4,125,128]{2,1,0:T(8,128)}, f32[4,125,128]{2,1,0:T(8,128)S(1)}, u32[]{:S(2)}) copy-start(f32[4,125,128]{2,1,0:T(8,128)S(1)} %get-tuple-element.85) | copy-start | bytes 768004
  29.3 11.6 %copy-start.72 = (f32[4,125,128]{2,1,0:T(8,128)}, f32[4,125,128]{2,1,0:T(8,128)S(1)}, u32[]{:S(2)}) copy-start(f32[4,125,128]{2,1,0:T(8,128)S(1)} %get-tuple-element.88) | copy-start | bytes 768004
  30.5 10.4 %copy-start.87 = (f32[4,3,128]{2,1,0:T(4,128)}, f32[4,3,128]{2,1,0:T(4,128)S(1)}, u32[]{:S(2)}) copy-start(f32[4,3,128]{2,1,0:T(4,128)S(1)} %get-tuple-element.75) | copy-start | bytes 18436
  30.5 10.4 %copy-start.89 = (f32[4,3,128]{2,1,0:T(4,128)}, f32[4,3,128]{2,1,0:T(4,128)S(1)}, u32[]{:S(2)}) copy-start(f32[4,3,128]{2,1,0:T(4,128)S(1)} %get-tuple-element.72) | copy-start | bytes 18436
  33.1 3.6 %copy-start.111 = (f32[128]{0:T(128)S(1)}, f32[128]{0:T(128)}, u32[]{:S(2)}) copy-start(f32[128]{0:T(128)} %get-tuple-element.198) | copy-start | bytes 1540
  33.1 3.6 %copy-start.112 = (f32[128]{0:T(128)S(1)}, f32[128]{0:T(128)}, u32[]{:S(2)}) copy-start(f32[128]{0:T(128)} %get-tuple-element.199) | copy-start | bytes 1540
  33.1 3.6 %copy-start.113 = (f32[128]{0:T(128)S(1)}, f32[128]{0:T(128)}, u32[]{:S(2)}) copy-start(f32[128]{0:T(128)} %get-tuple-element.200) | copy-start | bytes 1540
  33.2 3.6 %copy-start.114 = (f32[128]{0:T(128)S(1)}, f32[128]{0:T(128)}, u32[]{:S(2)}) copy-start(f32[128]{0:T(128)} %get-tuple-element.201) | copy-start | bytes 1540
  33.2 3.6 %copy-start.115 = (f32[128]{0:T(128)S(1)}, f32[128]{0:T(128)}, u32[]{:S(2)}) copy-start(f32[128]{0:T(128)} %get-tuple-element.202) | copy-start | bytes 1540
  33.2 3.6 %copy-start.116 = (f32[128]{0:T(128)S(1)}, f32[128]{0:T(128)}, u32[]{:S(2)}) copy-start(f32[128]{0:T(128)} %get-tuple-element.203) | copy-start | bytes 1540
  33.2 3.6 %copy-start.117 = (f32[128]{0:T(128)S(1)}, f32[128]{0:T(128)}, u32[]{:S(2)}) copy-start(f32[128]{0:T(128)} %get-tuple-element.204) | copy-start | bytes 1540
  33.2 3.6 %copy-start.118 = (f32[128]{0:T(128)S(1)}, f32[128]{0:T(128)}, u32[]{:S(2)}) copy-start(f32[128]{0:T(128)} %get-tuple-element.205) | copy-start | bytes 1540
  33.2 3.6 %copy-start.119 = (f32[128]{0:T(128)S(1)}, f32[128]{0:T(128)}, u32[]{:S(2)}) copy-start(f32[128]{0:T(128)} %get-tuple-element.206) | copy-start | bytes 1540
  33.2 3.6 %copy-start.120 = (f32[128]{0:T(128)S(1)}, f32[128]{0:T(128)}, u32[]{:S(2)}) copy-start(f32[128]{0:T(128)} %get-tuple-element.207) | copy-start | bytes 1540
  37.0 4.2 %copy-start.97 = (f32[128]{0:T(128)S(1)}, f32[128]{0:T(128)}, u32[]{:S(2)}) copy-start(f32[128]{0:T(128)} %param.12) | copy-start | bytes 1540
  43.9 6.6 %copy-start.74 = (bf16[512,512]{1,0:T(8,128)(2,1)}, bf16[512,512]{1,0:T(8,128)(2,1)S(1)}, u32[]{:S(2)}) copy-start(bf16[512,512]{1,0:T(8,128)(2,1)S(1)} %get-tuple-element.219) | copy-start | bytes 1572868
  43.9 6.5 %copy-start.84 = (f32[69,4,128]{2,1,0:T(4,128)S(1)}, f32[69,4,128]{2,1,0:T(4,128)}, u32[]{:S(2)}) copy-start(f32[69,4,128]{2,1,0:T(4,128)} %param.10) | copy-start | bytes 423940
  45.1 12.5 %all-to-all-start.1 = ((bf16[16,8,512]{2,1,0:T(8,128)(2,1)}), bf16[16,8,512]{2,1,0:T(8,128)(2,1)S(1)}, u32[]{:S(2)}, u32[]{:S(2)}) async-start(bf16[16,8,512]{2,1,0:T(8,128)(2,1)} %fusion.5), calls=%async_computation.1 | async-start | bytes 262144 | tf_op jit(solution)/shard_map/all_to_all | solution.py:39
  60.3 12.5 %all-to-all-start.2 = ((bf16[16,16,512]{2,1,0:T(8,128)(2,1)}), bf16[16,16,512]{2,1,0:T(8,128)(2,1)}, u32[]{:S(2)}, u32[]{:S(2)}) async-start(bf16[16,16,512]{2,1,0:T(8,128)(2,1)} %pad_maximum_fusion.43), calls=%async_computation.2 | async-start | bytes 524288 | tf_op jit(solution)/shard_map/all_to_all | solution.py:39
  64.7 10.1 %copy-start.81 = (bf16[32,16,128]{2,1,0:T(8,128)(2,1)S(1)}, bf16[32,16,128]{2,1,0:T(8,128)(2,1)}, u32[]{:S(2)}) copy-start(bf16[32,16,128]{2,1,0:T(8,128)(2,1)} %copy-done.80) | copy-start | bytes 393220
  89.5 6.7 %collective-permute-start.2 = (f32[16,36,128]{2,1,0:T(8,128)S(1)}, f32[16,36,128]{2,1,0:T(8,128)S(1)}, u32[]{:S(2)}, u32[]{:S(2)}) collective-permute-start(f32[16,36,128]{2,1,0:T(8,128)S(1)} %bitcast.243), channel_id=1, source_target_pairs={{0,1},{1,0},{2,3},{3,2},{4,5},{5,4},{6,7},{7,6},{8,9},{9,8},{10,11... | collective-permute-start | bytes 884744 | tf_op jit(solution)/shard_map/ppermute | solution.py:19
  111.0 22.7 %all-to-all-start.4 = ((f32[16,6,128]{2,1,0:T(8,128)}), f32[16,6,128]{2,1,0:T(8,128)S(1)}, u32[]{:S(2)}, u32[]{:S(2)}) async-start(f32[16,6,128]{2,1,0:T(8,128)} %pad_maximum_fusion.44), calls=%async_computation.4 | async-start | bytes 131072 | tf_op jit(solution)/shard_map/all_to_all | solution.py:39
  134.4 10.9 %all-to-all-start.5 = ((f32[16,6,128]{2,1,0:T(8,128)}), f32[16,6,128]{2,1,0:T(8,128)S(1)}, u32[]{:S(2)}, u32[]{:S(2)}) async-start(f32[16,6,128]{2,1,0:T(8,128)} %broadcast_in_dim.31), calls=%async_computation.5 | async-start | bytes 131072 | tf_op jit(solution)/shard_map/all_to_all | solution.py:39
  145.3 6.8 %collective-permute-start.3 = (f32[64,128]{1,0:T(8,128)S(1)}, f32[64,128]{1,0:T(8,128)S(1)}, u32[]{:S(2)}, u32[]{:S(2)}) collective-permute-start(f32[64,128]{1,0:T(8,128)S(1)} %bitcast.245), channel_id=1, source_target_pairs={{0,1},{1,0},{2,3},{3,2},{4,5},{5,4},{6,7},{7,6},{8,9},{9,8},{10,11... | collective-permute-start | bytes 98312 | tf_op jit(solution)/shard_map/ppermute | solution.py:19
  (77 other events, 160.1 us)

commit v2 on v1

--- a/solution.py
+++ b/solution.py
@@ -37,6 +37,25 @@
 
 def exchange(value, axis, groups=None):
     return lax.all_to_all(value, axis, 0, 0, tiled=True, axis_index_groups=groups)
+
+
+AXES = ("ens", "lat")
+
+
+def weight_groups(members, bands):
+    def at(e, band):
+        e = e if band < bands // 2 else e // 4 * 4 + (e + 2) % 4
+        return e * bands + band
+
+    return [[at(e, band) for band in range(bands)] for e in range(members)]
+
+
+def plane_groups(members, bands):
+    half = bands // 2
+    return [
+        [e * bands + h * half + rest for e in range(members) for h in range(2)]
+        for rest in range(half)
+    ]
 
 
 def gelu_parts(u):
@@ -110,7 +129,9 @@
 
     field = (features.astype(f32) + random_perturbation[0].astype(f32)).astype(bf16)
     pair = jnp.concatenate([widen_matrix, shrink_matrix], axis=0)
-    both = exchange(jnp.broadcast_to(pair[None], (bands,) + pair.shape), "lat")
+    both = exchange(
+        jnp.broadcast_to(pair[None], (bands,) + pair.shape), AXES, weight_groups(members, bands)
+    )
     above, below = halo_rows(field, half)
     extended = jnp.concatenate([above, field, below], axis=0)
     widen = both[:, :owned].reshape(hidden, channels)
@@ -210,35 +231,32 @@
         ],
         axis=0,
     )
-    halves = bands // 2
-    share = 128 // (2 * members)
-    big = jnp.stack([widen_grad, shrink_grad]).reshape(2, halves, 2, members, channels)
-    packed = jnp.concatenate(
-        [
-            big.transpose(2, 3, 0, 1, 4).reshape(2, members, 2 * halves, channels),
-            small.reshape(2, members, share, channels),
-        ],
-        axis=2,
-    )
-    mine = lax.dynamic_index_in_dim(packed, core, 0, keepdims=False)
-    theirs = core_swap(lax.dynamic_index_in_dim(packed, 1 - core, 0, keepdims=False))
-    part = jnp.sum(exchange(mine + theirs, "ens"), axis=0)
-    same_core = [list(range(c, bands, 2)) for c in range(2)]
+    depth_z = bands // 4
+    share = 128 // members
+    big = jnp.stack([widen_grad, shrink_grad]).reshape(2, 2, depth_z, 2, members, channels)
+    big = big.transpose(3, 4, 1, 0, 2, 5).reshape(2, 2 * members, 2 * depth_z, channels)
+    tail = jnp.broadcast_to(
+        small.reshape(members, 1, share, channels), (members, 2, share, channels)
+    ).reshape(2 * members, share, channels)
+    mine = lax.dynamic_index_in_dim(big, core, 0, keepdims=False)
+    sent = lax.dynamic_index_in_dim(big, 1 - core, 0, keepdims=False)
+    theirs = core_swap(jnp.concatenate([sent, tail], axis=1))
+    both_cores = jnp.concatenate([mine, tail], axis=1) + theirs
+    part = jnp.sum(exchange(both_cores, AXES, plane_groups(members, bands)), axis=0)
+    columns = [
+        list(range(h * bands // 2 + c, (h + 1) * bands // 2, 2)) for h in range(2) for c in range(2)
+    ]
     outgoing = jnp.concatenate(
         [
-            part[: 2 * halves].reshape(2, halves, channels).transpose(1, 0, 2),
-            jnp.broadcast_to(part[None, 2 * halves :], (halves, share, channels)),
+            part[: 2 * depth_z].reshape(2, depth_z, channels).transpose(1, 0, 2),
+            jnp.broadcast_to(part[None, 2 * depth_z :], (depth_z, share, channels)),
         ],
         axis=1,
     )
-    done = jnp.sum(exchange(outgoing, "lat", same_core), axis=0)
+    done = jnp.sum(exchange(outgoing, "lat", columns), axis=0)
     final = exchange(jnp.broadcast_to(done[None], (members,) + done.shape), "ens")
     owned_up, owned_down = final[:, 0], final[:, 1]
-    half_small = final[:, 2:].reshape(members * share, channels)
-    other_small = core_swap(half_small)
-    low = jnp.where(core == 0, half_small, other_small)
-    high = jnp.where(core == 0, other_small, half_small)
-    small = jnp.concatenate([low, high], axis=0)
+    small = final[:, 2:].reshape(members * share, channels)
     return (
         small[variables + 50, 0],
         small[variables : variables + 49],

time: 155 us -> 153 us (0.987)
  the two profiles are of different devices: /device:TPU:1 before, /device:TPU:8 now
where the time goes in v2:
time: 153 us; the launch traced here: 152 us
  starting transfers between devices  44.7 us (29%)
  waiting for transfers between devices  28.6 us (19%)
  other arithmetic  26 us (17%)
  blocking collectives  22.3 us (15%)
  local copies, waits for them, and re-layouts  19.1 us (12%)
  matrix products  7.7 us (5%)
  between operations  3.28 us (2%)
    all_to_all x5, starting transfers between devices, exchange(): lax.all_to_all(value, axis, 0, 0, tiled=True, axis_index_groups=groups)  36.5 us
    all_to_all x5, waiting for transfers between devices, exchange(): lax.all_to_all(value, axis, 0, 0, tiled=True, axis_index_groups=groups)  26.9 us
    all_to_all x1, blocking collectives, exchange(): lax.all_to_all(value, axis, 0, 0, tiled=True, axis_index_groups=groups)  22.3 us
    reduce_sum x6, other arithmetic, kernel_grad(): taps.append(jnp.sum((upstream * shifted).reshape(-1, channels), axis=0))  10.2 us
    ppermute x2, starting transfers between devices, core_swap(): return lax.ppermute(value, 'lat', [(i, i ^ 1) for i in range(count)])  7.56 us
    slice x8, other arithmetic, depthwise(): jnp.roll(band, half - b, axis=1)  5.49 us
    reduce_sum x1, other arithmetic, on_device(): centred = depth - jnp.mean(depth, axis=-1, keepdims=True)  3.81 us
  transfers between devices with their start and end apart: 8, of which 6 were waited for; matrix products, arithmetic and copies ran while one was open for 13% of the time, Pallas kernels for 0%

profile of v2, /device:TPU:8, one launch (start us, length us, event | category | flops | bytes accessed | tf_op | source)
XLA Modules:
  0.0 151.7 jit_solution(4733570253506172628)
XLA Ops:
  0.7 1.0 fusion.32
  1.7 0.7 collective-permute-start
  2.4 5.6 %collective-permute-start.1 = (bf16[3,128,128]{2,1,0:T(8,128)(2,1)S(1)}, bf16[3,128,128]{2,1,0:T(8,128)(2,1)S(1)}, u32[]{:S(2)}, u32[]{:S(2)}) collective-permute-start(bf16[3,128,128]{2,1,0:T(8,128)(2,1)S(1)} %get-tuple-element.167), channel_id=1, source_target_pairs={{0,1},{1,0},{2,3},{3,2},{4,5},{5,4},{6,7},{7,6},{8,9},{9,8},{10,11... | collective-permute-start | bytes 294920 | tf_op jit(solution)/shard_map/ppermute | solution.py:19
  8.0 0.7 pad_maximum_fusion.46
  8.7 0.7 broadcast_in_dim.28
  9.5 13.5 %all-to-all-start = ((bf16[32,32,128]{2,1,0:T(8,128)(2,1)}), bf16[32,32,128]{2,1,0:T(8,128)(2,1)}, u32[]{:S(2)}, u32[]{:S(2)}) async-start(bf16[32,32,128]{2,1,0:T(8,128)(2,1)} %broadcast_in_dim.28), calls=%async_computation | async-start | bytes 524288 | tf_op jit(solution)/shard_map/all_to_all | solution.py:39
  23.0 0.6 slice_bitcast_fusion.50
  23.6 0.6 slice_bitcast_fusion.49
  24.3 0.6 pad.17
  25.0 0.6 maximum_convert_fusion.9
  25.7 0.6 maximum_convert_fusion.37
  27.1 1.1 maximum_convert_fusion.36
  28.2 0.4 fusion.57
  29.0 0.6 maximum_convert_fusion.35
  29.6 0.7 maximum_convert_fusion.34
  30.3 0.6 maximum_convert_fusion.8
  31.0 0.6 fusion.54
  31.6 0.6 maximum_convert_fusion.33
  32.2 0.6 maximum_convert_fusion.32
  33.2 3.8 %fusion.53 = (f32[4,128]{1,0:T(4,128)S(1)}, f32[4,128,128]{2,1,0:T(8,128)S(1)}) fusion(f32[4,3,128]{2,1,0:T(4,128)S(1)} %get-tuple-element.149, f32[4,125,128]{2,1,0:T(8,128)S(1)} %get-tuple-element.89, f32[128]{0:T(128)S(1)} %copy-done.160, f32[4,2,128]{2,1,0:T(2,128)} %get-tuple-element.121, f32[4,126,128]{2,1,0:T(8,128)S(1)} %get-tuple-element.101, ...), kind=kLoop, calls=%fused_computation.283 | loop fusion | flops 9174528 | bytes 13134336 | tf_op jit(solution)/shard_map/reduce_sum | solution.py:141
  37.7 0.6 all-to-all-done
  38.3 1.0 fusion.58
  39.3 1.4 multiply_convert_fusion
  41.1 0.8 fusion.5
  41.9 6.5 %all-to-all-start.1 = ((bf16[16,8,512]{2,1,0:T(8,128)(2,1)}), bf16[16,8,512]{2,1,0:T(8,128)(2,1)S(1)}, u32[]{:S(2)}, u32[]{:S(2)}) async-start(bf16[16,8,512]{2,1,0:T(8,128)(2,1)} %fusion.5), calls=%async_computation.1 | async-start | bytes 262144 | tf_op jit(solution)/shard_map/all_to_all | solution.py:39
  48.6 7.1 %all-to-all-done.1 = bf16[16,8,512]{2,1,0:T(8,128)(2,1)S(1)} async-done(((bf16[16,8,512]{2,1,0:T(8,128)(2,1)}), bf16[16,8,512]{2,1,0:T(8,128)(2,1)S(1)}, u32[]{:S(2)}, u32[]{:S(2)}) %all-to-all-start.1) | async-done | bytes 131104 | tf_op jit(solution)/shard_map/all_to_all | solution.py:39
  55.7 1.2 fusion.1
  56.9 0.7 fusion.31
  57.7 0.7 pad_maximum_fusion.44
  58.4 5.1 %all-to-all-start.2 = ((bf16[16,16,512]{2,1,0:T(8,128)(2,1)}), bf16[16,16,512]{2,1,0:T(8,128)(2,1)}, u32[]{:S(2)}, u32[]{:S(2)}) async-start(bf16[16,16,512]{2,1,0:T(8,128)(2,1)} %pad_maximum_fusion.44), calls=%async_computation.2 | async-start | bytes 524288 | tf_op jit(solution)/shard_map/all_to_all | solution.py:39
  63.5 1.6 %copy.63 = f32[512,512]{0,1:T(8,128)S(1)} copy(f32[512,512]{1,0:T(8,128)} %get-tuple-element.218) | data formatting | bytes 2097152 | tf_op jit(solution)/shard_map/dot_general | solution.py:145
  65.1 6.9 %all-to-all-done.2 = bf16[16,16,512]{2,1,0:T(8,128)(2,1)} async-done(((bf16[16,16,512]{2,1,0:T(8,128)(2,1)}), bf16[16,16,512]{2,1,0:T(8,128)(2,1)}, u32[]{:S(2)}, u32[]{:S(2)}) %all-to-all-start.2) | async-done | bytes 262176 | tf_op jit(solution)/shard_map/all_to_all | solution.py:39
  72.1 1.0 slice.889
  73.1 0.9 fusion.3
  74.1 1.7 %fusion.19 = (bf16[512,512]{1,0:T(8,128)(2,1)S(1)}, f32[512,512]{1,0:T(8,128)}) fusion(f32[512,512]{1,0:T(8,128)S(1)} %copy-done.77, bf16[512,128]{1,0:T(8,128)(2,1)S(1)} %fusion.3, bf16[512,128]{1,0:T(8,128)(2,1)S(1)} %bitcast.244), kind=kOutput, calls=%fused_computation.30 | convolution fusion | flops 72089600 | bytes 2883584 | tf_op jit(solution)/shard_map/dot_general | solution.py:205
  75.9 0.8 multiply_reduce_fusion
  77.1 2.0 %multiply_reduce_fusion.7 = (f32[128]{0:T(128)}, f32[128]{0:T(128)}, f32[128]{0:T(128)}, f32[128]{0:T(128)}, f32[128]{0:T(128)}, /*index=5*/f32[128]{0:T(128)}, ...) fusion(f32[4,125,128]{2,1,0:T(8,128)S(1)} %copy-done.51, f32[4,3,128]{2,1,0:T(4,128)} %get-tuple-element.150, ...), kind=kLoop, calls=%fused_computation.104 | loop fusion | flops 2227072 | bytes 3159040 | tf_op jit(solution)/shard_map/reduce_sum | solution.py:90
  79.1 1.3 multiply_reduce_fusion.49
  80.5 1.8 %multiply_reduce_fusion.38 = (f32[128]{0:T(128)}, f32[128]{0:T(128)}, f32[128]{0:T(128)}, f32[128]{0:T(128)}, f32[128]{0:T(128)}, /*index=5*/f32[128]{0:T(128)}, f32[128]{0:T(128)}, f32[128]{0:T(128)}, f32[128]{0:T(128)}) fusion(f32[4,128,128]{2,1,0:T(8,128)S(1)} %get-tuple-element.68, f32[4,1,128]{2,1,0:T(1,128)} %get-tuple-element.147, ...), kind=kLoop, calls=%fused_computation.135 | loop fusion | flops 1768320 | bytes 2626048 | tf_op jit(solution)/shard_map/reduce_sum | solution.py:90
  82.4 1.7 %multiply_reduce_fusion.1 = (f32[128]{0:T(128)}, f32[128]{0:T(128)}, f32[128]{0:T(128)}, f32[128]{0:T(128)}, f32[128]{0:T(128)}, /*index=5*/f32[128]{0:T(128)}, ...) fusion(f32[4,128,128]{2,1,0:T(8,128)S(1)} %get-tuple-element.68, ...), kind=kLoop, calls=%fused_computation.98 | loop fusion | flops 1899008 | bytes 3414016 | tf_op jit(solution)/shard_map/reduce_sum | solution.py:90
  84.2 1.7 %multiply_reduce_fusion.28 = (f32[128]{0:T(128)S(1)}, f32[128]{0:T(128)S(1)}, f32[128]{0:T(128)}, f32[128]{0:T(128)}, f32[128]{0:T(128)}, /*index=5*/f32[128]{0:T(128)}, f32[128]{0:T(128)}, f32[128]{0:T(128)}, f32[128]{0:T(128)}) fusion(f32[4,128,128]{2,1,0:T(8,128)S(1)} %get-tuple-element.68, f32[4,125,128]{2,1,0:T(8,128)S(1)} %copy-done.1, ...), kind=kLoop, calls=%fused_computation.125 | loop fusion | flops 1768320 | bytes 2626048 | tf_op jit(solution)/shard_map/reduce_sum | solution.py:90
  86.0 1.7 %multiply_reduce_fusion.17 = (f32[128]{0:T(128)S(1)}, f32[128]{0:T(128)S(1)}, f32[128]{0:T(128)}, f32[128]{0:T(128)}, f32[128]{0:T(128)}, /*index=5*/f32[128]{0:T(128)}, f32[128]{0:T(128)}, f32[128]{0:T(128)}, f32[128]{0:T(128)}) fusion(f32[4,128,128]{2,1,0:T(8,128)S(1)} %get-tuple-element.68, f32[4,1,128]{2,1,0:T(1,128)} %get-tuple-element.131, ...), kind=kLoop, calls=%fused_computation.114 | loop fusion | flops 1768320 | bytes 2626048 | tf_op jit(solution)/shard_map/reduce_sum | solution.py:90
  88.0 1.1 fusion.33
  89.7 0.7 fusion.14
  91.7 0.6 broadcast_in_dim.32
  92.8 1.5 concatenate.241
  94.3 1.9 %collective-permute-start.2 = (f32[32,24,128]{2,1,0:T(8,128)S(1)}, f32[32,24,128]{2,1,0:T(8,128)S(1)}, u32[]{:S(2)}, u32[]{:S(2)}) collective-permute-start(f32[32,24,128]{2,1,0:T(8,128)S(1)} %pad_maximum_fusion), channel_id=1, source_target_pairs={{0,1},{1,0},{2,3},{3,2},{4,5},{5,4},{6,7},{7,6},{8,9},{9,8},{10,11... | collective-permute-start | bytes 1179656 | tf_op jit(solution)/shard_map/ppermute | solution.py:19
  96.3 1.7 %collective-permute-done.2 = f32[32,24,128]{2,1,0:T(8,128)S(1)} collective-permute-done((f32[32,24,128]{2,1,0:T(8,128)S(1)}, f32[32,24,128]{2,1,0:T(8,128)S(1)}, u32[]{:S(2)}, u32[]{:S(2)}) %collective-permute-start.2) | collective-permute-done | bytes 393248 | tf_op jit(solution)/shard_map/ppermute | solution.py:19
  98.0 22.3 %all_to_all.30 = f32[32,24,128]{2,1,0:T(8,128)S(1)} all-to-all(f32[32,24,128]{2,1,0:T(8,128)S(1)} %fusion.22), channel_id=1, replica_groups={{0,16,32,48,64,80,96,112,128,144,160,176,192,208,224,240,256,272,288,30..., dimensions={0} | all-to-all | bytes 786432 | tf_op jit(solution)/shard_map/all_to_all | solution.py:39
  120.4 0.6 pad_maximum_fusion.45
  121.0 6.7 %all-to-all-start.4 = ((f32[8,10,128]{2,1,0:T(8,128)}), f32[8,10,128]{2,1,0:T(8,128)S(1)}, u32[]{:S(2)}, u32[]{:S(2)}) async-start(f32[8,10,128]{2,1,0:T(8,128)} %pad_maximum_fusion.45), calls=%async_computation.4 | async-start | bytes 131072 | tf_op jit(solution)/shard_map/all_to_all | solution.py:39
  127.7 0.9 reshape.260
  128.7 0.7 reshape.261
  129.4 0.9 slice.903
  130.4 5.8 %all-to-all-done.4 = f32[8,10,128]{2,1,0:T(8,128)S(1)} async-done(((f32[8,10,128]{2,1,0:T(8,128)}), f32[8,10,128]{2,1,0:T(8,128)S(1)}, u32[]{:S(2)}, u32[]{:S(2)}) %all-to-all-start.4) | async-done | bytes 40992 | tf_op jit(solution)/shard_map/all_to_all | solution.py:39
  136.1 0.7 broadcast_in_dim.65
  136.8 4.7 %all-to-all-start.5 = ((f32[16,10,128]{2,1,0:T(8,128)}), f32[16,10,128]{2,1,0:T(8,128)S(1)}, u32[]{:S(2)}, u32[]{:S(2)}) async-start(f32[16,10,128]{2,1,0:T(8,128)} %broadcast_in_dim.65), calls=%async_computation.5 | async-start | bytes 262144 | tf_op jit(solution)/shard_map/all_to_all | solution.py:39
  141.5 0.7 reshape.268
  142.2 6.6 %all-to-all-done.5 = f32[16,10,128]{2,1,0:T(8,128)S(1)} async-done(((f32[16,10,128]{2,1,0:T(8,128)}), f32[16,10,128]{2,1,0:T(8,128)S(1)}, u32[]{:S(2)}, u32[]{:S(2)}) %all-to-all-start.5) | async-done | bytes 81952 | tf_op jit(solution)/shard_map/all_to_all | solution.py:39
  148.8 0.5 slice.895
  149.3 0.6 slice.896
  149.9 0.5 slice_bitcast_fusion.2
  150.4 0.6 slice.900
  151.0 0.6 fusion.59
  (372 shorter events, 4.7 us)
Async XLA Ops:
  0.6 22.3 %copy-start.96 = (f32[49,128]{1,0:T(8,128)S(1)}, f32[49,128]{1,0:T(8,128)}, u32[]{:S(2)}) copy-start(f32[49,128]{1,0:T(8,128)} %param.11) | copy-start | bytes 75268
  0.6 23.6 %copy-start.97 = (bf16[69,128]{1,0:T(8,128)(2,1)S(1)}, bf16[69,128]{1,0:T(8,128)(2,1)}, u32[]{:S(2)}) copy-start(bf16[69,128]{1,0:T(8,128)(2,1)} %param.15) | copy-start | bytes 52996
  1.7 23.3 %collective-permute-start = (bf16[3,128,128]{2,1,0:T(8,128)(2,1)S(1)}, bf16[3,128,128]{2,1,0:T(8,128)(2,1)S(1)}, u32[]{:S(2)}, u32[]{:S(2)}) collective-permute-start(bf16[3,128,128]{2,1,0:T(8,128)(2,1)S(1)} %get-tuple-element.166), channel_id=1, source_target_pairs={{1,2},{3,4},{5,6},{7,8},{9,10},{11,12},{13,14},{15,16},{17,18},{19... | collective-permute-start | bytes 294920 | tf_op jit(solution)/shard_map/ppermute | solution.py:25
  2.4 22.6 %collective-permute-start.1 = (bf16[3,128,128]{2,1,0:T(8,128)(2,1)S(1)}, bf16[3,128,128]{2,1,0:T(8,128)(2,1)S(1)}, u32[]{:S(2)}, u32[]{:S(2)}) collective-permute-start(bf16[3,128,128]{2,1,0:T(8,128)(2,1)S(1)} %get-tuple-element.167), channel_id=1, source_target_pairs={{0,1},{1,0},{2,3},{3,2},{4,5},{5,4},{6,7},{7,6},{8,9},{9,8},{10,11... | collective-permute-start | bytes 294920 | tf_op jit(solution)/shard_map/ppermute | solution.py:19
  9.5 28.9 %all-to-all-start = ((bf16[32,32,128]{2,1,0:T(8,128)(2,1)}), bf16[32,32,128]{2,1,0:T(8,128)(2,1)}, u32[]{:S(2)}, u32[]{:S(2)}) async-start(bf16[32,32,128]{2,1,0:T(8,128)(2,1)} %broadcast_in_dim.28), calls=%async_computation | async-start | bytes 524288 | tf_op jit(solution)/shard_map/all_to_all | solution.py:39
  26.6 6.2 %copy-start = (f32[4,125,128]{2,1,0:T(8,128)}, f32[4,125,128]{2,1,0:T(8,128)S(1)}, u32[]{:S(2)}) copy-start(f32[4,125,128]{2,1,0:T(8,128)S(1)} %get-tuple-element.78) | copy-start | bytes 768004
  26.6 6.2 %copy-start.2 = (f32[4,125,128]{2,1,0:T(8,128)}, f32[4,125,128]{2,1,0:T(8,128)S(1)}, u32[]{:S(2)}) copy-start(f32[4,125,128]{2,1,0:T(8,128)S(1)} %get-tuple-element.79) | copy-start | bytes 768004
  26.6 6.2 %copy-start.4 = (f32[4,125,128]{2,1,0:T(8,128)}, f32[4,125,128]{2,1,0:T(8,128)S(1)}, u32[]{:S(2)}) copy-start(f32[4,125,128]{2,1,0:T(8,128)S(1)} %get-tuple-element.82) | copy-start | bytes 768004
  26.6 6.2 %copy-start.6 = (f32[4,125,128]{2,1,0:T(8,128)}, f32[4,125,128]{2,1,0:T(8,128)S(1)}, u32[]{:S(2)}) copy-start(f32[4,125,128]{2,1,0:T(8,128)S(1)} %get-tuple-element.83) | copy-start | bytes 768004
  26.6 6.2 %copy-start.22 = (f32[4,125,128]{2,1,0:T(8,128)}, f32[4,125,128]{2,1,0:T(8,128)S(1)}, u32[]{:S(2)}) copy-start(f32[4,125,128]{2,1,0:T(8,128)S(1)} %get-tuple-element.89) | copy-start | bytes 768004
  26.6 6.2 %copy-start.36 = (f32[4,125,128]{2,1,0:T(8,128)}, f32[4,125,128]{2,1,0:T(8,128)S(1)}, u32[]{:S(2)}) copy-start(f32[4,125,128]{2,1,0:T(8,128)S(1)} %get-tuple-element.86) | copy-start | bytes 768004
  26.7 6.2 %copy-start.38 = (f32[4,125,128]{2,1,0:T(8,128)}, f32[4,125,128]{2,1,0:T(8,128)S(1)}, u32[]{:S(2)}) copy-start(f32[4,125,128]{2,1,0:T(8,128)S(1)} %get-tuple-element.87) | copy-start | bytes 768004
  26.7 6.2 %copy-start.46 = (f32[4,125,128]{2,1,0:T(8,128)}, f32[4,125,128]{2,1,0:T(8,128)S(1)}, u32[]{:S(2)}) copy-start(f32[4,125,128]{2,1,0:T(8,128)S(1)} %get-tuple-element.76) | copy-start | bytes 768004
  26.7 6.2 %copy-start.48 = (f32[4,125,128]{2,1,0:T(8,128)}, f32[4,125,128]{2,1,0:T(8,128)S(1)}, u32[]{:S(2)}) copy-start(f32[4,125,128]{2,1,0:T(8,128)S(1)} %get-tuple-element.77) | copy-start | bytes 768004
  26.7 6.2 %copy-start.50 = (f32[4,125,128]{2,1,0:T(8,128)}, f32[4,125,128]{2,1,0:T(8,128)S(1)}, u32[]{:S(2)}) copy-start(f32[4,125,128]{2,1,0:T(8,128)S(1)} %get-tuple-element.80) | copy-start | bytes 768004
  26.7 6.2 %copy-start.52 = (f32[4,125,128]{2,1,0:T(8,128)}, f32[4,125,128]{2,1,0:T(8,128)S(1)}, u32[]{:S(2)}) copy-start(f32[4,125,128]{2,1,0:T(8,128)S(1)} %get-tuple-element.85) | copy-start | bytes 768004
  26.7 6.2 %copy-start.54 = (f32[4,125,128]{2,1,0:T(8,128)}, f32[4,125,128]{2,1,0:T(8,128)S(1)}, u32[]{:S(2)}) copy-start(f32[4,125,128]{2,1,0:T(8,128)S(1)} %get-tuple-element.88) | copy-start | bytes 768004
  27.0 5.8 %copy-start.16 = (f32[4,126,128]{2,1,0:T(8,128)}, f32[4,126,128]{2,1,0:T(8,128)S(1)}, u32[]{:S(2)}) copy-start(f32[4,126,128]{2,1,0:T(8,128)S(1)} %get-tuple-element.96) | copy-start | bytes 774148
  27.0 5.8 %copy-start.18 = (f32[4,126,128]{2,1,0:T(8,128)}, f32[4,126,128]{2,1,0:T(8,128)S(1)}, u32[]{:S(2)}) copy-start(f32[4,126,128]{2,1,0:T(8,128)S(1)} %get-tuple-element.98) | copy-start | bytes 774148
  27.1 5.8 %copy-start.20 = (f32[4,126,128]{2,1,0:T(8,128)}, f32[4,126,128]{2,1,0:T(8,128)S(1)}, u32[]{:S(2)}) copy-start(f32[4,126,128]{2,1,0:T(8,128)S(1)} %get-tuple-element.99) | copy-start | bytes 774148
  27.1 5.8 %copy-start.24 = (f32[4,126,128]{2,1,0:T(8,128)}, f32[4,126,128]{2,1,0:T(8,128)S(1)}, u32[]{:S(2)}) copy-start(f32[4,126,128]{2,1,0:T(8,128)S(1)} %get-tuple-element.97) | copy-start | bytes 774148
  27.1 5.8 %copy-start.26 = (f32[4,126,128]{2,1,0:T(8,128)}, f32[4,126,128]{2,1,0:T(8,128)S(1)}, u32[]{:S(2)}) copy-start(f32[4,126,128]{2,1,0:T(8,128)S(1)} %get-tuple-element.101) | copy-start | bytes 774148
  27.1 5.8 %copy-start.40 = (f32[4,126,128]{2,1,0:T(8,128)}, f32[4,126,128]{2,1,0:T(8,128)S(1)}, u32[]{:S(2)}) copy-start(f32[4,126,128]{2,1,0:T(8,128)S(1)} %get-tuple-element.90) | copy-start | bytes 774148
  27.1 5.8 %copy-start.42 = (f32[4,126,128]{2,1,0:T(8,128)}, f32[4,126,128]{2,1,0:T(8,128)S(1)}, u32[]{:S(2)}) copy-start(f32[4,126,128]{2,1,0:T(8,128)S(1)} %get-tuple-element.100) | copy-start | bytes 774148
  27.1 5.8 %copy-start.44 = (f32[4,126,128]{2,1,0:T(8,128)}, f32[4,126,128]{2,1,0:T(8,128)S(1)}, u32[]{:S(2)}) copy-start(f32[4,126,128]{2,1,0:T(8,128)S(1)} %get-tuple-element.102) | copy-start | bytes 774148
  27.1 5.8 %copy-start.64 = (f32[4,126,128]{2,1,0:T(8,128)}, f32[4,126,128]{2,1,0:T(8,128)S(1)}, u32[]{:S(2)}) copy-start(f32[4,126,128]{2,1,0:T(8,128)S(1)} %get-tuple-element.92) | copy-start | bytes 774148
  27.1 5.8 %copy-start.66 = (f32[4,126,128]{2,1,0:T(8,128)}, f32[4,126,128]{2,1,0:T(8,128)S(1)}, u32[]{:S(2)}) copy-start(f32[4,126,128]{2,1,0:T(8,128)S(1)} %get-tuple-element.93) | copy-start | bytes 774148
  27.1 5.8 %copy-start.68 = (f32[4,126,128]{2,1,0:T(8,128)}, f32[4,126,128]{2,1,0:T(8,128)S(1)}, u32[]{:S(2)}) copy-start(f32[4,126,128]{2,1,0:T(8,128)S(1)} %get-tuple-element.95) | copy-start | bytes 774148
  28.6 8.4 %copy-start.8 = (f32[4,127,128]{2,1,0:T(8,128)}, f32[4,127,128]{2,1,0:T(8,128)S(1)}, u32[]{:S(2)}) copy-start(f32[4,127,128]{2,1,0:T(8,128)S(1)} %get-tuple-element.105) | copy-start | bytes 780292
  28.6 8.4 %copy-start.10 = (f32[4,127,128]{2,1,0:T(8,128)}, f32[4,127,128]{2,1,0:T(8,128)S(1)}, u32[]{:S(2)}) copy-start(f32[4,127,128]{2,1,0:T(8,128)S(1)} %get-tuple-element.106) | copy-start | bytes 780292
  28.6 8.4 %copy-start.12 = (f32[4,127,128]{2,1,0:T(8,128)}, f32[4,127,128]{2,1,0:T(8,128)S(1)}, u32[]{:S(2)}) copy-start(f32[4,127,128]{2,1,0:T(8,128)S(1)} %get-tuple-element.107) | copy-start | bytes 780292
  28.6 8.4 %copy-start.14 = (f32[4,127,128]{2,1,0:T(8,128)}, f32[4,127,128]{2,1,0:T(8,128)S(1)}, u32[]{:S(2)}) copy-start(f32[4,127,128]{2,1,0:T(8,128)S(1)} %get-tuple-element.111) | copy-start | bytes 780292
  28.7 8.4 %copy-start.28 = (f32[4,127,128]{2,1,0:T(8,128)}, f32[4,127,128]{2,1,0:T(8,128)S(1)}, u32[]{:S(2)}) copy-start(f32[4,127,128]{2,1,0:T(8,128)S(1)} %get-tuple-element.108) | copy-start | bytes 780292
  28.7 8.4 %copy-start.30 = (f32[4,127,128]{2,1,0:T(8,128)}, f32[4,127,128]{2,1,0:T(8,128)S(1)}, u32[]{:S(2)}) copy-start(f32[4,127,128]{2,1,0:T(8,128)S(1)} %get-tuple-element.110) | copy-start | bytes 780292
  28.7 8.4 %copy-start.32 = (f32[4,127,128]{2,1,0:T(8,128)}, f32[4,127,128]{2,1,0:T(8,128)S(1)}, u32[]{:S(2)}) copy-start(f32[4,127,128]{2,1,0:T(8,128)S(1)} %get-tuple-element.112) | copy-start | bytes 780292
  28.7 8.4 %copy-start.34 = (f32[4,127,128]{2,1,0:T(8,128)}, f32[4,127,128]{2,1,0:T(8,128)S(1)}, u32[]{:S(2)}) copy-start(f32[4,127,128]{2,1,0:T(8,128)S(1)} %get-tuple-element.115) | copy-start | bytes 780292
  28.7 8.4 %copy-start.56 = (f32[4,127,128]{2,1,0:T(8,128)}, f32[4,127,128]{2,1,0:T(8,128)S(1)}, u32[]{:S(2)}) copy-start(f32[4,127,128]{2,1,0:T(8,128)S(1)} %get-tuple-element.104) | copy-start | bytes 780292
  28.7 8.4 %copy-start.58 = (f32[4,127,128]{2,1,0:T(8,128)}, f32[4,127,128]{2,1,0:T(8,128)S(1)}, u32[]{:S(2)}) copy-start(f32[4,127,128]{2,1,0:T(8,128)S(1)} %get-tuple-element.113) | copy-start | bytes 780292
  28.7 8.4 %copy-start.60 = (f32[4,127,128]{2,1,0:T(8,128)}, f32[4,127,128]{2,1,0:T(8,128)S(1)}, u32[]{:S(2)}) copy-start(f32[4,127,128]{2,1,0:T(8,128)S(1)} %get-tuple-element.114) | copy-start | bytes 780292
  28.7 8.4 %copy-start.62 = (f32[4,127,128]{2,1,0:T(8,128)}, f32[4,127,128]{2,1,0:T(8,128)S(1)}, u32[]{:S(2)}) copy-start(f32[4,127,128]{2,1,0:T(8,128)S(1)} %get-tuple-element.116) | copy-start | bytes 780292
  28.7 8.4 %copy-start.70 = (f32[4,127,128]{2,1,0:T(8,128)}, f32[4,127,128]{2,1,0:T(8,128)S(1)}, u32[]{:S(2)}) copy-start(f32[4,127,128]{2,1,0:T(8,128)S(1)} %get-tuple-element.109) | copy-start | bytes 780292
  28.7 8.4 %copy-start.72 = (f32[4,127,128]{2,1,0:T(8,128)}, f32[4,127,128]{2,1,0:T(8,128)S(1)}, u32[]{:S(2)}) copy-start(f32[4,127,128]{2,1,0:T(8,128)S(1)} %get-tuple-element.117) | copy-start | bytes 780292
  28.8 4.2 %copy-start.139 = (f32[128]{0:T(128)S(1)}, f32[128]{0:T(128)}, u32[]{:S(2)}) copy-start(f32[128]{0:T(128)} %get-tuple-element.194) | copy-start | bytes 1540
  28.8 4.2 %copy-start.140 = (f32[128]{0:T(128)S(1)}, f32[128]{0:T(128)}, u32[]{:S(2)}) copy-start(f32[128]{0:T(128)} %get-tuple-element.195) | copy-start | bytes 1540
  28.8 4.2 %copy-start.141 = (f32[128]{0:T(128)S(1)}, f32[128]{0:T(128)}, u32[]{:S(2)}) copy-start(f32[128]{0:T(128)} %get-tuple-element.196) | copy-start | bytes 1540
  28.8 4.2 %copy-start.142 = (f32[128]{0:T(128)S(1)}, f32[128]{0:T(128)}, u32[]{:S(2)}) copy-start(f32[128]{0:T(128)} %get-tuple-element.197) | copy-start | bytes 1540
  28.8 4.2 %copy-start.143 = (f32[128]{0:T(128)S(1)}, f32[128]{0:T(128)}, u32[]{:S(2)}) copy-start(f32[128]{0:T(128)} %get-tuple-element.198) | copy-start | bytes 1540
  28.8 4.2 %copy-start.144 = (f32[128]{0:T(128)S(1)}, f32[128]{0:T(128)}, u32[]{:S(2)}) copy-start(f32[128]{0:T(128)} %get-tuple-element.199) | copy-start | bytes 1540
  28.8 4.2 %copy-start.145 = (f32[128]{0:T(128)S(1)}, f32[128]{0:T(128)}, u32[]{:S(2)}) copy-start(f32[128]{0:T(128)} %get-tuple-element.200) | copy-start | bytes 1540
  28.8 4.2 %copy-start.146 = (f32[128]{0:T(128)S(1)}, f32[128]{0:T(128)}, u32[]{:S(2)}) copy-start(f32[128]{0:T(128)} %get-tuple-element.201) | copy-start | bytes 1540
  28.8 4.2 %copy-start.147 = (f32[128]{0:T(128)S(1)}, f32[128]{0:T(128)}, u32[]{:S(2)}) copy-start(f32[128]{0:T(128)} %get-tuple-element.202) | copy-start | bytes 1540
  28.8 4.2 %copy-start.148 = (f32[128]{0:T(128)S(1)}, f32[128]{0:T(128)}, u32[]{:S(2)}) copy-start(f32[128]{0:T(128)} %get-tuple-element.203) | copy-start | bytes 1540
  28.9 4.2 %copy-start.149 = (f32[128]{0:T(128)S(1)}, f32[128]{0:T(128)}, u32[]{:S(2)}) copy-start(f32[128]{0:T(128)} %get-tuple-element.204) | copy-start | bytes 1540
  30.9 6.2 %copy-start.88 = (f32[4,3,128]{2,1,0:T(4,128)}, f32[4,3,128]{2,1,0:T(4,128)S(1)}, u32[]{:S(2)}) copy-start(f32[4,3,128]{2,1,0:T(4,128)S(1)} %get-tuple-element.155) | copy-start | bytes 18436
  30.9 6.2 %copy-start.90 = (f32[4,3,128]{2,1,0:T(4,128)}, f32[4,3,128]{2,1,0:T(4,128)S(1)}, u32[]{:S(2)}) copy-start(f32[4,3,128]{2,1,0:T(4,128)S(1)} %get-tuple-element.156) | copy-start | bytes 18436
  33.2 4.3 %copy-start.98 = (f32[128]{0:T(128)S(1)}, f32[128]{0:T(128)}, u32[]{:S(2)}) copy-start(f32[128]{0:T(128)} %param.12) | copy-start | bytes 1540
  40.8 7.8 %copy-start.74 = (bf16[512,512]{1,0:T(8,128)(2,1)}, bf16[512,512]{1,0:T(8,128)(2,1)S(1)}, u32[]{:S(2)}) copy-start(bf16[512,512]{1,0:T(8,128)(2,1)S(1)} %get-tuple-element.217) | copy-start | bytes 1572868
  40.8 7.7 %copy-start.85 = (f32[69,4,128]{2,1,0:T(4,128)S(1)}, f32[69,4,128]{2,1,0:T(4,128)}, u32[]{:S(2)}) copy-start(f32[69,4,128]{2,1,0:T(4,128)} %param.10) | copy-start | bytes 423940
  41.9 13.7 %all-to-all-start.1 = ((bf16[16,8,512]{2,1,0:T(8,128)(2,1)}), bf16[16,8,512]{2,1,0:T(8,128)(2,1)S(1)}, u32[]{:S(2)}, u32[]{:S(2)}) async-start(bf16[16,8,512]{2,1,0:T(8,128)(2,1)} %fusion.5), calls=%async_computation.1 | async-start | bytes 262144 | tf_op jit(solution)/shard_map/all_to_all | solution.py:39
  58.4 13.7 %all-to-all-start.2 = ((bf16[16,16,512]{2,1,0:T(8,128)(2,1)}), bf16[16,16,512]{2,1,0:T(8,128)(2,1)}, u32[]{:S(2)}, u32[]{:S(2)}) async-start(bf16[16,16,512]{2,1,0:T(8,128)(2,1)} %pad_maximum_fusion.44), calls=%async_computation.2 | async-start | bytes 524288 | tf_op jit(solution)/shard_map/all_to_all | solution.py:39
  63.5 10.5 %copy-start.81 = (bf16[32,16,128]{2,1,0:T(8,128)(2,1)S(1)}, bf16[32,16,128]{2,1,0:T(8,128)(2,1)}, u32[]{:S(2)}) copy-start(bf16[32,16,128]{2,1,0:T(8,128)(2,1)} %copy-done.80) | copy-start | bytes 393220
  94.3 3.6 %collective-permute-start.2 = (f32[32,24,128]{2,1,0:T(8,128)S(1)}, f32[32,24,128]{2,1,0:T(8,128)S(1)}, u32[]{:S(2)}, u32[]{:S(2)}) collective-permute-start(f32[32,24,128]{2,1,0:T(8,128)S(1)} %pad_maximum_fusion), channel_id=1, source_target_pairs={{0,1},{1,0},{2,3},{3,2},{4,5},{5,4},{6,7},{7,6},{8,9},{9,8},{10,11... | collective-permute-start | bytes 1179656 | tf_op jit(solution)/shard_map/ppermute | solution.py:19
  121.0 15.1 %all-to-all-start.4 = ((f32[8,10,128]{2,1,0:T(8,128)}), f32[8,10,128]{2,1,0:T(8,128)S(1)}, u32[]{:S(2)}, u32[]{:S(2)}) async-start(f32[8,10,128]{2,1,0:T(8,128)} %pad_maximum_fusion.45), calls=%async_computation.4 | async-start | bytes 131072 | tf_op jit(solution)/shard_map/all_to_all | solution.py:39
  136.8 12.0 %all-to-all-start.5 = ((f32[16,10,128]{2,1,0:T(8,128)}), f32[16,10,128]{2,1,0:T(8,128)S(1)}, u32[]{:S(2)}, u32[]{:S(2)}) async-start(f32[16,10,128]{2,1,0:T(8,128)} %broadcast_in_dim.65), calls=%async_computation.5 | async-start | bytes 262144 | tf_op jit(solution)/shard_map/all_to_all | solution.py:39
  (107 other events, 222.8 us)

commit v3 on v2

v3 whole, which is shorter than its diff:
```python
import math

import jax
import jax.numpy as jnp
from jax import lax
from jax.experimental import pallas as pl
from jax.experimental.pallas import tpu as pltpu
from jax.sharding import PartitionSpec as P

STENCIL_SIDE = 7
SQRT_TWO_PI = 0.7978845608028654
CUBIC = 0.044715
EPSILON = 1e-06
SMOOTHING = 0.01
PER_CHUNK = 5
CHUNK_ROWS = 8
EDGE = 8
STRIP = 16
TAPS_AT = 69
DEPTH_Z = 8
F32, BF16 = jnp.float32, jnp.bfloat16


def core_swap(value):
    count = lax.axis_size("lat")
    return lax.ppermute(value, "lat", [(i, i ^ 1) for i in range(count)])


def odd_swap(value):
    count = lax.axis_size("lat")
    pairs = [(i, i + 1) for i in range(1, count - 1, 2)]
    return lax.ppermute(value, "lat", pairs + [(b, a) for a, b in pairs])


def halo_rows(field, half):
    even = lax.rem(lax.axis_index("lat"), 2) == 0
    head, tail = field[:half], field[field.shape[0] - half :]
    return core_swap(jnp.where(even, tail, head)), odd_swap(jnp.where(even, head, tail))


def exchange(value, axis, groups=None):
    return lax.all_to_all(value, axis, 0, 0, tiled=True, axis_index_groups=groups)


AXES = ("ens", "lat")


def weight_groups(members, bands):
    def at(e, band):
        e = e if band < bands // 2 else e // 4 * 4 + (e + 2) % 4
        return e * bands + band

    return [[at(e, band) for band in range(bands)] for e in range(members)]


def plane_groups(members, bands):
    half = bands // 2
    return [
        [e * bands + h * half + rest for e in range(members) for h in range(2)]
        for rest in range(half)
    ]


def gelu_parts(u):
    inner = jnp.tanh(SQRT_TWO_PI * (u + CUBIC * u * u * u))
    value = 0.5 * u * (1.0 + inner)
    slope = 0.5 * (1.0 + inner) + 0.5 * u * (1.0 - inner * inner) * SQRT_TWO_PI * (
        1.0 + 3.0 * CUBIC * u * u
    )
    return value, slope


def vmem_call(body, outs, scratch=(), scalars=0, vectors=0):
    vmem = pl.BlockSpec(memory_space=pltpu.VMEM)
    smem = pl.BlockSpec(memory_space=pltpu.SMEM)
    return pl.pallas_call(
        body,
        out_shape=[jax.ShapeDtypeStruct(shape, dtype) for shape, dtype in outs],
        in_specs=[smem] * scalars + [vmem] * vectors,
        out_specs=[vmem] * len(outs),
        scratch_shapes=list(scratch),
    )


def dot(a, b, contract):
    return lax.dot_general(a, b, ((contract[:1], contract[1:]), ((), ())), preferred_element_type=F32)


def stencil_body(place, field, partner, other, taps, gain, ext, scaled, inverse, normed):
    even = place[0] == 0
    rows, zonal, _ = field.shape
    half = STENCIL_SIDE // 2
    for r in range(rows + 2 * half):
        if r < half:
            row = jnp.where(even, other[r].astype(F32), partner[r].astype(F32))
        elif r < rows + half:
            row = field[r - half].astype(F32)
        else:
            k = r - rows - half
            row = jnp.where(even, partner[k].astype(F32), other[k].astype(F32))
        ext[r, EDGE : EDGE + zonal, :] = row
        ext[r, EDGE - half : EDGE, :] = row[zonal - half :]
        ext[r, EDGE + zonal : EDGE + zonal + half, :] = row[:half]
    for start in range(0, zonal, STRIP):
        total = jnp.zeros((rows, STRIP, field.shape[2]), F32)
        for b in range(STENCIL_SIDE):
            first = EDGE - half + b + start
            slab = ext[:, first : first + STRIP, :]
            for a in range(STENCIL_SIDE):
                k = a * STENCIL_SIDE + b
                total = total + taps[k : k + 1, :][None] * slab[a : a + rows]
        centred = total - jnp.mean(total, axis=-1, keepdims=True)
        recip = lax.rsqrt(jnp.mean(centred * centred, axis=-1, keepdims=True) + EPSILON)
        value = centred * recip
        rounded = (gain[...][None] * value).astype(BF16)
        wide = jnp.broadcast_to(recip, value.shape)
        for i in range(rows):
            at = pl.ds(i * zonal + start, STRIP)
            scaled[at, :] = value[i]
            inverse[at, :] = wide[i]
            normed[at, :] = rounded[i]


def selector(rows, columns, chunk_bits, offsets, turned):
    place = lax.broadcasted_iota(jnp.int32, (rows, columns), 1 if turned else 0)
    variable = lax.broadcasted_iota(jnp.int32, (rows, columns), 0 if turned else 1)
    chunk = lax.shift_right_logical(place, chunk_bits)
    inside = place & ((1 << chunk_bits) - 1)
    result = jnp.zeros((rows, columns), F32)
    for offset in offsets:
        j = inside - offset
        hit = (j >= 0) & (j < PER_CHUNK) & (chunk * PER_CHUNK + j == variable)
        result = jnp.where(hit, 1.0, result)
    return result.astype(BF16)


def mlp_body(normed, both, field, readout, gated, slope, residual, chunks, upper):
    owned = both.shape[1] // 2
    hidden, channels = both.shape[0] * owned, both.shape[2]
    points = normed.shape[0]
    widen = both[:, :owned, :].reshape(hidden, channels)
    shrink = both[:, owned:, :].reshape(hidden, channels)
    upper[...] = dot(normed[...], widen, (1, 1))

    def step(i, carry):
        at = pl.ds(pl.multiple_of(i * 16, 16), 16)
        value, tilt = gelu_parts(upper[at, :])
        gated[at, :] = value.astype(BF16)
        slope[at, :] = tilt
        return carry

    lax.fori_loop(0, points // 16, step, 0, unroll=2)
    mixed = dot(gated[...], shrink, (1, 0))
    residual[...] = (field[...].reshape(points, channels).astype(F32) + mixed).astype(BF16)
    members = chunks.shape[0]
    spread = dot(selector(members * CHUNK_ROWS, readout.shape[0], 3, (0,), False), readout[...], (1, 0))
    outlook = dot(spread.astype(BF16), residual[...], (1, 1))
    for e in range(members):
        chunks[e] = outlook[e * CHUNK_ROWS : (e + 1) * CHUNK_ROWS].astype(BF16)


def outlook_body(readout, residual, out):
    out[...] = dot(readout[...], residual[...], (1, 1)).astype(BF16)


def pair_body(place, everyone, truth, weight, payload, loss, rows, seen):
    member = place[1]
    members, _, points = everyone.shape
    variables, bands, lanes = truth.shape
    for j in range(PER_CHUNK):
        row = truth[jnp.minimum(member * PER_CHUNK + j, variables - 1)]
        for q in range(bands):
            seen[j : j + 1, q * lanes : (q + 1) * lanes] = row[q : q + 1]
    seen[PER_CHUNK:, :] = jnp.zeros((CHUNK_ROWS - PER_CHUNK, points), F32)
    limit = jnp.minimum(PER_CHUNK, variables - member * PER_CHUNK)
    real = lax.broadcasted_iota(jnp.int32, (CHUNK_ROWS, lanes), 0) < limit
    pair_norm = 1.0 / (members * (members - 1))
    lost = jnp.zeros((CHUNK_ROWS, lanes), F32)
    for q in range(points // lanes):
        at = slice(q * lanes, (q + 1) * lanes)
        y = [everyone[m, :, at].astype(F32) for m in range(members)]
        spread = [jnp.full((CHUNK_ROWS, lanes), SMOOTHING**0.5, F32) for _ in range(members)]
        ranks = [jnp.zeros((CHUNK_ROWS, lanes), F32) for _ in range(members)]
        for m in range(members):
            for k in range(m):
                gap = y[m] - y[k]
                square = gap * gap + SMOOTHING
                root = lax.rsqrt(square)
                size, tilt = square * root, gap * root
                spread[m], spread[k] = spread[m] + size, spread[k] + size
                ranks[m], ranks[k] = ranks[m] + tilt, ranks[k] - tilt
        scale = weight[0:1, at]
        for m in range(members):
            miss = y[m] - seen[:, at]
            square = miss * miss + SMOOTHING
            root = lax.rsqrt(square)
            term = scale * (square * root * (1.0 / members) - 0.5 * pair_norm * spread[m])
            lost = lost + jnp.where(real, term, 0.0)
            flow = scale * (miss * root * (1.0 / members) - pair_norm * ranks[m])
            average = spread[m] * (1.0 / (members - 1))
            high = average.astype(BF16).astype(F32)
            rows[m, 0:CHUNK_ROWS, at] = jnp.where(real, flow, 0.0)
            rows[m, PER_CHUNK : PER_CHUNK + CHUNK_ROWS, at] = high
            rows[m, 2 * PER_CHUNK : 16, at] = (average - high)[: 16 - 2 * PER_CHUNK]
    for m in range(members):
        payload[m] = rows[m].astype(BF16)
    loss[...] = jnp.sum(lost, axis=0, keepdims=True)


def average_body(back, out):
    members, height, points = back.shape
    pick = selector(out.shape[0], members * height, 4, (PER_CHUNK, 2 * PER_CHUNK), True)
    out[...] = dot(pick, back[...].reshape(members * height, points), (1, 0))


def backward_body(
    back, readout, residual, gated, slope, normed, scaled, inverse, gain, both,
    widen_grad, shrink_grad, readout_grad, gain_grad, back_depth, gate, back_upper,
):
    members, height, points = back.shape
    owned = both.shape[1] // 2
    hidden, channels = both.shape[0] * owned, both.shape[2]
    widen = both[:, :owned, :].reshape(hidden, channels)
    shrink = both[:, owned:, :].reshape(hidden, channels)
    flow = back[...].reshape(members * height, points)
    spread = dot(selector(members * height, readout.shape[0], 4, (0,), False), readout[...], (1, 0))
    back_residual = dot(flow, spread.astype(BF16), (0, 0)).astype(BF16)
    gate[...] = dot(back_residual, shrink, (1, 1))
    readout_grad[...] = dot(flow, residual[...], (1, 0))
    shrink_grad[...] = dot(gated[...], back_residual, (0, 0))

    def step(i, carry):
        at = pl.ds(pl.multiple_of(i * 16, 16), 16)
        back_upper[at, :] = (gate[at, :] * slope[at, :]).astype(BF16)
        return carry

    lax.fori_loop(0, points // 16, step, 0, unroll=2)
    back_norm = dot(back_upper[...], widen, (1, 0))
    widen_grad[...] = dot(back_upper[...], normed[...], (0, 0))
    value = scaled[...]
    product = back_norm * value
    gain_grad[...] = jnp.sum(product, axis=0, keepdims=True)
    g = back_norm * gain[...]
    p = jnp.mean(g, axis=-1, keepdims=True)
    q = jnp.mean(g * value, axis=-1, keepdims=True)
    back_depth[...] = inverse[...] * (g - p - value * q)


def pack_body(place, back_depth, ext, widen_grad, shrink_grad, readout_grad, gain_grad, loss, send, keep, small):
    first_core = place[0] == 0
    half = STENCIL_SIDE // 2
    zonal = ext.shape[1] - 2 * EDGE
    rows = back_depth.shape[0] // zonal
    channels = ext.shape[2]
    members = small.shape[0] // CHUNK_ROWS
    height = readout_grad.shape[0] // members
    small[TAPS_AT + 48 :, :] = jnp.zeros((small.shape[0] - TAPS_AT - 48, channels), F32)
    for e in range(members):
        count = min(PER_CHUNK, TAPS_AT - e * PER_CHUNK)
        if count > 0:
            small[e * PER_CHUNK : e * PER_CHUNK + count, :] = readout_grad[e * height : e * height + count, :]
    for b in range(STENCIL_SIDE):
        totals = [jnp.zeros((STRIP, channels), F32) for _ in range(STENCIL_SIDE)]
        for start in range(0, zonal, STRIP):
            first = EDGE - half + b + start
            slab = ext[:, first : first + STRIP, :]
            up = [back_depth[i * zonal + start : i * zonal + start + STRIP, :] for i in range(rows)]
            for a in range(STENCIL_SIDE):
                for i in range(rows):
                    totals[a] = totals[a] + up[i] * slab[i + a]
        for a in range(STENCIL_SIDE):
            k = TAPS_AT + a * STENCIL_SIDE + b
            small[k : k + 1, :] = jnp.sum(totals[a], axis=0, keepdims=True)
    small[TAPS_AT + 49 : TAPS_AT + 50, :] = gain_grad[...]
    small[TAPS_AT + 50 : TAPS_AT + 51, :] = loss[...]
    depth_z = DEPTH_Z
    for e in range(members):
        tail = small[e * CHUNK_ROWS : (e + 1) * CHUNK_ROWS, :]
        for h in range(2):
            d = 2 * e + h
            for mat, grad in enumerate((widen_grad, shrink_grad)):
                base = h * depth_z * 2 * members + e
                even = grad[pl.ds(base, depth_z, stride=2 * members), :]
                odd = grad[pl.ds(base + members, depth_z, stride=2 * members), :]
                keep[d, mat * depth_z : (mat + 1) * depth_z, :] = jnp.where(first_core, even, odd)
                send[d, mat * depth_z : (mat + 1) * depth_z, :] = jnp.where(first_core, odd, even)
            keep[d, 2 * depth_z :, :] = tail
            send[d, 2 * depth_z :, :] = tail


def plane_body(arrived, out):
    total = jnp.sum(arrived[...], axis=0)
    depth_z = out.shape[0]
    for z in range(depth_z):
        out[z, 0:CHUNK_ROWS, :] = total[2 * depth_z :]
        out[z, CHUNK_ROWS : CHUNK_ROWS + 1, :] = total[z : z + 1]
        out[z, CHUNK_ROWS + 1 : CHUNK_ROWS + 2, :] = total[depth_z + z : depth_z + z + 1]


def column_body(arrived, out):
    out[...] = jnp.broadcast_to(jnp.sum(arrived[...], axis=0)[None], out.shape)


def final_body(arrived, up, down, taps, gain, readout, loss, small):
    members = arrived.shape[0]
    for e in range(members):
        small[e * CHUNK_ROWS : (e + 1) * CHUNK_ROWS, :] = arrived[e, 0:CHUNK_ROWS, :]
        up[e : e + 1, :] = arrived[e, CHUNK_ROWS : CHUNK_ROWS + 1, :]
        down[e : e + 1, :] = arrived[e, CHUNK_ROWS + 1 : CHUNK_ROWS + 2, :]
    readout[...] = small[0:TAPS_AT, :]
    taps[...] = small[TAPS_AT : TAPS_AT + 49, :]
    gain[...] = small[TAPS_AT + 49 : TAPS_AT + 50, :]
    loss[...] = jnp.sum(small[TAPS_AT + 50 : TAPS_AT + 51, :], axis=1, keepdims=True)


def on_device(
    features,
    random_perturbation,
    observed_truth,
    stencil_taps,
    affine_factor,
    widen_matrix,
    shrink_matrix,
    readout_matrix,
):
    rows, zonal, channels = features.shape
    variables = readout_matrix.shape[0]
    half = STENCIL_SIDE // 2
    bands, members = lax.axis_size("lat"), lax.axis_size("ens")
    band, member = lax.axis_index("lat"), lax.axis_index("ens")
    points = rows * zonal
    latitudes = rows * bands
    hidden = widen_matrix.shape[0] * bands
    depth_z = DEPTH_Z
    share = CHUNK_ROWS
    place = jnp.stack([lax.rem(band, 2), member]).astype(jnp.int32)
    gain = affine_factor.reshape(1, channels)

    pair = jnp.concatenate([widen_matrix, shrink_matrix], axis=0)
    both = exchange(
        jnp.broadcast_to(pair[None], (bands,) + pair.shape), AXES, weight_groups(members, bands)
    )
    field = (features.astype(F32) + random_perturbation[0].astype(F32)).astype(BF16)
    partner, other = halo_rows(field, half)
    latitude = (band * rows + jnp.arange(points, dtype=jnp.int32) // zonal).astype(F32)
    area = jnp.cos(math.pi * ((latitude + 0.5) / latitudes - 0.5))
    weight = (area * (1.0 / (latitudes * zonal)))[None, :]

    wide = (rows + 2 * half, zonal + 2 * EDGE, channels)
    ext, scaled, inverse, normed = vmem_call(
        stencil_body,
        [(wide, F32), ((points, channels), F32), ((points, channels), F32), ((points, channels), BF16)],
        scalars=1,
        vectors=5,
    )(place, field, partner, other, stencil_taps, gain)
    gated, slope, residual, chunks = vmem_call(
        mlp_body,
        [
            ((points, hidden), BF16),
            ((points, hidden), F32),
            ((points, channels), BF16),
            ((members, CHUNK_ROWS, points), BF16),
        ],
        [pltpu.VMEM((points, hidden), F32)],
        vectors=4,
    )(normed, both, field, readout_matrix)
    everyone = exchange(chunks, "ens")
    (outlook,) = vmem_call(outlook_body, [((variables, points), BF16)], vectors=2)(
        readout_matrix, residual
    )
    sample_outlook = outlook.reshape(1, variables, rows, zonal)
    payload, loss = vmem_call(
        pair_body,
        [((members, 16, points), BF16), ((1, zonal), F32)],
        [pltpu.VMEM((members, 16, points), F32), pltpu.VMEM((CHUNK_ROWS, points), F32)],
        scalars=1,
        vectors=3,
    )(place, everyone, observed_truth, weight)
    back = exchange(payload, "ens")
    (average,) = vmem_call(average_body, [((variables, points), F32)], vectors=1)(back)
    sample_average_spread = average.reshape(1, variables, rows, zonal)

    widen_grad, shrink_grad, readout_grad, gain_grad, back_depth = vmem_call(
        backward_body,
        [
            ((hidden, channels), F32),
            ((hidden, channels), F32),
            ((members * 16, channels), F32),
            ((1, channels), F32),
            ((points, channels), F32),
        ],
        [pltpu.VMEM((points, hidden), F32), pltpu.VMEM((points, hidden), BF16)],
        vectors=10,
    )(back, readout_matrix, residual, gated, slope, normed, scaled, inverse, gain, both)
    packet = ((2 * members, 2 * depth_z + share, channels), F32)
    send, keep = vmem_call(
        pack_body,
        [packet, packet],
        [pltpu.VMEM((members * share, channels), F32)],
        scalars=1,
        vectors=7,
    )(place, back_depth, ext, widen_grad, shrink_grad, readout_grad, gain_grad, loss)

    arrived = exchange(keep + core_swap(send), AXES, plane_groups(members, bands))
    columns = [
        list(range(h * bands // 2 + c, (h + 1) * bands // 2, 2)) for h in range(2) for c in range(2)
    ]
    (outgoing,) = vmem_call(plane_body, [((depth_z, share + 2, channels), F32)], vectors=1)(arrived)
    arrived = exchange(outgoing, "lat", columns)
    (outgoing,) = vmem_call(column_body, [((members, share + 2, channels), F32)], vectors=1)(arrived)
    arrived = exchange(outgoing, "ens")
    up, down, taps, gain_total, readout, loss = vmem_call(
        final_body,
        [
            ((members, channels), F32),
            ((members, channels), F32),
            ((STENCIL_SIDE * STENCIL_SIDE, channels), F32),
            ((1, channels), F32),
            ((variables, channels), F32),
            ((1, 1), F32),
        ],
        [pltpu.VMEM((members * share, channels), F32)],
        vectors=1,
    )(arrived)
    return (
        loss.reshape(()),
        taps,
        gain_total.reshape(channels),
        up,
        down,
        readout,
        sample_outlook,
        sample_average_spread,
    )


def solution(mesh):
    in_specs = (
        P("lat", None, None),
        P("ens", "lat", None, None),
        P(None, "lat", None),
        P(),
        P(),
        P("lat", None),
        P("lat", None),
        P(),
    )
    out_specs = (
        P(),
        P(),
        P(),
        P("lat", None),
        P("lat", None),
        P(),
        P("ens", None, "lat", None),
        P("ens", None, "lat", None),
    )
    return jax.shard_map(
        on_device, mesh=mesh, in_specs=in_specs, out_specs=out_specs, check_vma=False
    )
```

time: 153 us -> 136 us (0.89)
  blocking collectives: 22.3 us -> 51.8 us
  Pallas kernels: 0 us -> 25 us
  other arithmetic: 26 us -> 3.05 us
  starting transfers between devices: 44.7 us -> 30.3 us
  waiting for transfers between devices: 28.6 us -> 16.5 us
  local copies, waits for them, and re-layouts: 19.1 us -> 7.23 us
  matrix products: 7.7 us -> 0 us
  between operations: 3.28 us -> 0.75 us
    all_to_all x1 -> x3, blocking collectives: 22.3 us -> 51.8 us  [exchange(): lax.all_to_all(value, axis, 0, 0, tiled=True, axis_index_groups=groups)]
    pallas_call x0 -> x10, Pallas kernels: none -> 25 us  [the longest x1 4.09 us: on_device(): vmem_call(backward_body, [((hidden, channels), F32), ((hidden, channels),...]
    reduce_sum x12 -> x0, other arithmetic: 16.2 us -> none  [the longest x6 10.2 us: kernel_grad(): taps.append(jnp.sum((upstream * shifted).reshape(-1, channels), axis=0))]
    all_to_all x5 -> x3, waiting for transfers between devices: 26.9 us -> 14.6 us  [exchange(): lax.all_to_all(value, axis, 0, 0, tiled=True, axis_index_groups=groups)]
    all_to_all x5 -> x3, starting transfers between devices: 36.5 us -> 25.6 us  [exchange(): lax.all_to_all(value, axis, 0, 0, tiled=True, axis_index_groups=groups)]
    dot_general x9 -> x0, matrix products: 7.7 us -> none  [the longest x1 1.66 us: on_device(): lax.dot_general(back_residual, shrink, (((1,), (1,)), ((), ())), preferre...]
    slice x15 -> x0, local copies, waits for them, and re-layouts: 6.87 us -> none  [the longest x4 1.59 us: depthwise(): jnp.roll(band, half - b, axis=1)]
    slice x8 -> x0, other arithmetic: 5.49 us -> none  [depthwise(): jnp.roll(band, half - b, axis=1)]
  transfers between devices with their start and end apart: 8 -> 6, of which waited for: 6 -> 4; matrix products, arithmetic and copies ran while one was open for 13% -> 3% of each run, Pallas kernels for 0% -> 5%
where the time goes in v3:
time: 136 us; the launch traced here: 135 us
  blocking collectives  51.8 us (38%)
  starting transfers between devices  30.3 us (22%)
  Pallas kernels  25 us (18%)
  waiting for transfers between devices  16.5 us (12%)
  local copies, waits for them, and re-layouts  7.23 us (5%)
  other arithmetic  3.05 us (2%)
    all_to_all x3, blocking collectives, exchange(): lax.all_to_all(value, axis, 0, 0, tiled=True, axis_index_groups=groups)  51.8 us
    all_to_all x3, starting transfers between devices, exchange(): lax.all_to_all(value, axis, 0, 0, tiled=True, axis_index_groups=groups)  25.6 us
    all_to_all x3, waiting for transfers between devices, exchange(): lax.all_to_all(value, axis, 0, 0, tiled=True, axis_index_groups=groups)  14.6 us
    pallas_call x1, Pallas kernels, on_device(): vmem_call(backward_body, [((hidden, channels), F32), ((hidden, channels),...  4.09 us
    ppermute x2, starting transfers between devices, core_swap(): return lax.ppermute(value, 'lat', [(i, i ^ 1) for i in range(count)])  4.08 us
    pallas_call x1, Pallas kernels, on_device(): vmem_call(mlp_body, [((points, hidden), BF16), ((points, hidden), F32), (...  3.45 us
    pallas_call x1, Pallas kernels, on_device(): vmem_call(pack_body, [packet, packet], [pltpu.VMEM((members * share, chan...  3.44 us
    unnamed x16, local copies, waits for them, and re-layouts  3.31 us
  transfers between devices with their start and end apart: 6, of which 4 were waited for; matrix products, arithmetic and copies ran while one was open for 3% of the time, Pallas kernels for 5%

profile of v3, /device:TPU:8, one launch (start us, length us, event | category | flops | bytes accessed | tf_op | source)
XLA Modules:
  0.0 134.6 jit_solution(12045690581692206224)
XLA Ops:
  0.6 0.7 pad_maximum_fusion
  1.3 0.7 broadcast_in_dim.2
  2.1 0.0 copy-start.4
  2.1 0.0 copy-start.5
  2.1 13.6 %all-to-all-start = ((bf16[32,32,128]{2,1,0:T(8,128)(2,1)}), bf16[32,32,128]{2,1,0:T(8,128)(2,1)S(1)}, u32[]{:S(2)}, u32[]{:S(2)}) async-start(bf16[32,32,128]{2,1,0:T(8,128)(2,1)} %broadcast_in_dim.2), calls=%async_computation | async-start | bytes 524288 | tf_op jit(solution)/shard_map/all_to_all | solution.py:42
  15.7 0.0 copy-done.4
  15.7 0.0 copy-done.5
  15.8 0.0 copy-start
  15.8 0.6 copy-done
  16.5 2.2 %collective-permute-start = (bf16[3,128,128]{2,1,0:T(8,128)(2,1)S(1)}, bf16[3,128,128]{2,1,0:T(8,128)(2,1)S(1)}, u32[]{:S(2)}, u32[]{:S(2)}) collective-permute-start(bf16[3,128,128]{2,1,0:T(8,128)(2,1)S(1)} %get-tuple-element.55), channel_id=1, source_target_pairs={{0,1},{1,0},{2,3},{3,2},{4,5},{5,4},{6,7},{7,6},{8,9},{9,8},{10,11... | collective-permute-start | bytes 294920 | tf_op jit(solution)/shard_map/ppermute | solution.py:26
  18.6 0.7 collective-permute-start.1
  19.3 0.6 pad_add_fusion.place
  19.9 0.0 collective-permute-done.partner
  19.9 0.0 copy-start.6
  19.9 0.0 collective-permute-done.1.other
  19.9 0.0 copy-start.7
  19.9 0.6 copy-done.6
  20.5 0.1 copy-done.7
  20.6 3.2 %shard_map.143 = (f32[10,144,128]{2,1,0:T(8,128)}, f32[512,128]{1,0:T(8,128)}, f32[512,128]{1,0:T(8,128)}, bf16[512,128]{1,0:T(8,128)(2,1)}) custom-call(s32[2]{0:T(128)} %pad_add_fusion.place, bf16[4,128,128]{2,1,0:T(8,128)(2,1)} %copy-done, bf16[3,128,128]{2,1,0:T(8,128)(2,1)} %copy-done.6, bf16[3,128,128]{2,1,0:T(8,128)(2,1)} %copy-done.7, ...), custom_call_target="tpu_custom_call" | custom-call | tf_op jit(solution)/shard_map/pallas_call | solution.py:350
  23.8 7.4 %all-to-all-done.both = bf16[32,32,128]{2,1,0:T(8,128)(2,1)S(1)} async-done(((bf16[32,32,128]{2,1,0:T(8,128)(2,1)}), bf16[32,32,128]{2,1,0:T(8,128)(2,1)S(1)}, u32[]{:S(2)}, u32[]{:S(2)}) %all-to-all-start) | async-done | bytes 262176 | tf_op jit(solution)/shard_map/all_to_all | solution.py:42
  31.2 0.0 copy-start.1
  31.2 0.7 copy-done.1
  31.9 3.4 %shard_map.144 = (bf16[512,512]{1,0:T(8,128)(2,1)}, f32[512,512]{1,0:T(8,128)}, bf16[512,128]{1,0:T(8,128)(2,1)}, bf16[16,8,512]{2,1,0:T(8,128)(2,1)}) custom-call(bf16[512,128]{1,0:T(8,128)(2,1)} %get-tuple-element.31.normed, bf16[32,32,128]{2,1,0:T(8,128)(2,1)} %copy-done.1, bf16[4,128,128]{2,1,0:T(8,128)(2,1)} %copy-done, bf16[69,128]{1,0:T(8,128)(2,1)} %readout.5), custom_call_target="tpu_custom_call" | custom-call | tf_op jit(solution)/shard_map/pallas_call | solution.py:356
  35.3 7.2 %all-to-all-start.1 = ((bf16[16,8,512]{2,1,0:T(8,128)(2,1)}), bf16[16,8,512]{2,1,0:T(8,128)(2,1)S(1)}, u32[]{:S(2)}, u32[]{:S(2)}) async-start(bf16[16,8,512]{2,1,0:T(8,128)(2,1)} %get-tuple-element.32), calls=%async_computation.1 | async-start | bytes 262144 | tf_op jit(solution)/shard_map/all_to_all | solution.py:42
  42.5 0.7 fusion.8.weight
  43.2 6.6 %all-to-all-done.1.everyone = bf16[16,8,512]{2,1,0:T(8,128)(2,1)S(1)} async-done(((bf16[16,8,512]{2,1,0:T(8,128)(2,1)}), bf16[16,8,512]{2,1,0:T(8,128)(2,1)S(1)}, u32[]{:S(2)}, u32[]{:S(2)}) %all-to-all-start.1) | async-done | bytes 131104 | tf_op jit(solution)/shard_map/all_to_all | solution.py:42
  49.8 0.0 copy-start.3
  49.8 0.7 copy-done.3
  50.5 2.6 %shard_map.145 = (bf16[16,16,512]{2,1,0:T(8,128)(2,1)}, f32[1,128]{1,0:T(1,128)}) custom-call(s32[2]{0:T(128)} %pad_add_fusion.place, bf16[16,8,512]{2,1,0:T(8,128)(2,1)} %copy-done.3, f32[69,4,128]{2,1,0:T(4,128)} %truth.1, f32[1,512]{1,0:T(1,128)} %fusion.8.weight), custom_call_target="tpu_custom_call" | custom-call | tf_op jit(solution)/shard_map/pallas_call | solution.py:372
  53.1 13.6 %all_to_all.30.back = bf16[16,16,512]{2,1,0:T(8,128)(2,1)} all-to-all(bf16[16,16,512]{2,1,0:T(8,128)(2,1)} %get-tuple-element.33), channel_id=1, replica_groups=mesh['ens'=16,'lat'=32] {'ens'}, dimensions={0} | all-to-all | bytes 524288 | tf_op jit(solution)/shard_map/all_to_all | solution.py:42
  66.7 4.1 %shard_map.146 = (f32[512,128]{1,0:T(8,128)}, f32[512,128]{1,0:T(8,128)}, f32[256,128]{1,0:T(8,128)}, f32[1,128]{1,0:T(1,128)}, f32[512,128]{1,0:T(8,128)}) custom-call(bf16[16,16,512]{2,1,0:T(8,128)(2,1)} %all_to_all.30.back, bf16[69,128]{1,0:T(8,128)(2,1)} %readout.5, bf16[512,128]{1,0:T(8,128)(2,1)} %get-tuple-element.34.residual, ...), custom_call_target="tpu_custom_call" | custom-call | tf_op jit(solution)/shard_map/pallas_call | solution.py:383
  70.8 3.4 %shard_map.147 = (f32[32,24,128]{2,1,0:T(8,128)}, f32[32,24,128]{2,1,0:T(8,128)}) custom-call(s32[2]{0:T(128)} %pad_add_fusion.place, f32[512,128]{1,0:T(8,128)} %get-tuple-element.39.back_depth, f32[10,144,128]{2,1,0:T(8,128)} %get-tuple-element.40.ext, f32[512,128]{1,0:T(8,128)} %get-tuple-element.41.widen_grad, f32[512,128]{1,0:T(8,128)} %get-tuple-element.42.shrink_grad, ...), custom_call_target="tpu_custom_call" | custom-call | tf_op jit(solution)/shard_map/pallas_call | solution.py:396
  74.2 1.9 %collective-permute-start.2 = (f32[32,24,128]{2,1,0:T(8,128)}, f32[32,24,128]{2,1,0:T(8,128)S(1)}, u32[]{:S(2)}, u32[]{:S(2)}) collective-permute-start(f32[32,24,128]{2,1,0:T(8,128)} %get-tuple-element.47), channel_id=1, source_target_pairs={{0,1},{1,0},{2,3},{3,2},{4,5},{5,4},{6,7},{7,6},{8,9},{9,8},{10,11... | collective-permute-start | bytes 1179656 | tf_op jit(solution)/shard_map/ppermute | solution.py:26
  76.2 1.9 %collective-permute-done.2 = f32[32,24,128]{2,1,0:T(8,128)S(1)} collective-permute-done((f32[32,24,128]{2,1,0:T(8,128)}, f32[32,24,128]{2,1,0:T(8,128)S(1)}, u32[]{:S(2)}, u32[]{:S(2)}) %collective-permute-start.2) | collective-permute-done | bytes 393248 | tf_op jit(solution)/shard_map/ppermute | solution.py:26
  78.1 1.0 add.49
  79.1 25.8 %all_to_all.31.arrived = f32[32,24,128]{2,1,0:T(8,128)} all-to-all(f32[32,24,128]{2,1,0:T(8,128)S(1)} %add.49), channel_id=1, replica_groups={{0,16,32,48,64,80,96,112,128,144,160,176,192,208,224,240,256,272,288,30..., dimensions={0} | all-to-all | bytes 786432 | tf_op jit(solution)/shard_map/all_to_all | solution.py:42
  104.9 1.7 %shard_map.148 = f32[8,10,128]{2,1,0:T(8,128)} custom-call(f32[32,24,128]{2,1,0:T(8,128)} %all_to_all.31.arrived), custom_call_target="tpu_custom_call" | custom-call | tf_op jit(solution)/shard_map/pallas_call | solution.py:408
  106.6 12.3 %all_to_all.32.arrived = f32[8,10,128]{2,1,0:T(8,128)} all-to-all(f32[8,10,128]{2,1,0:T(8,128)} %shard_map.148), channel_id=1, replica_groups={{0,2,4,6,8,10,12,14},{1,3,5,7,9,11,13,15},{16,18,20,22,24,26,28,30},{17..., dimensions={0} | all-to-all | bytes 81920 | tf_op jit(solution)/shard_map/all_to_all | solution.py:42
  118.9 1.5 %shard_map.149 = f32[16,10,128]{2,1,0:T(8,128)} custom-call(f32[8,10,128]{2,1,0:T(8,128)} %all_to_all.32.arrived), custom_call_target="tpu_custom_call" | custom-call | tf_op jit(solution)/shard_map/pallas_call | solution.py:410
  120.4 4.7 %all-to-all-start.5 = ((f32[16,10,128]{2,1,0:T(8,128)}), f32[16,10,128]{2,1,0:T(8,128)S(1)}, u32[]{:S(2)}, u32[]{:S(2)}) async-start(f32[16,10,128]{2,1,0:T(8,128)} %shard_map.149), calls=%async_computation.5 | async-start | bytes 262144 | tf_op jit(solution)/shard_map/all_to_all | solution.py:42
  125.1 1.7 %shard_map.151 = bf16[69,512]{1,0:T(8,128)(2,1)} custom-call(bf16[69,128]{1,0:T(8,128)(2,1)} %readout.5, bf16[512,128]{1,0:T(8,128)(2,1)} %get-tuple-element.34.residual), custom_call_target="tpu_custom_call" | custom-call | tf_op jit(solution)/shard_map/pallas_call | solution.py:368
  126.8 1.6 %reshape.95 = bf16[1,69,4,128]{3,2,1,0:T(4,128)(2,1)} reshape(bf16[69,512]{1,0:T(8,128)(2,1)} %shard_map.151) | data formatting | bytes 141312 | tf_op jit(solution)/shard_map/reshape | solution.py:371
  128.4 1.8 %shard_map.152 = f32[69,512]{1,0:T(8,128)} custom-call(bf16[16,16,512]{2,1,0:T(8,128)(2,1)} %all_to_all.30.back), custom_call_target="tpu_custom_call" | custom-call | tf_op jit(solution)/shard_map/pallas_call | solution.py:380
  130.2 1.6 %reshape.96 = f32[1,69,4,128]{3,2,1,0:T(4,128)} reshape(f32[69,512]{1,0:T(8,128)} %shard_map.152) | data formatting | bytes 282624 | tf_op jit(solution)/shard_map/reshape | solution.py:381
  131.8 0.6 all-to-all-done.5.arrived
  132.4 0.0 copy-start.2
  132.4 0.6 copy-done.2
  133.0 1.6 %shard_map.150 = (f32[16,128]{1,0:T(8,128)}, f32[16,128]{1,0:T(8,128)}, f32[49,128]{1,0:T(8,128)}, f32[1,128]{1,0:T(1,128)}, f32[69,128]{1,0:T(8,128)}, /*index=5*/f32[1,1]{1,0:T(1,128)}) custom-call(f32[16,10,128]{2,1,0:T(8,128)} %copy-done.2), custom_call_target="tpu_custom_call" | custom-call | tf_op jit(solution)/shard_map/pallas_call | solution.py:412
  (2 shorter events, 0.1 us)
Async XLA Ops:
  2.1 13.7 %copy-start.4 = (bf16[4,128,128]{2,1,0:T(8,128)(2,1)S(1)}, bf16[4,128,128]{2,1,0:T(8,128)(2,1)}, u32[]{:S(2)}) copy-start(bf16[4,128,128]{2,1,0:T(8,128)(2,1)} %param.8) | copy-start | bytes 393220
  2.1 13.7 %copy-start.5 = (bf16[1,4,128,128]{3,2,1,0:T(8,128)(2,1)S(1)}, bf16[1,4,128,128]{3,2,1,0:T(8,128)(2,1)}, u32[]{:S(2)}) copy-start(bf16[1,4,128,128]{3,2,1,0:T(8,128)(2,1)} %param.9) | copy-start | bytes 393220
  2.1 29.1 %all-to-all-start = ((bf16[32,32,128]{2,1,0:T(8,128)(2,1)}), bf16[32,32,128]{2,1,0:T(8,128)(2,1)S(1)}, u32[]{:S(2)}, u32[]{:S(2)}) async-start(bf16[32,32,128]{2,1,0:T(8,128)(2,1)} %broadcast_in_dim.2), calls=%async_computation | async-start | bytes 524288 | tf_op jit(solution)/shard_map/all_to_all | solution.py:42
  15.8 0.7 copy-start
  16.5 3.4 %collective-permute-start = (bf16[3,128,128]{2,1,0:T(8,128)(2,1)S(1)}, bf16[3,128,128]{2,1,0:T(8,128)(2,1)S(1)}, u32[]{:S(2)}, u32[]{:S(2)}) collective-permute-start(bf16[3,128,128]{2,1,0:T(8,128)(2,1)S(1)} %get-tuple-element.55), channel_id=1, source_target_pairs={{0,1},{1,0},{2,3},{3,2},{4,5},{5,4},{6,7},{7,6},{8,9},{9,8},{10,11... | collective-permute-start | bytes 294920 | tf_op jit(solution)/shard_map/ppermute | solution.py:26
  18.6 1.3 collective-permute-start.1
  19.9 0.6 copy-start.6
  19.9 0.7 copy-start.7
  31.2 0.7 copy-start.1
  35.3 14.5 %all-to-all-start.1 = ((bf16[16,8,512]{2,1,0:T(8,128)(2,1)}), bf16[16,8,512]{2,1,0:T(8,128)(2,1)S(1)}, u32[]{:S(2)}, u32[]{:S(2)}) async-start(bf16[16,8,512]{2,1,0:T(8,128)(2,1)} %get-tuple-element.32), calls=%async_computation.1 | async-start | bytes 262144 | tf_op jit(solution)/shard_map/all_to_all | solution.py:42
  49.8 0.7 copy-start.3
  74.2 3.8 %collective-permute-start.2 = (f32[32,24,128]{2,1,0:T(8,128)}, f32[32,24,128]{2,1,0:T(8,128)S(1)}, u32[]{:S(2)}, u32[]{:S(2)}) collective-permute-start(f32[32,24,128]{2,1,0:T(8,128)} %get-tuple-element.47), channel_id=1, source_target_pairs={{0,1},{1,0},{2,3},{3,2},{4,5},{5,4},{6,7},{7,6},{8,9},{9,8},{10,11... | collective-permute-start | bytes 1179656 | tf_op jit(solution)/shard_map/ppermute | solution.py:26
  120.4 12.0 %all-to-all-start.5 = ((f32[16,10,128]{2,1,0:T(8,128)}), f32[16,10,128]{2,1,0:T(8,128)S(1)}, u32[]{:S(2)}, u32[]{:S(2)}) async-start(f32[16,10,128]{2,1,0:T(8,128)} %shard_map.149), calls=%async_computation.5 | async-start | bytes 262144 | tf_op jit(solution)/shard_map/all_to_all | solution.py:42
  132.4 0.7 copy-start.2

commit v4 on v3

--- a/solution.py
+++ b/solution.py
@@ -61,13 +61,16 @@
     ]
 
 
-def gelu_parts(u):
+def gelu_value(u):
     inner = jnp.tanh(SQRT_TWO_PI * (u + CUBIC * u * u * u))
-    value = 0.5 * u * (1.0 + inner)
-    slope = 0.5 * (1.0 + inner) + 0.5 * u * (1.0 - inner * inner) * SQRT_TWO_PI * (
+    return 0.5 * u * (1.0 + inner)
+
+
+def gelu_slope(u):
+    inner = jnp.tanh(SQRT_TWO_PI * (u + CUBIC * u * u * u))
+    return 0.5 * (1.0 + inner) + 0.5 * u * (1.0 - inner * inner) * SQRT_TWO_PI * (
         1.0 + 3.0 * CUBIC * u * u
     )
-    return value, slope
 
 
 def vmem_call(body, outs, scratch=(), scalars=0, vectors=0):
@@ -134,7 +137,7 @@
     return result.astype(BF16)
 
 
-def mlp_body(normed, both, field, readout, gated, slope, residual, chunks, upper):
+def mlp_body(normed, both, field, readout, gated, upper, residual, chunks):
     owned = both.shape[1] // 2
     hidden, channels = both.shape[0] * owned, both.shape[2]
     points = normed.shape[0]
@@ -144,9 +147,7 @@
 
     def step(i, carry):
         at = pl.ds(pl.multiple_of(i * 16, 16), 16)
-        value, tilt = gelu_parts(upper[at, :])
-        gated[at, :] = value.astype(BF16)
-        slope[at, :] = tilt
+        gated[at, :] = gelu_value(upper[at, :]).astype(BF16)
         return carry
 
     lax.fori_loop(0, points // 16, step, 0, unroll=2)
@@ -157,6 +158,15 @@
     outlook = dot(spread.astype(BF16), residual[...], (1, 1))
     for e in range(members):
         chunks[e] = outlook[e * CHUNK_ROWS : (e + 1) * CHUNK_ROWS].astype(BF16)
+
+
+def slope_body(upper, slope):
+    def step(i, carry):
+        at = pl.ds(pl.multiple_of(i * 16, 16), 16)
+        slope[at, :] = gelu_slope(upper[at, :])
+        return carry
+
+    lax.fori_loop(0, upper.shape[0] // 16, step, 0, unroll=2)
 
 
 def outlook_body(readout, residual, out):
@@ -288,17 +298,18 @@
             send[d, 2 * depth_z :, :] = tail
 
 
-def plane_body(arrived, out):
-    total = jnp.sum(arrived[...], axis=0)
-    depth_z = out.shape[0]
-    for z in range(depth_z):
-        out[z, 0:CHUNK_ROWS, :] = total[2 * depth_z :]
-        out[z, CHUNK_ROWS : CHUNK_ROWS + 1, :] = total[z : z + 1]
-        out[z, CHUNK_ROWS + 1 : CHUNK_ROWS + 2, :] = total[depth_z + z : depth_z + z + 1]
-
-
-def column_body(arrived, out):
-    out[...] = jnp.broadcast_to(jnp.sum(arrived[...], axis=0)[None], out.shape)
+def gradient_body(
+    place, back, readout, residual, gated, slope, normed, scaled, inverse, gain, both, ext, loss,
+    send, keep, gate, back_upper, widen_grad, shrink_grad, readout_grad, gain_grad, back_depth, small,
+):
+    backward_body(
+        back, readout, residual, gated, slope, normed, scaled, inverse, gain, both,
+        widen_grad, shrink_grad, readout_grad, gain_grad, back_depth, gate, back_upper,
+    )
+    pack_body(
+        place, back_depth, ext, widen_grad, shrink_grad, readout_grad, gain_grad, loss,
+        send, keep, small,
+    )
 
 
 def final_body(arrived, up, down, taps, gain, readout, loss, small):
@@ -336,12 +347,14 @@
     place = jnp.stack([lax.rem(band, 2), member]).astype(jnp.int32)
     gain = affine_factor.reshape(1, channels)
 
-    pair = jnp.concatenate([widen_matrix, shrink_matrix], axis=0)
-    both = exchange(
-        jnp.broadcast_to(pair[None], (bands,) + pair.shape), AXES, weight_groups(members, bands)
-    )
     field = (features.astype(F32) + random_perturbation[0].astype(F32)).astype(BF16)
     partner, other = halo_rows(field, half)
+    shape = (bands,) + widen_matrix.shape
+    pair = jnp.concatenate(
+        [jnp.broadcast_to(widen_matrix[None], shape), jnp.broadcast_to(shrink_matrix[None], shape)],
+        axis=1,
+    )
+    both = exchange(pair, AXES, weight_groups(members, bands))
     latitude = (band * rows + jnp.arange(points, dtype=jnp.int32) // zonal).astype(F32)
     area = jnp.cos(math.pi * ((latitude + 0.5) / latitudes - 0.5))
     weight = (area * (1.0 / (latitudes * zonal)))[None, :]
@@ -353,7 +366,7 @@
         scalars=1,
         vectors=5,
     )(place, field, partner, other, stencil_taps, gain)
-    gated, slope, residual, chunks = vmem_call(
+    gated, upper, residual, chunks = vmem_call(
         mlp_body,
         [
             ((points, hidden), BF16),
@@ -361,10 +374,10 @@
             ((points, channels), BF16),
             ((members, CHUNK_ROWS, points), BF16),
         ],
-        [pltpu.VMEM((points, hidden), F32)],
         vectors=4,
     )(normed, both, field, readout_matrix)
     everyone = exchange(chunks, "ens")
+    (slope,) = vmem_call(slope_body, [((points, hidden), F32)], vectors=1)(upper)
     (outlook,) = vmem_call(outlook_body, [((variables, points), BF16)], vectors=2)(
         readout_matrix, residual
     )
@@ -380,35 +393,41 @@
     (average,) = vmem_call(average_body, [((variables, points), F32)], vectors=1)(back)
     sample_average_spread = average.reshape(1, variables, rows, zonal)
 
-    widen_grad, shrink_grad, readout_grad, gain_grad, back_depth = vmem_call(
-        backward_body,
-        [
-            ((hidden, channels), F32),
-            ((hidden, channels), F32),
-            ((members * 16, channels), F32),
-            ((1, channels), F32),
-            ((points, channels), F32),
-        ],
-        [pltpu.VMEM((points, hidden), F32), pltpu.VMEM((points, hidden), BF16)],
-        vectors=10,
-    )(back, readout_matrix, residual, gated, slope, normed, scaled, inverse, gain, both)
     packet = ((2 * members, 2 * depth_z + share, channels), F32)
     send, keep = vmem_call(
-        pack_body,
+        gradient_body,
         [packet, packet],
-        [pltpu.VMEM((members * share, channels), F32)],
+        [
+            pltpu.VMEM((points, hidden), F32),
+            pltpu.VMEM((points, hidden), BF16),
+            pltpu.VMEM((hidden, channels), F32),
+            pltpu.VMEM((hidden, channels), F32),
+            pltpu.VMEM((members * 16, channels), F32),
+            pltpu.VMEM((1, channels), F32),
+            pltpu.VMEM((points, channels), F32),
+            pltpu.VMEM((members * share, channels), F32),
+        ],
         scalars=1,
-        vectors=7,
-    )(place, back_depth, ext, widen_grad, shrink_grad, readout_grad, gain_grad, loss)
+        vectors=12,
+    )(
+        place, back, readout_matrix, residual, gated, slope, normed, scaled, inverse, gain, both,
+        ext, loss,
+    )
 
     arrived = exchange(keep + core_swap(send), AXES, plane_groups(members, bands))
     columns = [
         list(range(h * bands // 2 + c, (h + 1) * bands // 2, 2)) for h in range(2) for c in range(2)
     ]
-    (outgoing,) = vmem_call(plane_body, [((depth_z, share + 2, channels), F32)], vectors=1)(arrived)
-    arrived = exchange(outgoing, "lat", columns)
-    (outgoing,) = vmem_call(column_body, [((members, share + 2, channels), F32)], vectors=1)(arrived)
-    arrived = exchange(outgoing, "ens")
+    part = jnp.sum(arrived, axis=0)
+    outgoing = jnp.concatenate(
+        [
+            jnp.broadcast_to(part[None, 2 * depth_z :], (depth_z, share, channels)),
+            part[: 2 * depth_z].reshape(2, depth_z, channels).transpose(1, 0, 2),
+        ],
+        axis=1,
+    )
+    done = jnp.sum(exchange(outgoing, "lat", columns), axis=0)
+    arrived = exchange(jnp.broadcast_to(done[None], (members,) + done.shape), "ens")
     up, down, taps, gain_total, readout, loss = vmem_call(
         final_body,
         [
@@ -455,6 +474,7 @@
         P("ens", None, "lat", None),
         P("ens", None, "lat", None),
     )
+
     return jax.shard_map(
         on_device, mesh=mesh, in_specs=in_specs, out_specs=out_specs, check_vma=False
     )

time: 136 us -> 130 us (0.956)
  blocking collectives: 51.8 us -> 36.5 us
  waiting for transfers between devices: 16.5 us -> 22 us
  starting transfers between devices: 30.3 us -> 34.8 us
  Pallas kernels: 25 us -> 23.4 us
    all_to_all x3 -> x2, blocking collectives: 51.8 us -> 36.5 us  [exchange(): lax.all_to_all(value, axis, 0, 0, tiled=True, axis_index_groups=groups)]
    all_to_all x3 -> x4, waiting for transfers between devices: 14.6 us -> 20.1 us  [exchange(): lax.all_to_all(value, axis, 0, 0, tiled=True, axis_index_groups=groups)]
    all_to_all x3 -> x4, starting transfers between devices: 25.6 us -> 30.1 us  [exchange(): lax.all_to_all(value, axis, 0, 0, tiled=True, axis_index_groups=groups)]
    pallas_call x4 -> x2, Pallas kernels: 10.7 us -> 9.45 us  [the longest x1 6.51 us: on_device(): vmem_call(gradient_body, [packet, packet], [pltpu.VMEM((points, hidden),...]
    unnamed x16 -> x20, local copies, waits for them, and re-layouts: 3.31 us -> 4 us
  transfers between devices with their start and end apart: 6 -> 7, of which waited for: 4 -> 5; matrix products, arithmetic and copies ran while one was open for 3% -> 3% of each run, Pallas kernels for 5% -> 7%
where the time goes in v4:
time: 130 us; the launch traced here: 129 us
  blocking collectives  36.5 us (28%)
  starting transfers between devices  34.8 us (27%)
  Pallas kernels  23.4 us (18%)
  waiting for transfers between devices  22 us (17%)
  local copies, waits for them, and re-layouts  8.58 us (7%)
  other arithmetic  3.12 us (2%)
    all_to_all x2, blocking collectives, exchange(): lax.all_to_all(value, axis, 0, 0, tiled=True, axis_index_groups=groups)  36.5 us
    all_to_all x4, starting transfers between devices, exchange(): lax.all_to_all(value, axis, 0, 0, tiled=True, axis_index_groups=groups)  30.1 us
    all_to_all x4, waiting for transfers between devices, exchange(): lax.all_to_all(value, axis, 0, 0, tiled=True, axis_index_groups=groups)  20.1 us
    pallas_call x1, Pallas kernels, on_device(): vmem_call(gradient_body, [packet, packet], [pltpu.VMEM((points, hidden),...  6.51 us
    ppermute x2, starting transfers between devices, core_swap(): return lax.ppermute(value, 'lat', [(i, i ^ 1) for i in range(count)])  4.08 us
    unnamed x20, local copies, waits for them, and re-layouts  4 us
    pallas_call x1, Pallas kernels, on_device(): vmem_call(stencil_body, [(wide, F32), ((points, channels), F32), ((points...  3.17 us
    pallas_call x1, Pallas kernels, on_device(): vmem_call(mlp_body, [((points, hidden), BF16), ((points, hidden), F32), (...  3.08 us
  transfers between devices with their start and end apart: 7, of which 5 were waited for; matrix products, arithmetic and copies ran while one was open for 3% of the time, Pallas kernels for 7%

profile of v4, /device:TPU:8, one launch (start us, length us, event | category | flops | bytes accessed | tf_op | source)
XLA Modules:
  0.0 129.2 jit_solution(6049063839711339847)
XLA Ops:
  0.6 0.0 copy-start.9
  0.6 0.7 broadcast_in_dim.8
  1.4 0.0 copy-done.9
  1.4 0.7 pad_maximum_fusion
  2.1 0.0 copy-start.5
  2.1 0.0 copy-start.6
  2.1 13.6 %all-to-all-start = ((bf16[32,32,128]{2,1,0:T(8,128)(2,1)}), bf16[32,32,128]{2,1,0:T(8,128)(2,1)S(1)}, u32[]{:S(2)}, u32[]{:S(2)}) async-start(bf16[32,32,128]{2,1,0:T(8,128)(2,1)} %pad_maximum_fusion), calls=%async_computation | async-start | bytes 524288 | tf_op jit(solution)/shard_map/all_to_all | solution.py:42
  15.8 0.0 copy-done.5
  15.8 0.0 copy-done.6
  15.8 0.0 copy-start
  15.9 0.6 copy-done
  16.5 2.2 %collective-permute-start = (bf16[3,128,128]{2,1,0:T(8,128)(2,1)S(1)}, bf16[3,128,128]{2,1,0:T(8,128)(2,1)S(1)}, u32[]{:S(2)}, u32[]{:S(2)}) collective-permute-start(bf16[3,128,128]{2,1,0:T(8,128)(2,1)S(1)} %get-tuple-element.45), channel_id=1, source_target_pairs={{0,1},{1,0},{2,3},{3,2},{4,5},{5,4},{6,7},{7,6},{8,9},{9,8},{10,11... | collective-permute-start | bytes 294920 | tf_op jit(solution)/shard_map/ppermute | solution.py:26
  18.7 0.7 collective-permute-start.1
  19.3 0.6 pad_add_fusion.place
  19.9 0.0 collective-permute-done.partner
  19.9 0.0 copy-start.7
  19.9 0.0 collective-permute-done.1.other
  19.9 0.0 copy-start.8
  19.9 0.6 copy-done.7
  20.6 0.0 copy-done.8
  20.6 3.2 %shard_map.143 = (f32[10,144,128]{2,1,0:T(8,128)}, f32[512,128]{1,0:T(8,128)}, f32[512,128]{1,0:T(8,128)}, bf16[512,128]{1,0:T(8,128)(2,1)}) custom-call(s32[2]{0:T(128)} %pad_add_fusion.place, bf16[4,128,128]{2,1,0:T(8,128)(2,1)} %copy-done, bf16[3,128,128]{2,1,0:T(8,128)(2,1)} %copy-done.7, bf16[3,128,128]{2,1,0:T(8,128)(2,1)} %copy-done.8, ...), custom_call_target="tpu_custom_call" | custom-call | tf_op jit(solution)/shard_map/pallas_call | solution.py:363
  23.8 7.4 %all-to-all-done.both = bf16[32,32,128]{2,1,0:T(8,128)(2,1)S(1)} async-done(((bf16[32,32,128]{2,1,0:T(8,128)(2,1)}), bf16[32,32,128]{2,1,0:T(8,128)(2,1)S(1)}, u32[]{:S(2)}, u32[]{:S(2)}) %all-to-all-start) | async-done | bytes 262176 | tf_op jit(solution)/shard_map/all_to_all | solution.py:42
  31.2 0.0 copy-start.1
  31.2 0.7 copy-done.1
  31.9 3.1 %shard_map.144 = (bf16[512,512]{1,0:T(8,128)(2,1)}, f32[512,512]{1,0:T(8,128)}, bf16[512,128]{1,0:T(8,128)(2,1)}, bf16[16,8,512]{2,1,0:T(8,128)(2,1)}) custom-call(bf16[512,128]{1,0:T(8,128)(2,1)} %get-tuple-element.26.normed, bf16[32,32,128]{2,1,0:T(8,128)(2,1)} %copy-done.1, bf16[4,128,128]{2,1,0:T(8,128)(2,1)} %copy-done, bf16[69,128]{1,0:T(8,128)(2,1)} %readout.5), custom_call_target="tpu_custom_call" | custom-call | tf_op jit(solution)/shard_map/pallas_call | solution.py:369
  35.0 7.2 %all-to-all-start.1 = ((bf16[16,8,512]{2,1,0:T(8,128)(2,1)}), bf16[16,8,512]{2,1,0:T(8,128)(2,1)S(1)}, u32[]{:S(2)}, u32[]{:S(2)}) async-start(bf16[16,8,512]{2,1,0:T(8,128)(2,1)} %get-tuple-element.27), calls=%async_computation.1 | async-start | bytes 262144 | tf_op jit(solution)/shard_map/all_to_all | solution.py:42
  42.2 0.7 fusion.8.weight
  42.8 6.6 %all-to-all-done.1.everyone = bf16[16,8,512]{2,1,0:T(8,128)(2,1)S(1)} async-done(((bf16[16,8,512]{2,1,0:T(8,128)(2,1)}), bf16[16,8,512]{2,1,0:T(8,128)(2,1)S(1)}, u32[]{:S(2)}, u32[]{:S(2)}) %all-to-all-start.1) | async-done | bytes 131104 | tf_op jit(solution)/shard_map/all_to_all | solution.py:42
  49.5 0.0 copy-start.4
  49.5 0.7 copy-done.4
  50.1 2.6 %shard_map.145 = (bf16[16,16,512]{2,1,0:T(8,128)(2,1)}, f32[1,128]{1,0:T(1,128)}) custom-call(s32[2]{0:T(128)} %pad_add_fusion.place, bf16[16,8,512]{2,1,0:T(8,128)(2,1)} %copy-done.4, f32[69,4,128]{2,1,0:T(4,128)} %truth.1, f32[1,512]{1,0:T(1,128)} %fusion.8.weight), custom_call_target="tpu_custom_call" | custom-call | tf_op jit(solution)/shard_map/pallas_call | solution.py:385
  52.7 4.5 %all-to-all-start.2 = ((bf16[16,16,512]{2,1,0:T(8,128)(2,1)}), bf16[16,16,512]{2,1,0:T(8,128)(2,1)S(1)}, u32[]{:S(2)}, u32[]{:S(2)}) async-start(bf16[16,16,512]{2,1,0:T(8,128)(2,1)} %get-tuple-element.28), calls=%async_computation.2 | async-start | bytes 524288 | tf_op jit(solution)/shard_map/all_to_all | solution.py:42
  57.3 2.9 %shard_map.146.slope = f32[512,512]{1,0:T(8,128)} custom-call(f32[512,512]{1,0:T(8,128)} %get-tuple-element.31.upper), custom_call_target="tpu_custom_call" | custom-call | tf_op jit(solution)/shard_map/pallas_call | solution.py:380
  60.2 5.5 %all-to-all-done.2.back = bf16[16,16,512]{2,1,0:T(8,128)(2,1)S(1)} async-done(((bf16[16,16,512]{2,1,0:T(8,128)(2,1)}), bf16[16,16,512]{2,1,0:T(8,128)(2,1)S(1)}, u32[]{:S(2)}, u32[]{:S(2)}) %all-to-all-start.2) | async-done | bytes 262176 | tf_op jit(solution)/shard_map/all_to_all | solution.py:42
  65.7 0.0 copy-start.2
  65.7 0.7 copy-done.2
  66.4 6.5 %shard_map.147 = (f32[32,24,128]{2,1,0:T(8,128)}, f32[32,24,128]{2,1,0:T(8,128)}) custom-call(s32[2]{0:T(128)} %pad_add_fusion.place, bf16[16,16,512]{2,1,0:T(8,128)(2,1)} %copy-done.2, bf16[69,128]{1,0:T(8,128)(2,1)} %readout.5, bf16[512,128]{1,0:T(8,128)(2,1)} %get-tuple-element.29.residual, bf16[512,512]{1,0:T(8,128)(2,1)} %get-tuple-element.30.gated, ...), custom_call_target="tpu_custom_call" | custom-call | tf_op jit(solution)/shard_map/pallas_call | solution.py:397
  72.9 1.9 %collective-permute-start.2 = (f32[32,24,128]{2,1,0:T(8,128)}, f32[32,24,128]{2,1,0:T(8,128)S(1)}, u32[]{:S(2)}, u32[]{:S(2)}) collective-permute-start(f32[32,24,128]{2,1,0:T(8,128)} %get-tuple-element.37), channel_id=1, source_target_pairs={{0,1},{1,0},{2,3},{3,2},{4,5},{5,4},{6,7},{7,6},{8,9},{9,8},{10,11... | collective-permute-start | bytes 1179656 | tf_op jit(solution)/shard_map/ppermute | solution.py:26
  74.8 1.9 %collective-permute-done.2 = f32[32,24,128]{2,1,0:T(8,128)S(1)} collective-permute-done((f32[32,24,128]{2,1,0:T(8,128)}, f32[32,24,128]{2,1,0:T(8,128)S(1)}, u32[]{:S(2)}, u32[]{:S(2)}) %collective-permute-start.2) | collective-permute-done | bytes 393248 | tf_op jit(solution)/shard_map/ppermute | solution.py:26
  76.7 1.0 add.49
  77.8 25.7 %all_to_all.30 = f32[32,24,128]{2,1,0:T(8,128)S(1)} all-to-all(f32[32,24,128]{2,1,0:T(8,128)S(1)} %add.49), channel_id=1, replica_groups={{0,16,32,48,64,80,96,112,128,144,160,176,192,208,224,240,256,272,288,30..., dimensions={0} | all-to-all | bytes 786432 | tf_op jit(solution)/shard_map/all_to_all | solution.py:42
  103.6 10.8 %all_to_all.31 = f32[8,10,128]{2,1,0:T(8,128)S(1)} all-to-all(f32[8,10,128]{2,1,0:T(8,128)S(1)} %pad_maximum_fusion.1), channel_id=1, replica_groups={{0,2,4,6,8,10,12,14},{1,3,5,7,9,11,13,15},{16,18,20,22,24,26,28,30},{17..., dimensions={0} | all-to-all | bytes 81920 | tf_op jit(solution)/shard_map/all_to_all | solution.py:42
  114.4 0.7 broadcast_in_dim.11
  115.0 4.7 %all-to-all-start.5 = ((f32[16,10,128]{2,1,0:T(8,128)}), f32[16,10,128]{2,1,0:T(8,128)S(1)}, u32[]{:S(2)}, u32[]{:S(2)}) async-start(f32[16,10,128]{2,1,0:T(8,128)} %broadcast_in_dim.11), calls=%async_computation.5 | async-start | bytes 262144 | tf_op jit(solution)/shard_map/all_to_all | solution.py:42
  119.7 1.7 %shard_map.149 = bf16[69,512]{1,0:T(8,128)(2,1)} custom-call(bf16[69,128]{1,0:T(8,128)(2,1)} %readout.5, bf16[512,128]{1,0:T(8,128)(2,1)} %get-tuple-element.29.residual), custom_call_target="tpu_custom_call" | custom-call | tf_op jit(solution)/shard_map/pallas_call | solution.py:381
  121.4 1.6 %reshape.102 = bf16[1,69,4,128]{3,2,1,0:T(4,128)(2,1)} reshape(bf16[69,512]{1,0:T(8,128)(2,1)} %shard_map.149) | data formatting | bytes 141312 | tf_op jit(solution)/shard_map/reshape | solution.py:384
  123.0 1.8 %shard_map.150 = f32[69,512]{1,0:T(8,128)} custom-call(bf16[16,16,512]{2,1,0:T(8,128)(2,1)} %copy-done.2), custom_call_target="tpu_custom_call" | custom-call | tf_op jit(solution)/shard_map/pallas_call | solution.py:393
  124.8 1.6 %reshape.103 = f32[1,69,4,128]{3,2,1,0:T(4,128)} reshape(f32[69,512]{1,0:T(8,128)} %shard_map.150) | data formatting | bytes 282624 | tf_op jit(solution)/shard_map/reshape | solution.py:394
  126.4 0.6 all-to-all-done.5.arrived
  127.0 0.0 copy-start.3
  127.0 0.6 copy-done.3
  127.6 1.6 %shard_map.148 = (f32[16,128]{1,0:T(8,128)}, f32[16,128]{1,0:T(8,128)}, f32[49,128]{1,0:T(8,128)}, f32[1,128]{1,0:T(1,128)}, f32[69,128]{1,0:T(8,128)}, /*index=5*/f32[1,1]{1,0:T(1,128)}) custom-call(f32[16,10,128]{2,1,0:T(8,128)} %copy-done.3), custom_call_target="tpu_custom_call" | custom-call | tf_op jit(solution)/shard_map/pallas_call | solution.py:431
  (10 shorter events, 0.2 us)
Async XLA Ops:
  0.6 0.7 copy-start.9
  2.1 13.7 %copy-start.5 = (bf16[4,128,128]{2,1,0:T(8,128)(2,1)S(1)}, bf16[4,128,128]{2,1,0:T(8,128)(2,1)}, u32[]{:S(2)}) copy-start(bf16[4,128,128]{2,1,0:T(8,128)(2,1)} %param.8) | copy-start | bytes 393220
  2.1 13.7 %copy-start.6 = (bf16[1,4,128,128]{3,2,1,0:T(8,128)(2,1)S(1)}, bf16[1,4,128,128]{3,2,1,0:T(8,128)(2,1)}, u32[]{:S(2)}) copy-start(bf16[1,4,128,128]{3,2,1,0:T(8,128)(2,1)} %param.9) | copy-start | bytes 393220
  2.1 29.1 %all-to-all-start = ((bf16[32,32,128]{2,1,0:T(8,128)(2,1)}), bf16[32,32,128]{2,1,0:T(8,128)(2,1)S(1)}, u32[]{:S(2)}, u32[]{:S(2)}) async-start(bf16[32,32,128]{2,1,0:T(8,128)(2,1)} %pad_maximum_fusion), calls=%async_computation | async-start | bytes 524288 | tf_op jit(solution)/shard_map/all_to_all | solution.py:42
  15.8 0.7 copy-start
  16.5 3.4 %collective-permute-start = (bf16[3,128,128]{2,1,0:T(8,128)(2,1)S(1)}, bf16[3,128,128]{2,1,0:T(8,128)(2,1)S(1)}, u32[]{:S(2)}, u32[]{:S(2)}) collective-permute-start(bf16[3,128,128]{2,1,0:T(8,128)(2,1)S(1)} %get-tuple-element.45), channel_id=1, source_target_pairs={{0,1},{1,0},{2,3},{3,2},{4,5},{5,4},{6,7},{7,6},{8,9},{9,8},{10,11... | collective-permute-start | bytes 294920 | tf_op jit(solution)/shard_map/ppermute | solution.py:26
  18.7 1.3 collective-permute-start.1
  19.9 0.7 copy-start.7
  19.9 0.7 copy-start.8
  31.2 0.7 copy-start.1
  35.0 14.5 %all-to-all-start.1 = ((bf16[16,8,512]{2,1,0:T(8,128)(2,1)}), bf16[16,8,512]{2,1,0:T(8,128)(2,1)S(1)}, u32[]{:S(2)}, u32[]{:S(2)}) async-start(bf16[16,8,512]{2,1,0:T(8,128)(2,1)} %get-tuple-element.27), calls=%async_computation.1 | async-start | bytes 262144 | tf_op jit(solution)/shard_map/all_to_all | solution.py:42
  49.5 0.7 copy-start.4
  52.7 13.0 %all-to-all-start.2 = ((bf16[16,16,512]{2,1,0:T(8,128)(2,1)}), bf16[16,16,512]{2,1,0:T(8,128)(2,1)S(1)}, u32[]{:S(2)}, u32[]{:S(2)}) async-start(bf16[16,16,512]{2,1,0:T(8,128)(2,1)} %get-tuple-element.28), calls=%async_computation.2 | async-start | bytes 524288 | tf_op jit(solution)/shard_map/all_to_all | solution.py:42
  65.7 0.7 copy-start.2
  72.9 3.8 %collective-permute-start.2 = (f32[32,24,128]{2,1,0:T(8,128)}, f32[32,24,128]{2,1,0:T(8,128)S(1)}, u32[]{:S(2)}, u32[]{:S(2)}) collective-permute-start(f32[32,24,128]{2,1,0:T(8,128)} %get-tuple-element.37), channel_id=1, source_target_pairs={{0,1},{1,0},{2,3},{3,2},{4,5},{5,4},{6,7},{7,6},{8,9},{9,8},{10,11... | collective-permute-start | bytes 1179656 | tf_op jit(solution)/shard_map/ppermute | solution.py:26
  115.0 12.0 %all-to-all-start.5 = ((f32[16,10,128]{2,1,0:T(8,128)}), f32[16,10,128]{2,1,0:T(8,128)S(1)}, u32[]{:S(2)}, u32[]{:S(2)}) async-start(f32[16,10,128]{2,1,0:T(8,128)} %broadcast_in_dim.11), calls=%async_computation.5 | async-start | bytes 262144 | tf_op jit(solution)/shard_map/all_to_all | solution.py:42
  127.0 0.6 copy-start.3

commit v5 on v4

--- a/solution.py
+++ b/solution.py
@@ -73,16 +73,28 @@
     )
 
 
-def vmem_call(body, outs, scratch=(), scalars=0, vectors=0):
+def vmem_call(body, outs, scratch=(), scalars=0, vectors=0, kept=()):
     vmem = pl.BlockSpec(memory_space=pltpu.VMEM)
     smem = pl.BlockSpec(memory_space=pltpu.SMEM)
-    return pl.pallas_call(
+    call = pl.pallas_call(
         body,
-        out_shape=[jax.ShapeDtypeStruct(shape, dtype) for shape, dtype in outs],
+        out_shape=[
+            jax.ShapeDtypeStruct(*out) if i in kept else pltpu.VMEM(*out)
+            for i, out in enumerate(outs)
+        ],
         in_specs=[smem] * scalars + [vmem] * vectors,
         out_specs=[vmem] * len(outs),
         scratch_shapes=list(scratch),
-    )
+        compiler_params=pltpu.CompilerParams(vmem_limit_bytes=16 << 20),
+    )
+
+    def run(*operands):
+        operands = operands[:scalars] + tuple(
+            pltpu.with_memory_space_constraint(x, pltpu.VMEM) for x in operands[scalars:]
+        )
+        return call(*operands)
+
+    return run
 
 
 def dot(a, b, contract):

time: 130 us -> 128 us (0.985)
  Pallas kernels: 23.4 us -> 11.4 us
  waiting for transfers between devices: 22 us -> 31.3 us
  local copies, waits for them, and re-layouts: 8.58 us -> 11.5 us
  other arithmetic: 3.12 us -> 1.05 us
  blocking collectives: 36.5 us -> 34.8 us
    pallas_call x8, Pallas kernels: 23.4 us -> 11.4 us  [run(): return call(*operands)]
    all_to_all x4, waiting for transfers between devices: 20.1 us -> 29.4 us  [exchange(): lax.all_to_all(value, axis, 0, 0, tiled=True, axis_index_groups=groups)]
    unnamed x20 -> x35, local copies, waits for them, and re-layouts: 4 us -> 8.7 us
    all_to_all x2, blocking collectives: 36.5 us -> 34.8 us  [exchange(): lax.all_to_all(value, axis, 0, 0, tiled=True, axis_index_groups=groups)]
  transfers between devices with their start and end apart: 7 -> 7, of which waited for: 5 -> 6; matrix products, arithmetic and copies ran while one was open for 3% -> 1% of each run, Pallas kernels for 7% -> 2%
where the time goes in v5:
time: 128 us; the launch traced here: 127 us
  starting transfers between devices  35 us (27%)
  blocking collectives  34.8 us (27%)
  waiting for transfers between devices  31.3 us (24%)
  local copies, waits for them, and re-layouts  11.5 us (9%)
  Pallas kernels  11.4 us (9%)
  between operations  2.02 us (2%)
    all_to_all x2, blocking collectives, exchange(): lax.all_to_all(value, axis, 0, 0, tiled=True, axis_index_groups=groups)  34.8 us
    all_to_all x4, starting transfers between devices, exchange(): lax.all_to_all(value, axis, 0, 0, tiled=True, axis_index_groups=groups)  30.2 us
    all_to_all x4, waiting for transfers between devices, exchange(): lax.all_to_all(value, axis, 0, 0, tiled=True, axis_index_groups=groups)  29.4 us
    pallas_call x8, Pallas kernels, run(): return call(*operands)  11.4 us
    unnamed x35, local copies, waits for them, and re-layouts  8.7 us
    ppermute x2, starting transfers between devices, core_swap(): return lax.ppermute(value, 'lat', [(i, i ^ 1) for i in range(count)])  4.1 us
  transfers between devices with their start and end apart: 7, of which 6 were waited for; matrix products, arithmetic and copies ran while one was open for 1% of the time, Pallas kernels for 2%

profile of v5, /device:TPU:8, one launch (start us, length us, event | category | flops | bytes accessed | tf_op | source)
XLA Modules:
  0.0 127.1 jit_solution(2867622868842774479)
XLA Ops:
  0.6 0.0 copy-start.14
  0.6 0.7 broadcast_in_dim.8
  1.4 0.0 copy-done.14
  1.4 0.7 pad_maximum_fusion
  2.1 0.0 copy-start.12
  2.1 0.0 copy-start.13
  2.1 13.6 %all-to-all-start = ((bf16[32,32,128]{2,1,0:T(8,128)(2,1)}), bf16[32,32,128]{2,1,0:T(8,128)(2,1)S(1)}, u32[]{:S(2)}, u32[]{:S(2)}) async-start(bf16[32,32,128]{2,1,0:T(8,128)(2,1)} %pad_maximum_fusion), calls=%async_computation | async-start | bytes 524288 | tf_op jit(solution)/shard_map/all_to_all | solution.py:42
  15.8 0.0 copy-done.12
  15.8 0.0 copy-done.13
  15.8 0.0 copy-start.10
  15.9 2.2 %collective-permute-start = (bf16[3,128,128]{2,1,0:T(8,128)(2,1)S(1)}, bf16[3,128,128]{2,1,0:T(8,128)(2,1)S(1)}, u32[]{:S(2)}, u32[]{:S(2)}) collective-permute-start(bf16[3,128,128]{2,1,0:T(8,128)(2,1)S(1)} %get-tuple-element.45), channel_id=1, source_target_pairs={{0,1},{1,0},{2,3},{3,2},{4,5},{5,4},{6,7},{7,6},{8,9},{9,8},{10,11... | collective-permute-start | bytes 294920 | tf_op jit(solution)/shard_map/ppermute | solution.py:26
  18.1 0.7 collective-permute-start.1
  18.7 0.1 pad_add_fusion.place
  18.8 0.0 copy-start.11
  18.8 0.2 collective-permute-done.partner
  19.1 0.0 collective-permute-done.1.other
  19.1 0.0 copy-done.10
  19.1 0.4 copy-done.11
  19.5 0.0 copy-start.8
  19.5 2.0 %shard_map.143 = (f32[10,144,128]{2,1,0:T(8,128)S(1)}, f32[512,128]{1,0:T(8,128)S(1)}, f32[512,128]{1,0:T(8,128)S(1)}, bf16[512,128]{1,0:T(8,128)(2,1)S(1)}) custom-call(s32[2]{0:T(128)S(1)} %pad_add_fusion.place, bf16[4,128,128]{2,1,0:T(8,128)(2,1)S(1)} %fusion.field, bf16[3,128,128]{2,1,0:T(8,128)(2,1)S(1)} %collective-permute-done.partner, ...), custom_call_target="tpu_custom_call" | custom-call | tf_op jit(solution)/shard_map/pallas_call | solution.py:95
  21.5 0.0 copy-start.6
  21.5 0.7 copy-done.6
  22.2 0.0 copy-start
  22.2 0.0 copy-start.4
  22.2 9.0 %all-to-all-done.both = bf16[32,32,128]{2,1,0:T(8,128)(2,1)S(1)} async-done(((bf16[32,32,128]{2,1,0:T(8,128)(2,1)}), bf16[32,32,128]{2,1,0:T(8,128)(2,1)S(1)}, u32[]{:S(2)}, u32[]{:S(2)}) %all-to-all-start) | async-done | bytes 262176 | tf_op jit(solution)/shard_map/all_to_all | solution.py:42
  31.2 0.0 copy-done.8
  31.2 2.0 %shard_map.144 = (bf16[512,512]{1,0:T(8,128)(2,1)S(1)}, f32[512,512]{1,0:T(8,128)S(1)}, bf16[512,128]{1,0:T(8,128)(2,1)S(1)}, bf16[16,8,512]{2,1,0:T(8,128)(2,1)}) custom-call(bf16[512,128]{1,0:T(8,128)(2,1)S(1)} %get-tuple-element.26.normed, bf16[32,32,128]{2,1,0:T(8,128)(2,1)S(1)} %all-to-all-done.both, bf16[4,128,128]{2,1,0:T(8,128)(2,1)S(1)} %fusion.field, ...), custom_call_target="tpu_custom_call" | custom-call | tf_op jit(solution)/shard_map/pallas_call | solution.py:95
  33.1 0.0 copy-done
  33.1 0.0 copy-done.4
  33.1 0.0 copy-start.2
  33.1 0.8 copy-done.2
  33.9 0.0 copy-start.9
  33.9 7.4 %all-to-all-start.1 = ((bf16[16,8,512]{2,1,0:T(8,128)(2,1)}), bf16[16,8,512]{2,1,0:T(8,128)(2,1)S(1)}, u32[]{:S(2)}, u32[]{:S(2)}) async-start(bf16[16,8,512]{2,1,0:T(8,128)(2,1)} %get-tuple-element.27), calls=%async_computation.1 | async-start | bytes 262144 | tf_op jit(solution)/shard_map/all_to_all | solution.py:42
  41.3 0.1 fusion.8.weight
  41.4 7.2 %all-to-all-done.1.everyone = bf16[16,8,512]{2,1,0:T(8,128)(2,1)S(1)} async-done(((bf16[16,8,512]{2,1,0:T(8,128)(2,1)}), bf16[16,8,512]{2,1,0:T(8,128)(2,1)S(1)}, u32[]{:S(2)}, u32[]{:S(2)}) %all-to-all-start.1) | async-done | bytes 131104 | tf_op jit(solution)/shard_map/all_to_all | solution.py:42
  48.6 0.0 copy-done.9
  48.6 2.2 %shard_map.145 = (bf16[16,16,512]{2,1,0:T(8,128)(2,1)}, f32[1,128]{1,0:T(1,128)S(1)}) custom-call(s32[2]{0:T(128)S(1)} %pad_add_fusion.place, bf16[16,8,512]{2,1,0:T(8,128)(2,1)S(1)} %all-to-all-done.1.everyone, f32[69,4,128]{2,1,0:T(4,128)S(1)} %copy-done.9, f32[1,512]{1,0:T(1,128)S(1)} %fusion.8.weight), custom_call_target="tpu_custom_call" | custom-call | tf_op jit(solution)/shard_map/pallas_call | solution.py:95
  50.8 4.5 %all-to-all-start.2 = ((bf16[16,16,512]{2,1,0:T(8,128)(2,1)}), bf16[16,16,512]{2,1,0:T(8,128)(2,1)S(1)}, u32[]{:S(2)}, u32[]{:S(2)}) async-start(bf16[16,16,512]{2,1,0:T(8,128)(2,1)} %get-tuple-element.28), calls=%async_computation.2 | async-start | bytes 524288 | tf_op jit(solution)/shard_map/all_to_all | solution.py:42
  55.3 0.7 shard_map.146.slope
  56.0 7.7 %all-to-all-done.2.back = bf16[16,16,512]{2,1,0:T(8,128)(2,1)S(1)} async-done(((bf16[16,16,512]{2,1,0:T(8,128)(2,1)}), bf16[16,16,512]{2,1,0:T(8,128)(2,1)S(1)}, u32[]{:S(2)}, u32[]{:S(2)}) %all-to-all-start.2) | async-done | bytes 262176 | tf_op jit(solution)/shard_map/all_to_all | solution.py:42
  63.7 0.0 copy-start.1
  63.7 0.9 copy-done.1
  64.6 1.0 copy-done.3
  65.7 0.9 copy-done.5
  66.6 0.9 copy-done.7
  67.6 4.1 %shard_map.147 = (f32[32,24,128]{2,1,0:T(8,128)S(1)}, f32[32,24,128]{2,1,0:T(8,128)S(1)}) custom-call(s32[2]{0:T(128)S(1)} %pad_add_fusion.place, bf16[16,16,512]{2,1,0:T(8,128)(2,1)S(1)} %all-to-all-done.2.back, bf16[69,128]{1,0:T(8,128)(2,1)S(1)} %copy-done.8, bf16[512,128]{1,0:T(8,128)(2,1)S(1)} %get-tuple-element.29.residual, ...), custom_call_target="tpu_custom_call" | custom-call | tf_op jit(solution)/shard_map/pallas_call | solution.py:95
  71.7 1.9 %collective-permute-start.2 = (f32[32,24,128]{2,1,0:T(8,128)S(1)}, f32[32,24,128]{2,1,0:T(8,128)S(1)}, u32[]{:S(2)}, u32[]{:S(2)}) collective-permute-start(f32[32,24,128]{2,1,0:T(8,128)S(1)} %get-tuple-element.37), channel_id=1, source_target_pairs={{0,1},{1,0},{2,3},{3,2},{4,5},{5,4},{6,7},{7,6},{8,9},{9,8},{10,11... | collective-permute-start | bytes 1179656 | tf_op jit(solution)/shard_map/ppermute | solution.py:26
  73.6 1.7 %collective-permute-done.2 = f32[32,24,128]{2,1,0:T(8,128)S(1)} collective-permute-done((f32[32,24,128]{2,1,0:T(8,128)S(1)}, f32[32,24,128]{2,1,0:T(8,128)S(1)}, u32[]{:S(2)}, u32[]{:S(2)}) %collective-permute-start.2) | collective-permute-done | bytes 393248 | tf_op jit(solution)/shard_map/ppermute | solution.py:26
  75.3 0.1 add.49
  75.4 24.0 %all_to_all.30 = f32[32,24,128]{2,1,0:T(8,128)S(1)} all-to-all(f32[32,24,128]{2,1,0:T(8,128)S(1)} %add.49), channel_id=1, replica_groups={{0,16,32,48,64,80,96,112,128,144,160,176,192,208,224,240,256,272,288,30..., dimensions={0} | all-to-all | bytes 786432 | tf_op jit(solution)/shard_map/all_to_all | solution.py:42
  99.5 10.8 %all_to_all.31 = f32[8,10,128]{2,1,0:T(8,128)S(1)} all-to-all(f32[8,10,128]{2,1,0:T(8,128)S(1)} %pad_maximum_fusion.1), channel_id=1, replica_groups={{0,2,4,6,8,10,12,14},{1,3,5,7,9,11,13,15},{16,18,20,22,24,26,28,30},{17..., dimensions={0} | all-to-all | bytes 81920 | tf_op jit(solution)/shard_map/all_to_all | solution.py:42
  110.3 0.7 broadcast_in_dim.11
  110.9 4.7 %all-to-all-start.5 = ((f32[16,10,128]{2,1,0:T(8,128)}), f32[16,10,128]{2,1,0:T(8,128)S(1)}, u32[]{:S(2)}, u32[]{:S(2)}) async-start(f32[16,10,128]{2,1,0:T(8,128)} %broadcast_in_dim.11), calls=%async_computation.5 | async-start | bytes 262144 | tf_op jit(solution)/shard_map/all_to_all | solution.py:42
  115.6 0.2 shard_map.149
  115.8 0.7 reshape.102
  116.5 0.2 shard_map.150
  116.7 0.7 reshape.103
  117.4 5.5 %all-to-all-done.5.arrived = f32[16,10,128]{2,1,0:T(8,128)S(1)} async-done(((f32[16,10,128]{2,1,0:T(8,128)}), f32[16,10,128]{2,1,0:T(8,128)S(1)}, u32[]{:S(2)}, u32[]{:S(2)}) %all-to-all-start.5) | async-done | bytes 81952 | tf_op jit(solution)/shard_map/all_to_all | solution.py:42
  122.9 0.1 shard_map.148
  123.0 0.6 copy.26
  123.6 0.6 copy.22
  124.2 0.6 copy.24
  124.8 0.6 copy.25
  125.5 0.5 copy.23
  (13 shorter events, 0.2 us)
Async XLA Ops:
  0.6 0.7 copy-start.14
  2.1 13.7 %copy-start.12 = (bf16[4,128,128]{2,1,0:T(8,128)(2,1)S(1)}, bf16[4,128,128]{2,1,0:T(8,128)(2,1)}, u32[]{:S(2)}) copy-start(bf16[4,128,128]{2,1,0:T(8,128)(2,1)} %param.8) | copy-start | bytes 393220
  2.1 13.7 %copy-start.13 = (bf16[1,4,128,128]{3,2,1,0:T(8,128)(2,1)S(1)}, bf16[1,4,128,128]{3,2,1,0:T(8,128)(2,1)}, u32[]{:S(2)}) copy-start(bf16[1,4,128,128]{3,2,1,0:T(8,128)(2,1)} %param.9) | copy-start | bytes 393220
  2.1 29.1 %all-to-all-start = ((bf16[32,32,128]{2,1,0:T(8,128)(2,1)}), bf16[32,32,128]{2,1,0:T(8,128)(2,1)S(1)}, u32[]{:S(2)}, u32[]{:S(2)}) async-start(bf16[32,32,128]{2,1,0:T(8,128)(2,1)} %pad_maximum_fusion), calls=%async_computation | async-start | bytes 524288 | tf_op jit(solution)/shard_map/all_to_all | solution.py:42
  15.8 3.2 %copy-start.10 = (f32[49,128]{1,0:T(8,128)S(1)}, f32[49,128]{1,0:T(8,128)}, u32[]{:S(2)}) copy-start(f32[49,128]{1,0:T(8,128)} %taps.1) | copy-start | bytes 75268
  15.9 3.2 %collective-permute-start = (bf16[3,128,128]{2,1,0:T(8,128)(2,1)S(1)}, bf16[3,128,128]{2,1,0:T(8,128)(2,1)S(1)}, u32[]{:S(2)}, u32[]{:S(2)}) collective-permute-start(bf16[3,128,128]{2,1,0:T(8,128)(2,1)S(1)} %get-tuple-element.45), channel_id=1, source_target_pairs={{0,1},{1,0},{2,3},{3,2},{4,5},{5,4},{6,7},{7,6},{8,9},{9,8},{10,11... | collective-permute-start | bytes 294920 | tf_op jit(solution)/shard_map/ppermute | solution.py:26
  18.1 1.0 collective-permute-start.1
  18.8 0.7 copy-start.11
  19.5 11.7 %copy-start.8 = (bf16[69,128]{1,0:T(8,128)(2,1)S(1)}, bf16[69,128]{1,0:T(8,128)(2,1)}, u32[]{:S(2)}) copy-start(bf16[69,128]{1,0:T(8,128)(2,1)} %readout.5) | copy-start | bytes 52996
  21.5 0.7 copy-start.6
  22.2 11.0 %copy-start = (bf16[512,128]{1,0:T(8,128)(2,1)}, bf16[512,128]{1,0:T(8,128)(2,1)S(1)}, u32[]{:S(2)}) copy-start(bf16[512,128]{1,0:T(8,128)(2,1)S(1)} %get-tuple-element.26.normed) | copy-start | bytes 393220
  22.2 11.0 %copy-start.4 = (f32[512,128]{1,0:T(8,128)}, f32[512,128]{1,0:T(8,128)S(1)}, u32[]{:S(2)}) copy-start(f32[512,128]{1,0:T(8,128)S(1)} %get-tuple-element.32.scaled) | copy-start | bytes 786436
  33.1 0.8 copy-start.2
  33.9 14.7 %copy-start.9 = (f32[69,4,128]{2,1,0:T(4,128)S(1)}, f32[69,4,128]{2,1,0:T(4,128)}, u32[]{:S(2)}) copy-start(f32[69,4,128]{2,1,0:T(4,128)} %truth.1) | copy-start | bytes 423940
  33.9 14.7 %all-to-all-start.1 = ((bf16[16,8,512]{2,1,0:T(8,128)(2,1)}), bf16[16,8,512]{2,1,0:T(8,128)(2,1)S(1)}, u32[]{:S(2)}, u32[]{:S(2)}) async-start(bf16[16,8,512]{2,1,0:T(8,128)(2,1)} %get-tuple-element.27), calls=%async_computation.1 | async-start | bytes 262144 | tf_op jit(solution)/shard_map/all_to_all | solution.py:42
  50.8 13.0 %all-to-all-start.2 = ((bf16[16,16,512]{2,1,0:T(8,128)(2,1)}), bf16[16,16,512]{2,1,0:T(8,128)(2,1)S(1)}, u32[]{:S(2)}, u32[]{:S(2)}) async-start(bf16[16,16,512]{2,1,0:T(8,128)(2,1)} %get-tuple-element.28), calls=%async_computation.2 | async-start | bytes 524288 | tf_op jit(solution)/shard_map/all_to_all | solution.py:42
  63.7 0.9 copy-start.1
  64.6 1.0 copy-start.3
  65.7 0.9 copy-start.5
  66.6 0.9 copy-start.7
  71.7 3.6 %collective-permute-start.2 = (f32[32,24,128]{2,1,0:T(8,128)S(1)}, f32[32,24,128]{2,1,0:T(8,128)S(1)}, u32[]{:S(2)}, u32[]{:S(2)}) collective-permute-start(f32[32,24,128]{2,1,0:T(8,128)S(1)} %get-tuple-element.37), channel_id=1, source_target_pairs={{0,1},{1,0},{2,3},{3,2},{4,5},{5,4},{6,7},{7,6},{8,9},{9,8},{10,11... | collective-permute-start | bytes 1179656 | tf_op jit(solution)/shard_map/ppermute | solution.py:26
  110.9 12.0 %all-to-all-start.5 = ((f32[16,10,128]{2,1,0:T(8,128)}), f32[16,10,128]{2,1,0:T(8,128)S(1)}, u32[]{:S(2)}, u32[]{:S(2)}) async-start(f32[16,10,128]{2,1,0:T(8,128)} %broadcast_in_dim.11), calls=%async_computation.5 | async-start | bytes 262144 | tf_op jit(solution)/shard_map/all_to_all | solution.py:42
